TPU v7x, 256 devices: a whole 4x4x8 slice. The times are simulated.
256 devices in a mesh: tm: 4 (over x), rows: 64 (over y, z, core).
Axes of the slice: x: 4, y: 4, z: 8, core: 2. Of those that a mesh axis runs over, the one named last changes fastest.
Arguments:
- latent: bfloat16 [4, 64, 160, 512], P('tm', 'rows'), may hold values from -350 to 350, as said below
- norm_gain: float32 [512], replicated, may hold values from 0.1 to 1.9
- norm_bias: float32 [512], replicated, may hold values from -4 to 4
- conv_weight: bfloat16 [3, 3, 3, 512, 512], P(None, None, None, 'rows', 'tm'), may hold values from -0.0546875 to 0.0546875
- cotangent: bfloat16 [4, 128, 320, 512], P('tm', 'rows'), may hold values from -180 to 180
Outputs:
- latent_grad: float32 [4, 64, 160, 512], P('tm', 'rows')
- gain_grad: float32 [512], replicated
- bias_grad: float32 [512], replicated
Inputs may be any that keep to these rules, and one draw needn't show every extreme that they name: `latent`: features of the unit's input.
All inputs are finite; a program needn't handle non-finite values.
Results may differ from a plain program's by a relative error of at most 0.0003.
Values may be sent and summed in bfloat16 or wider, within the bound.
No kernel may reach another device: no remote copies, remote signals or barrier semaphores. Data moves between devices by JAX's collectives and lax.ppermute only.
A program may use at most 320 MiB of HBM per device.

v0:
```python
import jax
import jax.numpy as jnp
from jax import lax
from jax.sharding import PartitionSpec as P

GROUPS = 32


def extended(block, sides, width):
    for axis, dim in sides:
        count = lax.axis_size(axis)
        forward = [(i, i + 1) for i in range(count - 1)]
        backward = [(target, source) for source, target in forward]
        low = lax.ppermute(
            lax.slice_in_dim(block, block.shape[dim] - width, None, axis=dim), axis, forward
        )
        high = lax.ppermute(lax.slice_in_dim(block, 0, width, axis=dim), axis, backward)
        block = jnp.concatenate([low, block, high], axis=dim)
    return block


def from_behind(value, axis, steps):
    count = lax.axis_size(axis)
    first, last = (max(0, -steps), min(count, count - steps))
    return lax.ppermute(value, axis, [(source, source + steps) for source in range(first, last)])


def shifted_rows(frames, extra_frames):
    padded = jnp.pad(frames, ((0, extra_frames), (0, 0), (1, 1), (0, 0)))
    fine_rows = frames.shape[1] - 2
    return [padded[:, 2 - row_tap : 2 - row_tap + fine_rows] for row_tap in range(3)]


def tap_total(row_slabs, weights, tap_pairs, frames_out, span_cols):
    running = None
    for offset, tap_index in tap_pairs:
        for row_tap in range(3):
            source = row_slabs[row_tap][offset : offset + frames_out]
            for col_tap in range(3):
                product = lax.dot_general(
                    source,
                    weights[tap_index, row_tap, col_tap],
                    (((3,), (1,)), ((), ())),
                    preferred_element_type=jnp.float32,
                )
                piece = product[:, :, 2 - col_tap : 2 - col_tap + span_cols, :]
                running = piece if running is None else running + piece
    return running


def pool_pairs(fine_grad):
    frames, fine_rows, span_cols, channels = fine_grad.shape
    return fine_grad.reshape(frames, fine_rows // 2, 2, span_cols // 2, 2, channels).sum(
        axis=(2, 4)
    )


def block_grad(row_slabs, weights, frames_out, first_frame):
    span_cols = row_slabs[0].shape[2] - 2

    def extra_terms():
        return tap_total(row_slabs, weights, ((0, 1), (0, 0), (1, 0)), 1, span_cols)

    def no_terms():
        return jnp.zeros((1, row_slabs[0].shape[1], span_cols, weights.shape[3]), jnp.float32)

    main_part = tap_total(row_slabs, weights, ((0, 2), (1, 1), (2, 0)), frames_out, span_cols)
    main_part = main_part + lax.cond(first_frame, extra_terms, no_terms)
    return pool_pairs(main_part)


def on_device(latent, norm_gain, norm_bias, conv_weight, cotangent):
    frames_all = lax.axis_size("tm")
    rows_all = lax.axis_size("rows")
    low_rows = latent.shape[1]
    low_cols = latent.shape[2]
    channels = latent.shape[3]
    per_group = channels // GROUPS
    cell_count = frames_all * rows_all * low_rows * low_cols
    rimmed = extended(cotangent, (("rows", 1),), 1)
    following = from_behind(rimmed, "tm", -1)
    further = from_behind(rimmed, "tm", -2)
    stacked = jnp.concatenate([rimmed, following, further], axis=0)
    weight_wide = lax.all_gather(conv_weight, "tm", axis=4, tiled=True)
    weight_full = lax.all_gather(weight_wide, "rows", axis=3, tiled=True)
    up_grad = block_grad(shifted_rows(stacked, 0), weight_full, 1, lax.axis_index("tm") == 0)
    features = latent.astype(jnp.float32)
    sum_x = jnp.sum(features, axis=(0, 1, 2))
    sum_sq = jnp.sum(features * features, axis=(0, 1, 2))
    total_x, total_sq = lax.psum((sum_x, sum_sq), ("tm", "rows"))
    group_x = total_x.reshape(GROUPS, per_group).sum(axis=1)
    group_sq = total_sq.reshape(GROUPS, per_group).sum(axis=1)
    group_mean = group_x / (cell_count * per_group)
    group_var = group_sq / (cell_count * per_group) - group_mean * group_mean
    inv_std = lax.rsqrt(group_var + 1e-06)
    mean_chan = jnp.repeat(group_mean, per_group)
    inv_chan = jnp.repeat(inv_std, per_group)
    normed = (features - mean_chan) * inv_chan
    pre = normed * norm_gain + norm_bias
    sigmoid_pre = jax.nn.sigmoid(pre)
    act_grad = up_grad * sigmoid_pre * (1.0 + pre * (1.0 - sigmoid_pre))
    sum_act, sum_scaled = lax.psum(
        (jnp.sum(act_grad, axis=(0, 1, 2)), jnp.sum(act_grad * normed, axis=(0, 1, 2))),
        ("tm", "rows"),
    )
    gain_grad = sum_scaled / cell_count
    bias_grad = sum_act / cell_count
    mean_q = (norm_gain * sum_act).reshape(GROUPS, per_group).sum(axis=1) / (cell_count * per_group)
    mean_qn = (norm_gain * sum_scaled).reshape(GROUPS, per_group).sum(axis=1) / (
        cell_count * per_group
    )
    latent_grad = inv_chan * (
        act_grad * norm_gain
        - jnp.repeat(mean_q, per_group)
        - normed * jnp.repeat(mean_qn, per_group)
    )
    return (latent_grad, gain_grad, bias_grad)


def solution(mesh):
    placed = (
        P("tm", "rows", None, None),
        P(),
        P(),
        P(None, None, None, "rows", "tm"),
        P("tm", "rows", None, None),
    )
    return jax.shard_map(
        on_device,
        mesh=mesh,
        in_specs=placed,
        out_specs=(P("tm", "rows", None, None), P(), P()),
        check_vma=False,
    )
```

profile of v0, /device:TPU:32, one launch (start us, length us, event | category | flops | bytes accessed | tf_op | source)
XLA Modules:
  0.0 353.9 jit_solution(4041163253013684087)
XLA Ops:
  7.2 12.8 %all_gather.6 = bf16[3,3,3,8,512]{4,3,2,1,0:T(8,128)(2,1)} all-gather(bf16[3,3,3,8,128]{4,3,2,1,0:T(8,128)(2,1)} %param.10), channel_id=1, replica_groups=mesh['tm'=4,'rows'=64] {'tm'}, dimensions={4}, use_global_device_ids=true | all-gather | bytes 276480 | tf_op jit(solution)/shard_map/all_gather | solution.py:84
  21.2 2.1 collective-permute-start
  23.3 3.6 %collective-permute-start.1 = (bf16[1,1,320,512]{3,2,1,0:T(8,128)(2,1)S(1)}, bf16[1,1,320,512]{3,2,1,0:T(8,128)(2,1)S(1)}, u32[]{:S(2)}, u32[]{:S(2)}) collective-permute-start(bf16[1,1,320,512]{3,2,1,0:T(8,128)(2,1)S(1)} %get-tuple-element.26), channel_id=1, source_target_pairs={{1,0},{2,1},{3,2},{4,3},{5,4},{6,5},{7,6},{8,7},{9,8},{10,9},{11,1... | collective-permute-start | bytes 983048 | tf_op jit(solution)/shard_map/ppermute | solution.py:17
  26.9 2.8 collective-permute-done
  29.8 1.7 collective-permute-done.1
  34.4 130.9 %all-reduce.2 = (f32[32,16]{1,0:T(8,128)S(1)}, f32[32,16]{1,0:T(8,128)S(1)}) all-reduce(f32[32,16]{1,0:T(8,128)S(1)} %reshape.178, f32[32,16]{1,0:T(8,128)S(1)} %reshape.177), channel_id=1, replica_groups=mesh['tm'=4,'rows'=64] {'tm','rows'}, use_global_device_ids=true, to_apply=%region_4.5 | all-reduce | flops 1024 | bytes 8192 | tf_op jit(solution)/shard_map/psum | solution.py:90
  165.8 3.9 %fusion.113 = bf16[3,4,322,512]{3,2,1,0:T(8,128)(2,1)} fusion(bf16[1,4,320,512]{3,2,1,0:T(8,128)(2,1)} %collective-permute-done.3, bf16[1,4,320,512]{3,2,1,0:T(8,128)(2,1)} %collective-permute-done.2, bf16[1,4,320,512]{3,2,1,0:T(8,128)(2,1)S(1)} %constant_dynamic-update-slice_fusion), kind=kLoop, calls=%fused_computation.168 | loop fusion | flops 23740416 | bytes 7888896 | tf_op jit(solution)/shard_map/concatenate | solution.py:83
  169.7 48.1 %conditional.1 = (f32[1,2,320,512]{3,2,1,0:T(8,128)}) conditional(s32[]{:T(128)} %convert_element_type.9, () %tuple.14, (bf16[3,4,322,512]{3,2,1,0:T(8,128)(2,1)}, bf16[3,3,3,512,512]{4,3,2,1,0:T(8,128)(2,1)}) %tuple.15), branch_computations={%region_6.7_spmd, %region_7.8_spmd} | conditional | flops 9124839424 | bytes 177053760 | solution.py:68
  169.7 1.9 convolution_bitcast_fusion.15
  171.6 1.8 convolution_bitcast_fusion.16
  173.5 1.7 convolution_bitcast_fusion.17
  175.2 2.0 convolution_bitcast_fusion.24
  177.2 2.1 convolution_bitcast_fusion.25
  192.3 1.7 convolution_bitcast_fusion.3
  195.6 1.6 convolution_bitcast_fusion
  200.4 1.7 convolution_bitcast_fusion.5
  202.1 1.7 convolution_bitcast_fusion.8
  203.8 1.7 convolution_bitcast_fusion.20
  205.5 1.6 convolution_bitcast_fusion.23
  208.8 9.0 %slice_add_fusion = f32[1,2,320,512]{3,2,1,0:T(8,128)} fusion(f32[1,2,322,512]{3,2,1,0:T(8,128)} %convolution_bitcast_fusion, f32[1,2,322,512]{3,2,1,0:T(8,128)} %convolution_bitcast_fusion.1, f32[1,2,322,512]{3,2,1,0:T(8,128)} %convolution_bitcast_fusion.2, f32[1,2,322,512]{3,2,1,0:T(8,128)} %convolution_bitcast_fusion.3, ...), kind=kLoop, calls=%fused_computation.27 | loop fusion | flops 8519680 | bytes 36700160 | tf_op jit(solution)/shard_map/cond/branch_1_fun/add | solution.py:47
  217.8 1.9 convolution_bitcast_fusion.28
  219.8 1.8 convolution_bitcast_fusion.27
  221.6 1.7 convolution_bitcast_fusion.31
  223.3 2.0 convolution_bitcast_fusion.30
  225.3 2.1 convolution_bitcast_fusion.34
  235.0 1.7 convolution_bitcast_fusion.45
  236.7 1.7 convolution_bitcast_fusion.49
  241.6 1.6 convolution_bitcast_fusion.51
  249.7 1.7 convolution_bitcast_fusion.41
  256.2 1.7 convolution_bitcast_fusion.53
  257.9 10.1 %fusion.115 = f32[320,512]{1,0:T(8,128)} fusion(f32[1,2,320,512]{3,2,1,0:T(8,128)} %get-tuple-element.34, f32[1,2,322,512]{3,2,1,0:T(8,128)S(1)} %convolution_bitcast_fusion.27, f32[1,2,322,512]{3,2,1,0:T(8,128)S(1)} %convolution_bitcast_fusion.28, f32[1,2,322,512]{3,2,1,0:T(8,128)} %convolution_bitcast_fusion.29, ...), kind=kLoop, calls=%fused_computation.198 | loop fusion | flops 9011200 | bytes 37355520 | tf_op jit(solution)/shard_map/reduce_sum | solution.py:53
  270.5 74.4 %all-reduce.1 = (f32[512]{0:T(512)S(1)}, f32[512]{0:T(512)S(1)}) all-reduce(f32[512]{0:T(512)S(1)} %get-tuple-element.18, f32[512]{0:T(512)S(1)} %get-tuple-element.17), channel_id=1, replica_groups=mesh['tm'=4,'rows'=64] {'tm','rows'}, use_global_device_ids=true, to_apply=%region_14.15 | all-reduce | flops 1024 | bytes 8192 | tf_op jit(solution)/shard_map/psum | solution.py:102
  (85 shorter events, 50.5 us)
Async XLA Ops:
  7.2 22.6 %copy-start.4 = (bf16[1,2,320,512]{3,2,1,0:T(8,128)(2,1)S(1)}, bf16[1,2,320,512]{3,2,1,0:T(8,128)(2,1)}, u32[]{:S(2)}) copy-start(bf16[1,2,320,512]{3,2,1,0:T(8,128)(2,1)} %param.11) | copy-start | bytes 1966084
  7.2 162.5 %all-gather.2.cloned.1.call-start = ((), (), s32[]{:S(2)}) async-start(), calls=%async_computation | async-start | bytes 14376960 | tf_op jit(solution)/shard_map/all_gather | solution.py:85
  21.2 12.9 %copy-start.5 = (bf16[1,1,160,512]{3,2,1,0:T(8,128)(2,1)S(1)}, bf16[1,1,160,512]{3,2,1,0:T(8,128)(2,1)}, u32[]{:S(2)}) copy-start(bf16[1,1,160,512]{3,2,1,0:T(8,128)(2,1)} %param.7) | copy-start | bytes 491524
  21.2 8.5 %collective-permute-start = (bf16[1,1,320,512]{3,2,1,0:T(8,128)(2,1)S(1)}, bf16[1,1,320,512]{3,2,1,0:T(8,128)(2,1)S(1)}, u32[]{:S(2)}, u32[]{:S(2)}) collective-permute-start(bf16[1,1,320,512]{3,2,1,0:T(8,128)(2,1)S(1)} %get-tuple-element.27), channel_id=1, source_target_pairs={{0,1},{1,2},{2,3},{3,4},{4,5},{5,6},{6,7},{7,8},{8,9},{9,10},{10,1... | collective-permute-start | bytes 983048 | tf_op jit(solution)/shard_map/ppermute | solution.py:14
  23.3 8.2 %collective-permute-start.1 = (bf16[1,1,320,512]{3,2,1,0:T(8,128)(2,1)S(1)}, bf16[1,1,320,512]{3,2,1,0:T(8,128)(2,1)S(1)}, u32[]{:S(2)}, u32[]{:S(2)}) collective-permute-start(bf16[1,1,320,512]{3,2,1,0:T(8,128)(2,1)S(1)} %get-tuple-element.26), channel_id=1, source_target_pairs={{1,0},{2,1},{3,2},{4,3},{5,4},{6,5},{7,6},{8,7},{9,8},{10,9},{11,1... | collective-permute-start | bytes 983048 | tf_op jit(solution)/shard_map/ppermute | solution.py:17
  31.5 134.3 %collective-permute-start.3 = (bf16[1,4,320,512]{3,2,1,0:T(8,128)(2,1)S(1)}, bf16[1,4,320,512]{3,2,1,0:T(8,128)(2,1)}, u32[]{:S(2)}, u32[]{:S(2)}) collective-permute-start(bf16[1,4,320,512]{3,2,1,0:T(8,128)(2,1)S(1)} %constant_dynamic-update-slice_fusion), channel_id=1, source_target_pairs={{128,0},{192,64},{129,1},{193,65},{130,2},{194,66},{131,3},{195,67... | collective-permute-start | bytes 3932168 | tf_op jit(solution)/shard_map/ppermute | solution.py:25
  32.8 133.0 %collective-permute-start.2 = (bf16[1,4,320,512]{3,2,1,0:T(8,128)(2,1)S(1)}, bf16[1,4,320,512]{3,2,1,0:T(8,128)(2,1)}, u32[]{:S(2)}, u32[]{:S(2)}) collective-permute-start(bf16[1,4,320,512]{3,2,1,0:T(8,128)(2,1)S(1)} %constant_dynamic-update-slice_fusion), channel_id=1, source_target_pairs={{64,0},{128,64},{192,128},{65,1},{129,65},{193,129},{66,2},{130,66... | collective-permute-start | bytes 3932168 | tf_op jit(solution)/shard_map/ppermute | solution.py:25
  169.7 3.7 %copy-start.1 = (bf16[3,4,322,512]{3,2,1,0:T(8,128)(2,1)S(1)}, bf16[3,4,322,512]{3,2,1,0:T(8,128)(2,1)}, u32[]{:S(2)}) copy-start(bf16[3,4,322,512]{3,2,1,0:T(8,128)(2,1)} %get-tuple-element.12) | copy-start | bytes 11870212 | tf_op jit(solution)/shard_map/cond
  173.4 10.7 %copy-start.3 = (bf16[3,3,3,512,512]{4,3,2,1,0:T(8,128)(2,1)S(1)}, bf16[3,3,3,512,512]{4,3,2,1,0:T(8,128)(2,1)}, u32[]{:S(2)}) copy-start(bf16[3,3,3,512,512]{4,3,2,1,0:T(8,128)(2,1)} %get-tuple-element.13) | copy-start | bytes 42467332 | tf_op jit(solution)/shard_map/cond
  217.8 3.7 %copy-start = (bf16[3,4,322,512]{3,2,1,0:T(8,128)(2,1)S(1)}, bf16[3,4,322,512]{3,2,1,0:T(8,128)(2,1)}, u32[]{:S(2)}) copy-start(bf16[3,4,322,512]{3,2,1,0:T(8,128)(2,1)} %fusion.113) | copy-start | bytes 11870212
  221.6 10.7 %copy-start.2 = (bf16[3,3,3,512,512]{4,3,2,1,0:T(8,128)(2,1)S(1)}, bf16[3,3,3,512,512]{4,3,2,1,0:T(8,128)(2,1)}, u32[]{:S(2)}) copy-start(bf16[3,3,3,512,512]{4,3,2,1,0:T(8,128)(2,1)} %all-gather.2.cloned.1.call-done) | copy-start | bytes 42467332
  268.0 2.3 copy-start.6
  268.0 2.3 copy-start.7
Sparse Core Ops, SparseCore 0:
  20.2 102.6 all-gather.1
where the time goes:
time: 355 us; the launch traced here: 354 us
  blocking collectives  218 us (61%)
  matrix products  78.8 us (22%)
  other arithmetic  26 us (7%)
  between operations  14.3 us (4%)
  starting transfers between devices  8.32 us (2%)
  waiting for transfers between devices  4.51 us (1%)
  local copies, waits for them, and re-layouts  3.66 us (1%)
    psum x1, blocking collectives, on_device(): total_x, total_sq = lax.psum((sum_x, sum_sq), ('tm', 'rows'))  131 us
    dot_general x54, matrix products, tap_total(): lax.dot_general(source, weights[tap_index, row_tap, col_tap], (((3,), (1,...  78.8 us
    psum x1, blocking collectives, on_device(): lax.psum((jnp.sum(act_grad, axis=(0, 1, 2)), jnp.sum(act_grad * normed, a...  74.4 us
    all_gather x1, blocking collectives, on_device(): weight_wide = lax.all_gather(conv_weight, 'tm', axis=4, tiled=True)  12.8 us
    reduce_sum x2, other arithmetic, pool_pairs(): fine_grad.reshape(frames, fine_rows // 2, 2, span_cols // 2, 2, channels)  10.9 us
    add x1, other arithmetic, tap_total(): running = piece if running is None else running + piece  9.05 us
  transfers between devices with their start and end apart: 5, of which 2 were waited for; matrix products, arithmetic and copies ran while one was open for 2% of the time, Pallas kernels for 0%

commit v1 on v0

v1 whole, which is shorter than its diff:
```python
import functools

import jax
import jax.numpy as jnp
from jax import lax
from jax.experimental import pallas as pl
from jax.experimental.pallas import tpu as pltpu
from jax.sharding import PartitionSpec as P

GROUPS = 32
YS, ZS, CS = 4, 8, 2
ROWS = YS * ZS * CS
FRAMES = 4
TAPS = 9
UNITS = ((0, 1, 2, 3), (0, 1, 2), (0, 1))


def spot(y, z, c):
    return ((y % YS) * ZS + z % ZS) * CS + c


def rows_perm(move):
    pairs = []
    for y in range(YS):
        for z in range(ZS):
            for c in range(CS):
                pairs.append((spot(y, z, c), spot(*move(y, z, c))))
    return pairs


def send_y(value, step):
    return lax.ppermute(value, "rows", rows_perm(lambda y, z, c: (y + step, z, c)))


def send_z(value, step):
    return lax.ppermute(value, "rows", rows_perm(lambda y, z, c: (y, z + step, c)))


def swap_core(value):
    return lax.ppermute(value, "rows", rows_perm(lambda y, z, c: (y, z, 1 - c)))


def send_frames(value, step):
    return lax.ppermute(value, "tm", [(i, (i + step) % FRAMES) for i in range(FRAMES)])


def pool_kernel(cot0, cot1, cot2, cot3, low, high, out2, out1, out0, sums, pooled):
    cells = out2.shape[1] // FRAMES
    fine = 2 * cells
    place = lax.axis_index("tm")
    zero = jnp.zeros((8, 128), jnp.float32)
    for band in range(3):
        sums[band, 0:8] = zero
        sums[band, 8 + fine : 16 + fine] = zero
    for k, cot in enumerate((cot0, cot1, cot2, cot3)):
        frame = lax.rem(place + FRAMES - k, FRAMES)
        upper = cot[0].astype(jnp.float32)
        lower = cot[1].astype(jnp.float32)
        sums[0, 8 : 8 + fine] = lower + high[k].astype(jnp.float32)
        sums[1, 8 : 8 + fine] = upper + lower
        sums[2, 8 : 8 + fine] = low[k].astype(jnp.float32) + upper
        for band in range(3):
            at = sums.at[band]
            before = at[pl.ds(7, cells, stride=2), :]
            even = at[pl.ds(8, cells, stride=2), :]
            odd = at[pl.ds(9, cells, stride=2), :]
            after = at[pl.ds(10, cells, stride=2), :]
            pooled[frame, band * 3 + 0] = odd + after
            pooled[frame, band * 3 + 1] = even + odd
            pooled[frame, band * 3 + 2] = before + even
    for tap in range(TAPS):
        lanes = slice(tap * 128, tap * 128 + 128)

        def put(out, unit, value):
            head = value.astype(jnp.bfloat16)
            tail = (value - head.astype(jnp.float32)).astype(jnp.bfloat16)
            out[0, unit * cells : (unit + 1) * cells, lanes] = head
            out[1, unit * cells : (unit + 1) * cells, lanes] = tail

        p0, p1, p2, p3 = (pooled[t, tap] for t in range(FRAMES))
        put(out2, 0, p0)
        put(out2, 1, p1)
        put(out2, 2, p2)
        put(out2, 3, p3)
        p01 = p0 + p1
        put(out1, 0, p01)
        put(out1, 1, p2)
        put(out1, 2, p3)
        put(out0, 0, p01 + p2)
        put(out0, 1, p3)


def pool(cots, low, high):
    cells = cots[0].shape[1] // 2
    shapes = [
        jax.ShapeDtypeStruct((2, len(units) * cells, TAPS * 128), jnp.bfloat16) for units in UNITS
    ]
    return pl.pallas_call(
        pool_kernel,
        out_shape=shapes,
        in_specs=[pl.BlockSpec(memory_space=pltpu.VMEM)] * 6,
        out_specs=[pl.BlockSpec(memory_space=pltpu.VMEM)] * 3,
        scratch_shapes=[
            pltpu.VMEM((3, 2 * cells + 16, 128), jnp.float32),
            pltpu.VMEM((FRAMES, TAPS, cells, 128), jnp.float32),
        ],
        compiler_params=pltpu.CompilerParams(vmem_limit_bytes=40 << 20),
        cost_estimate=pl.CostEstimate(flops=20_000_000, bytes_accessed=9_000_000, transcendentals=0),
    )(*cots, low, high)


def product_kernel(z_steps, *refs):
    pieces = refs[: 2 * len(z_steps)]
    left2, left1, left0, out, weights, sems = refs[2 * len(z_steps) :]
    at = lax.axis_index("rows")
    y, z, c = at // (ZS * CS), lax.rem(at // CS, ZS), lax.rem(at, CS)
    copies = []
    for side in range(2):
        core = c if side == 0 else 1 - c
        for index, (step, first) in enumerate(z_steps):
            piece = pieces[side * len(z_steps) + index]
            source_z = lax.rem(z + ZS - step, ZS)
            for j in range(piece.shape[0]):
                source_y = lax.rem(y + YS - (first + j), YS)
                row = pl.multiple_of(source_y * (ZS * CS * 8) + source_z * (CS * 8) + core * 8, 8)
                copies.append(
                    pltpu.make_async_copy(
                        piece.at[j, 0 : 3 * TAPS],
                        weights.at[:, pl.ds(row, 8), :],
                        sems.at[len(copies)],
                    )
                )
    for copy in copies:
        copy.start()
    for copy in copies:
        copy.wait()
    for n in range(out.shape[1] // 256):
        cols = slice(n * 256, n * 256 + 256)
        for tap, left in ((2, left2), (1, left1), (0, left0)):
            right = jnp.concatenate(
                [weights[tap * TAPS + t, cols, :] for t in range(TAPS)], axis=1
            )
            total = None
            for half in range(2):
                part = lax.dot_general(
                    left[half], right, (((1,), (1,)), ((), ())), preferred_element_type=jnp.float32
                )
                total = part if total is None else total + part
            if tap == 2:
                out[:, cols] = total
            else:
                out[0 : total.shape[0], cols] += total


def product(pieces, z_steps, lefts, channels):
    rows = lefts[0].shape[1]
    count = 2 * sum(piece.shape[0] for piece in pieces[: len(z_steps)])
    return pl.pallas_call(
        functools.partial(product_kernel, z_steps),
        out_shape=jax.ShapeDtypeStruct((rows, channels), jnp.float32),
        in_specs=[pl.BlockSpec(memory_space=pl.ANY)] * len(pieces)
        + [pl.BlockSpec(memory_space=pltpu.VMEM)] * 3,
        out_specs=pl.BlockSpec(memory_space=pltpu.VMEM),
        scratch_shapes=[
            pltpu.VMEM((3 * TAPS, channels, 128), jnp.bfloat16),
            pltpu.SemaphoreType.DMA((count,)),
        ],
        compiler_params=pltpu.CompilerParams(vmem_limit_bytes=40 << 20),
        cost_estimate=pl.CostEstimate(
            flops=3_400_000_000, bytes_accessed=11_000_000, transcendentals=0
        ),
    )(*pieces, *lefts)


def three_parts(value):
    head = lax.reduce_precision(value, 8, 7)
    rest = value - head
    middle = lax.reduce_precision(rest, 8, 7)
    return [part.astype(jnp.bfloat16) for part in (head, middle, rest - middle)]


def on_device(latent, norm_gain, norm_bias, conv_weight, cotangent):
    place = lax.axis_index("tm")
    cells, channels = latent.shape[2], latent.shape[3]
    fine_cols = cotangent.shape[2]
    per_group = channels // GROUPS
    cell_count = FRAMES * ROWS * cells

    own = latent[0, 0].astype(jnp.float32)
    stats = jnp.stack([jnp.sum(own, axis=0), jnp.sum(own * own, axis=0)])
    parts = jnp.stack([part.reshape(8, 128) for part in three_parts(stats)])
    message = jnp.concatenate([conv_weight.reshape(3 * TAPS, 8, 128), parts], axis=0)
    block = jnp.stack([message] + [send_y(message, step) for step in range(1, YS)])
    forth, back = block, block
    pieces, z_steps = [block], [(0, 0)]
    for step in range(1, ZS // 2):
        forth, back = send_z(forth, 1), send_z(back, -1)
        pieces += [forth, back]
        z_steps += [(step, 0), (-step, 0)]
    half = YS // 2
    pieces += [send_z(forth[:half], 1), send_z(back[half:], -1)]
    z_steps += [(ZS // 2, 0), (ZS // 2, half)]
    pieces = pieces + [swap_core(piece) for piece in pieces]

    latents = [latent[0, 0]] + [send_frames(latent[0, 0], step) for step in range(1, FRAMES)]
    split = cotangent[0].reshape(2, fine_cols, FRAMES, 128).transpose(2, 0, 1, 3)
    cots = []
    for step in range(FRAMES):
        chunk = lax.dynamic_index_in_dim(split, lax.rem(place + step, FRAMES), 0, keepdims=False)
        cots.append(chunk if step == 0 else send_frames(chunk, step))
    low = lax.ppermute(
        jnp.stack([cot[1] for cot in cots]), "rows", [(i, i + 1) for i in range(ROWS - 1)]
    )
    high = lax.ppermute(
        jnp.stack([cot[0] for cot in cots]), "rows", [(i + 1, i) for i in range(ROWS - 1)]
    )
    lefts = pool(cots, low, high)
    partial = product(pieces, tuple(z_steps), lefts, channels).reshape(FRAMES, cells, channels)

    gathered = sum(
        jnp.sum(piece[:, 3 * TAPS :].astype(jnp.float32), axis=(0, 1)) for piece in pieces
    ).reshape(2, channels)
    total = gathered + sum(send_frames(gathered, step) for step in range(1, FRAMES))
    group = total.reshape(2, GROUPS, per_group).sum(axis=2) / (cell_count * per_group)
    group_mean = group[0]
    group_var = group[1] - group_mean * group_mean
    inv_std = lax.rsqrt(group_var + 1e-06)
    mean_chan = jnp.repeat(group_mean, per_group)
    inv_chan = jnp.repeat(inv_std, per_group)

    def slope(features):
        normed = (features.astype(jnp.float32) - mean_chan) * inv_chan
        pre = normed * norm_gain + norm_bias
        sigmoid_pre = jax.nn.sigmoid(pre)
        return normed, sigmoid_pre * (1.0 + pre * (1.0 - sigmoid_pre))

    here = []
    for step in range(FRAMES):
        frame = lax.rem(place + FRAMES - step, FRAMES)
        here.append(lax.dynamic_index_in_dim(partial, frame, 0, keepdims=False))
    sum_act = jnp.zeros((channels,), jnp.float32)
    sum_scaled = jnp.zeros((channels,), jnp.float32)
    for step in range(FRAMES):
        normed, gate = slope(latents[step])
        act = here[step] * gate
        sum_act = sum_act + jnp.sum(act, axis=0)
        sum_scaled = sum_scaled + jnp.sum(act * normed, axis=0)
    up_grad = here[0] + sum(
        send_frames(here[FRAMES - step], step) for step in range(1, FRAMES)
    )
    sums = jnp.stack([sum_act, sum_scaled]).reshape(1, 8, 128)
    sums = lax.all_to_all(
        jnp.broadcast_to(sums, (ROWS, 8, 128)), "rows", 0, 0, tiled=True
    ).sum(axis=0)
    sums = sums + sum(send_frames(sums, step) for step in range(1, FRAMES))
    sum_act, sum_scaled = sums.reshape(2, channels)

    gain_grad = sum_scaled / cell_count
    bias_grad = sum_act / cell_count
    scale = cell_count * per_group
    mean_q = (norm_gain * sum_act).reshape(GROUPS, per_group).sum(axis=1) / scale
    mean_qn = (norm_gain * sum_scaled).reshape(GROUPS, per_group).sum(axis=1) / scale
    normed, gate = slope(latents[0])
    latent_grad = inv_chan * (
        up_grad * gate * norm_gain
        - jnp.repeat(mean_q, per_group)
        - normed * jnp.repeat(mean_qn, per_group)
    )
    return (latent_grad.reshape(1, 1, cells, channels), gain_grad, bias_grad)


def solution(mesh):
    placed = (
        P("tm", "rows", None, None),
        P(),
        P(),
        P(None, None, None, "rows", "tm"),
        P("tm", "rows", None, None),
    )
    return jax.shard_map(
        on_device,
        mesh=mesh,
        in_specs=placed,
        out_specs=(P("tm", "rows", None, None), P(), P()),
        check_vma=False,
    )
```

time: 355 us -> 147 us (0.41)
  blocking collectives: 218 us -> 22.8 us
  matrix products: 78.8 us -> 0 us
  starting transfers between devices: 8.32 us -> 46.7 us
  waiting for transfers between devices: 4.51 us -> 29.6 us
  local copies, waits for them, and re-layouts: 3.66 us -> 26.8 us
  other arithmetic: 26 us -> 10.3 us
  between operations: 14.3 us -> 1.14 us
  Pallas kernels: 0 us -> 7.24 us
    psum x2 -> x0, blocking collectives: 205 us -> none  [the longest x1 131 us: on_device(): total_x, total_sq = lax.psum((sum_x, sum_sq), ('tm', 'rows'))]
    dot_general x54 -> x0, matrix products: 78.8 us -> none  [tap_total(): lax.dot_general(source, weights[tap_index, row_tap, col_tap], (((3,), (1,...]
    ppermute x4 -> x37, starting transfers between devices: 8.28 us -> 46.7 us  [the longest x15 23.6 us: send_frames(): lax.ppermute(value, 'tm', [(i, (i + step) % FRAMES) for i in range(FRAMES)])]
    ppermute x4 -> x37, waiting for transfers between devices: 4.5 us -> 29.6 us  [the longest x15 18 us: send_frames(): lax.ppermute(value, 'tm', [(i, (i + step) % FRAMES) for i in range(FRAMES)])]
    all_to_all x0 -> x1, blocking collectives: none -> 22.8 us  [on_device(): lax.all_to_all(jnp.broadcast_to(sums, (ROWS, 8, 128)), 'rows', 0, 0, tile...]
    unnamed x14 -> x56, local copies, waits for them, and re-layouts: 0.1 us -> 22.8 us
    all_gather x1 -> x0, blocking collectives: 12.8 us -> none  [on_device(): weight_wide = lax.all_gather(conv_weight, 'tm', axis=4, tiled=True)]
    add x1 -> x5, other arithmetic: 9.05 us -> 0.74 us  [the longest x1 0.69 us: on_device(): sums = sums + sum((send_frames(sums, step) for step in range(1, FRAMES)))]
  transfers between devices with their start and end apart: 5 -> 37, of which waited for: 2 -> 9; matrix products, arithmetic and copies ran while one was open for 2% -> 5% of each run, Pallas kernels for 0% -> 5%
where the time goes in v1:
time: 147 us; the launch traced here: 144 us
  starting transfers between devices  46.7 us (32%)
  waiting for transfers between devices  29.6 us (20%)
  local copies, waits for them, and re-layouts  26.8 us (18%)
  blocking collectives  22.8 us (16%)
  other arithmetic  10.3 us (7%)
  Pallas kernels  7.24 us (5%)
    ppermute x15, starting transfers between devices, send_frames(): lax.ppermute(value, 'tm', [(i, (i + step) % FRAMES) for i in range(FRAMES)])  23.6 us
    unnamed x56, local copies, waits for them, and re-layouts  22.8 us
    all_to_all x1, blocking collectives, on_device(): lax.all_to_all(jnp.broadcast_to(sums, (ROWS, 8, 128)), 'rows', 0, 0, tile...  22.8 us
    ppermute x15, waiting for transfers between devices, send_frames(): lax.ppermute(value, 'tm', [(i, (i + step) % FRAMES) for i in range(FRAMES)])  18 us
    ppermute x8, starting transfers between devices, send_z(): lax.ppermute(value, 'rows', rows_perm(lambda y, z, c: (y, z + step, c)))  10.7 us
    ppermute x8, waiting for transfers between devices, send_z(): lax.ppermute(value, 'rows', rows_perm(lambda y, z, c: (y, z + step, c)))  9.86 us
    ppermute x3, starting transfers between devices, send_y(): lax.ppermute(value, 'rows', rows_perm(lambda y, z, c: (y + step, z, c)))  5.9 us
    pallas_call x1, Pallas kernels, product(): pl.pallas_call(functools.partial(product_kernel, z_steps), out_shape=jax....  5.78 us
  transfers between devices with their start and end apart: 37, of which 9 were waited for; matrix products, arithmetic and copies ran while one was open for 5% of the time, Pallas kernels for 5%

profile of v1, /device:TPU:32, one launch (start us, length us, event | category | flops | bytes accessed | tf_op | source)
XLA Modules:
  0.0 144.5 jit_solution(16767860503063278453)
XLA Ops:
  2.5 1.7 %collective-permute-start = (bf16[30,8,128]{2,1,0:T(8,128)(2,1)S(1)}, bf16[30,8,128]{2,1,0:T(8,128)(2,1)S(1)}, u32[]{:S(2)}, u32[]{:S(2)}) collective-permute-start(bf16[30,8,128]{2,1,0:T(8,128)(2,1)S(1)} %get-tuple-element.46), channel_id=1, source_target_pairs={{0,16},{1,17},{2,18},{3,19},{4,20},{5,21},{6,22},{7,23},{8,24},{9,... | collective-permute-start | bytes 184328 | tf_op jit(solution)/shard_map/ppermute | solution.py:32
  4.1 2.9 %collective-permute-start.1 = (bf16[30,8,128]{2,1,0:T(8,128)(2,1)S(1)}, bf16[30,8,128]{2,1,0:T(8,128)(2,1)S(1)}, u32[]{:S(2)}, u32[]{:S(2)}) collective-permute-start(bf16[30,8,128]{2,1,0:T(8,128)(2,1)S(1)} %get-tuple-element.46), channel_id=1, source_target_pairs={{0,32},{1,33},{2,34},{3,35},{4,36},{5,37},{6,38},{7,39},{8,40},{9,... | collective-permute-start | bytes 184328 | tf_op jit(solution)/shard_map/ppermute | solution.py:32
  8.4 1.6 %reshape_squeeze.3 = bf16[2,320,4,128]{3,2,1,0:T(4,128)(2,1)S(1)} reshape(bf16[1,2,320,512]{3,2,1,0:T(8,128)(2,1)} %param.9) | data formatting | bytes 1310720 | tf_op jit(solution)/shard_map/reshape;squeeze | solution.py:206
  11.5 1.6 %collective-permute-start.23 = (bf16[2,320,128]{2,1,0:T(8,128)(2,1)S(1)}, bf16[2,320,128]{2,1,0:T(8,128)(2,1)S(1)}, u32[]{:S(2)}, u32[]{:S(2)}) collective-permute-start(bf16[2,320,128]{2,1,0:T(8,128)(2,1)S(1)} %bitcast.91), channel_id=1, source_target_pairs={{0,64},{64,128},{128,192},{192,0},{1,65},{65,129},{129,193},{193,1... | collective-permute-start | bytes 491528 | tf_op jit(solution)/shard_map/ppermute | solution.py:44
  13.0 2.8 %collective-permute-start.24 = (bf16[2,320,128]{2,1,0:T(8,128)(2,1)S(1)}, bf16[2,320,128]{2,1,0:T(8,128)(2,1)S(1)}, u32[]{:S(2)}, u32[]{:S(2)}) collective-permute-start(bf16[2,320,128]{2,1,0:T(8,128)(2,1)S(1)} %bitcast.90), channel_id=1, source_target_pairs={{0,128},{64,192},{128,0},{192,64},{1,129},{65,193},{129,1},{193,65... | collective-permute-start | bytes 491528 | tf_op jit(solution)/shard_map/ppermute | solution.py:44
  16.0 1.5 %collective-permute-start.25 = (bf16[2,320,128]{2,1,0:T(8,128)(2,1)S(1)}, bf16[2,320,128]{2,1,0:T(8,128)(2,1)S(1)}, u32[]{:S(2)}, u32[]{:S(2)}) collective-permute-start(bf16[2,320,128]{2,1,0:T(8,128)(2,1)S(1)} %bitcast.92), channel_id=1, source_target_pairs={{0,192},{64,0},{128,64},{192,128},{1,193},{65,1},{129,65},{193,129... | collective-permute-start | bytes 491528 | tf_op jit(solution)/shard_map/ppermute | solution.py:44
  17.5 2.0 %collective-permute-start.3 = (bf16[4,30,8,128]{3,2,1,0:T(8,128)(2,1)S(1)}, bf16[4,30,8,128]{3,2,1,0:T(8,128)(2,1)S(1)}, u32[]{:S(2)}, u32[]{:S(2)}) collective-permute-start(bf16[4,30,8,128]{3,2,1,0:T(8,128)(2,1)S(1)} %pad_maximum_fusion.2.refs_0_), channel_id=1, source_target_pairs={{0,2},{1,3},{2,4},{3,5},{4,6},{5,7},{6,8},{7,9},{8,10},{9,11},{10,... | collective-permute-start | bytes 737288 | tf_op jit(solution)/shard_map/ppermute | solution.py:36
  19.8 2.6 %collective-permute-done.24.cot2 = bf16[2,320,128]{2,1,0:T(8,128)(2,1)S(1)} collective-permute-done((bf16[2,320,128]{2,1,0:T(8,128)(2,1)S(1)}, bf16[2,320,128]{2,1,0:T(8,128)(2,1)S(1)}, u32[]{:S(2)}, u32[]{:S(2)}) %collective-permute-start.24) | collective-permute-done | bytes 163872 | tf_op jit(solution)/shard_map/ppermute | solution.py:44
  22.4 3.5 %collective-permute-start.27 = (bf16[4,320,128]{2,1,0:T(8,128)(2,1)S(1)}, bf16[4,320,128]{2,1,0:T(8,128)(2,1)S(1)}, u32[]{:S(2)}, u32[]{:S(2)}) collective-permute-start(bf16[4,320,128]{2,1,0:T(8,128)(2,1)S(1)} %pad_maximum_fusion.1), channel_id=1, source_target_pairs={{1,0},{2,1},{3,2},{4,3},{5,4},{6,5},{7,6},{8,7},{9,8},{10,9},{11,1... | collective-permute-start | bytes 983048 | tf_op jit(solution)/shard_map/ppermute | solution.py:214
  26.0 1.9 %collective-permute-start.26 = (bf16[4,320,128]{2,1,0:T(8,128)(2,1)S(1)}, bf16[4,320,128]{2,1,0:T(8,128)(2,1)S(1)}, u32[]{:S(2)}, u32[]{:S(2)}) collective-permute-start(bf16[4,320,128]{2,1,0:T(8,128)(2,1)S(1)} %pad_maximum_fusion), channel_id=1, source_target_pairs={{0,1},{1,2},{2,3},{3,4},{4,5},{5,6},{6,7},{7,8},{8,9},{9,10},{10,1... | collective-permute-start | bytes 983048 | tf_op jit(solution)/shard_map/ppermute | solution.py:211
  28.4 1.7 %collective-permute-start.5 = (bf16[4,30,8,128]{3,2,1,0:T(8,128)(2,1)S(1)}, bf16[4,30,8,128]{3,2,1,0:T(8,128)(2,1)S(1)}, u32[]{:S(2)}, u32[]{:S(2)}) collective-permute-start(bf16[4,30,8,128]{3,2,1,0:T(8,128)(2,1)S(1)} %collective-permute-done.3.refs_1_), channel_id=1, source_target_pairs={{0,2},{1,3},{2,4},{3,5},{4,6},{5,7},{6,8},{7,9},{8,10},{9,11},{10,... | collective-permute-start | bytes 737288 | tf_op jit(solution)/shard_map/ppermute | solution.py:36
  30.7 2.3 %collective-permute-start.33 = (bf16[160,512]{1,0:T(8,128)(2,1)}, bf16[160,512]{1,0:T(8,128)(2,1)}, u32[]{:S(2)}, u32[]{:S(2)}) collective-permute-start(bf16[160,512]{1,0:T(8,128)(2,1)} %bitcast.1), channel_id=1, source_target_pairs={{0,192},{64,0},{128,64},{192,128},{1,193},{65,1},{129,65},{193,129... | collective-permute-start | bytes 491528 | tf_op jit(solution)/shard_map/ppermute | solution.py:44
  34.4 1.5 %shard_map.76 = (bf16[2,640,1152]{2,1,0:T(8,128)(2,1)S(1)}, bf16[2,480,1152]{2,1,0:T(8,128)(2,1)S(1)}, bf16[2,320,1152]{2,1,0:T(8,128)(2,1)S(1)}) custom-call(bf16[2,320,128]{2,1,0:T(8,128)(2,1)S(1)} %bitcast.89, bf16[2,320,128]{2,1,0:T(8,128)(2,1)S(1)} %collective-permute-done.23.cot1, bf16[2,320,128]{2,1,0:T(8,128)(2,1)S(1)} %collective-permute-done.24.cot2, ...), custom_call_target="tpu_custom_call" | custom-call | flops 20000000 | bytes 9000000 | tf_op jit(solution)/shard_map/pallas_call | solution.py:98
  35.9 1.6 %copy-done.18 = bf16[2,640,1152]{2,1,0:T(8,128)(2,1)} copy-done((bf16[2,640,1152]{2,1,0:T(8,128)(2,1)}, bf16[2,640,1152]{2,1,0:T(8,128)(2,1)S(1)}, u32[]{:S(2)}) %copy-start.18) | copy-done | bytes 2949144
  40.0 3.2 %collective-permute-start.8 = (bf16[4,30,8,128]{3,2,1,0:T(8,128)(2,1)S(1)}, bf16[4,30,8,128]{3,2,1,0:T(8,128)(2,1)S(1)}, u32[]{:S(2)}, u32[]{:S(2)}) collective-permute-start(bf16[4,30,8,128]{3,2,1,0:T(8,128)(2,1)S(1)} %collective-permute-done.6.refs_4_), channel_id=1, source_target_pairs={{0,14},{1,15},{2,0},{3,1},{4,2},{5,3},{6,4},{7,5},{8,6},{9,7},{10,... | collective-permute-start | bytes 737288 | tf_op jit(solution)/shard_map/ppermute | solution.py:36
  44.3 8.3 %collective-permute-done.7.refs_5_ = bf16[4,30,8,128]{3,2,1,0:T(8,128)(2,1)S(1)} collective-permute-done((bf16[4,30,8,128]{3,2,1,0:T(8,128)(2,1)S(1)}, bf16[4,30,8,128]{3,2,1,0:T(8,128)(2,1)S(1)}, u32[]{:S(2)}, u32[]{:S(2)}) %collective-permute-start.7) | collective-permute-done | bytes 245792 | tf_op jit(solution)/shard_map/ppermute | solution.py:36
  52.8 3.0 %collective-permute-start.10 = (bf16[2,30,8,128]{3,2,1,0:T(8,128)(2,1)S(1)}, bf16[2,30,8,128]{3,2,1,0:T(8,128)(2,1)S(1)}, u32[]{:S(2)}, u32[]{:S(2)}) collective-permute-start(bf16[2,30,8,128]{3,2,1,0:T(8,128)(2,1)S(1)} %slice.139), channel_id=1, source_target_pairs={{0,14},{1,15},{2,0},{3,1},{4,2},{5,3},{6,4},{7,5},{8,6},{9,7},{10,... | collective-permute-start | bytes 368648 | tf_op jit(solution)/shard_map/ppermute | solution.py:36
  57.5 1.6 %collective-permute-done.10.refs_8_ = bf16[2,30,8,128]{3,2,1,0:T(8,128)(2,1)S(1)} collective-permute-done((bf16[2,30,8,128]{3,2,1,0:T(8,128)(2,1)S(1)}, bf16[2,30,8,128]{3,2,1,0:T(8,128)(2,1)S(1)}, u32[]{:S(2)}, u32[]{:S(2)}) %collective-permute-start.10) | collective-permute-done | bytes 122912 | tf_op jit(solution)/shard_map/ppermute | solution.py:36
  63.7 2.0 %collective-permute-start.20 = (f32[2,512]{1,0:T(2,128)S(1)}, f32[2,512]{1,0:T(2,128)S(1)}, u32[]{:S(2)}, u32[]{:S(2)}) collective-permute-start(f32[2,512]{1,0:T(2,128)S(1)} %add.294), channel_id=1, source_target_pairs={{0,64},{64,128},{128,192},{192,0},{1,65},{65,129},{129,193},{193,1... | collective-permute-start | bytes 12296 | tf_op jit(solution)/shard_map/ppermute | solution.py:44
  65.7 1.8 %collective-permute-start.21 = (f32[2,512]{1,0:T(2,128)S(1)}, f32[2,512]{1,0:T(2,128)S(1)}, u32[]{:S(2)}, u32[]{:S(2)}) collective-permute-start(f32[2,512]{1,0:T(2,128)S(1)} %add.294), channel_id=1, source_target_pairs={{0,128},{64,192},{128,0},{192,64},{1,129},{65,193},{129,1},{193,65... | collective-permute-start | bytes 12296 | tf_op jit(solution)/shard_map/ppermute | solution.py:44
  77.1 1.8 %copy-done.19 = bf16[2,640,1152]{2,1,0:T(8,128)(2,1)S(1)} copy-done((bf16[2,640,1152]{2,1,0:T(8,128)(2,1)S(1)}, bf16[2,640,1152]{2,1,0:T(8,128)(2,1)}, u32[]{:S(2)}) %copy-start.19) | copy-done | bytes 2949144
  79.0 1.6 %copy-done.21 = bf16[2,480,1152]{2,1,0:T(8,128)(2,1)S(1)} copy-done((bf16[2,480,1152]{2,1,0:T(8,128)(2,1)S(1)}, bf16[2,480,1152]{2,1,0:T(8,128)(2,1)}, u32[]{:S(2)}) %copy-start.21) | copy-done | bytes 2211864
  82.0 5.8 %shard_map.77 = f32[640,512]{1,0:T(8,128)S(1)} custom-call(bf16[4,30,8,128]{3,2,1,0:T(8,128)(2,1)S(1)} %pad_maximum_fusion.2.refs_0_, bf16[4,30,8,128]{3,2,1,0:T(8,128)(2,1)S(1)} %collective-permute-done.3.refs_1_, bf16[4,30,8,128]{3,2,1,0:T(8,128)(2,1)S(1)} %collective-permute-done.4.refs_2_, bf16[4,30,8,128]{3,2,1,0:T(8,128)(2,1)S(1)} %collective-permute-done.5.refs_3_, ...), custom_call_target="tpu_custom_call" | custom-call | flops 3400000000 | bytes 11000000 | tf_op jit(solution)/shard_map/pallas_call | solution.py:158
  90.7 4.6 %collective-permute-done.32 = bf16[160,512]{1,0:T(8,128)(2,1)S(1)} collective-permute-done((bf16[160,512]{1,0:T(8,128)(2,1)}, bf16[160,512]{1,0:T(8,128)(2,1)S(1)}, u32[]{:S(2)}, u32[]{:S(2)}) %collective-permute-start.32) | collective-permute-done | bytes 163872 | tf_op jit(solution)/shard_map/ppermute | solution.py:44
  95.3 1.6 %fusion.27 = (f32[512]{0:T(512)S(1)}, f32[512]{0:T(512)S(1)}, f32[512]{0:T(512)S(1)}, f32[512]{0:T(512)S(1)}, f32[160,512]{1,0:T(8,128)S(1)}, /*index=5*/f32[160...) fusion(f32[160,512]{1,0:T(8,128)S(1)} %get-tuple-element.25, f32[512]{0:T(512)S(1)} %mul.151, ...), kind=kLoop, calls=%fused_computation.97 | loop fusion | flops 3930112 | bytes 3293196 | tf_op jit(solution)/shard_map/reduce_sum | solution.py:246
  98.1 22.8 %all_to_all.5 = f32[64,8,128]{2,1,0:T(8,128)S(1)} all-to-all(f32[64,8,128]{2,1,0:T(8,128)S(1)} %broadcast_in_dim.15), channel_id=1, replica_groups=mesh['tm'=4,'rows'=64] {'rows'}, dimensions={0} | all-to-all | bytes 524288 | tf_op jit(solution)/shard_map/all_to_all | solution.py:252
  121.8 2.3 %collective-permute-start.35 = (f32[8,128]{1,0:T(8,128)}, f32[8,128]{1,0:T(8,128)S(1)}, u32[]{:S(2)}, u32[]{:S(2)}) collective-permute-start(f32[8,128]{1,0:T(8,128)} %reduce_sum.356), channel_id=1, source_target_pairs={{0,128},{64,192},{128,0},{192,64},{1,129},{65,193},{129,1},{193,65... | collective-permute-start | bytes 12296 | tf_op jit(solution)/shard_map/ppermute | solution.py:44
  124.9 2.8 %collective-permute-start.29 = (f32[160,512]{1,0:T(8,128)S(1)}, f32[160,512]{1,0:T(8,128)S(1)}, u32[]{:S(2)}, u32[]{:S(2)}) collective-permute-start(f32[160,512]{1,0:T(8,128)S(1)} %get-tuple-element.28), channel_id=1, source_target_pairs={{0,128},{64,192},{128,0},{192,64},{1,129},{65,193},{129,1},{193,65... | collective-permute-start | bytes 983048 | tf_op jit(solution)/shard_map/ppermute | solution.py:44
  131.8 5.4 %collective-permute-done.29 = f32[160,512]{1,0:T(8,128)S(1)} collective-permute-done((f32[160,512]{1,0:T(8,128)S(1)}, f32[160,512]{1,0:T(8,128)S(1)}, u32[]{:S(2)}, u32[]{:S(2)}) %collective-permute-start.29) | collective-permute-done | bytes 327712 | tf_op jit(solution)/shard_map/ppermute | solution.py:44
  137.1 3.7 %collective-permute-done.30 = f32[160,512]{1,0:T(8,128)S(1)} collective-permute-done((f32[160,512]{1,0:T(8,128)S(1)}, f32[160,512]{1,0:T(8,128)S(1)}, u32[]{:S(2)}, u32[]{:S(2)}) %collective-permute-start.30) | collective-permute-done | bytes 327712 | tf_op jit(solution)/shard_map/ppermute | solution.py:44
  140.8 1.7 %collective-permute-done.28 = f32[160,512]{1,0:T(8,128)S(1)} collective-permute-done((f32[160,512]{1,0:T(8,128)S(1)}, f32[160,512]{1,0:T(8,128)S(1)}, u32[]{:S(2)}, u32[]{:S(2)}) %collective-permute-start.28) | collective-permute-done | bytes 327712 | tf_op jit(solution)/shard_map/ppermute | solution.py:44
  142.6 1.9 %fusion.16 = f32[1,1,160,512]{3,2,1,0:T(8,128)} fusion(f32[160,512]{1,0:T(8,128)S(1)} %collective-permute-done.30, f32[160,512]{1,0:T(8,128)S(1)} %collective-permute-done.28, f32[160,512]{1,0:T(8,128)S(1)} %collective-permute-done.29, f32[4,160,512]{2,1,0:T(8,128)S(1)} %bitcast.87, s32[]{:T(128)S(6)} %select_n.24, f32[512]{0:T(512)S(1)} %mul.182, ...), kind=kLoop, calls=%fused_computation.19 | loop fusion | flops 1720320 | bytes 1814532 | tf_op jit(solution)/shard_map/reshape | solution.py:269
  (170 shorter events, 38.4 us)
Async XLA Ops:
  2.5 13.5 %collective-permute-start = (bf16[30,8,128]{2,1,0:T(8,128)(2,1)S(1)}, bf16[30,8,128]{2,1,0:T(8,128)(2,1)S(1)}, u32[]{:S(2)}, u32[]{:S(2)}) collective-permute-start(bf16[30,8,128]{2,1,0:T(8,128)(2,1)S(1)} %get-tuple-element.46), channel_id=1, source_target_pairs={{0,16},{1,17},{2,18},{3,19},{4,20},{5,21},{6,22},{7,23},{8,24},{9,... | collective-permute-start | bytes 184328 | tf_op jit(solution)/shard_map/ppermute | solution.py:32
  4.1 13.3 %collective-permute-start.1 = (bf16[30,8,128]{2,1,0:T(8,128)(2,1)S(1)}, bf16[30,8,128]{2,1,0:T(8,128)(2,1)S(1)}, u32[]{:S(2)}, u32[]{:S(2)}) collective-permute-start(bf16[30,8,128]{2,1,0:T(8,128)(2,1)S(1)} %get-tuple-element.46), channel_id=1, source_target_pairs={{0,32},{1,33},{2,34},{3,35},{4,36},{5,37},{6,38},{7,39},{8,40},{9,... | collective-permute-start | bytes 184328 | tf_op jit(solution)/shard_map/ppermute | solution.py:32
  7.0 10.4 %collective-permute-start.2 = (bf16[30,8,128]{2,1,0:T(8,128)(2,1)S(1)}, bf16[30,8,128]{2,1,0:T(8,128)(2,1)S(1)}, u32[]{:S(2)}, u32[]{:S(2)}) collective-permute-start(bf16[30,8,128]{2,1,0:T(8,128)(2,1)S(1)} %get-tuple-element.46), channel_id=1, source_target_pairs={{0,48},{1,49},{2,50},{3,51},{4,52},{5,53},{6,54},{7,55},{8,56},{9,... | collective-permute-start | bytes 184328 | tf_op jit(solution)/shard_map/ppermute | solution.py:32
  11.5 8.2 %collective-permute-start.23 = (bf16[2,320,128]{2,1,0:T(8,128)(2,1)S(1)}, bf16[2,320,128]{2,1,0:T(8,128)(2,1)S(1)}, u32[]{:S(2)}, u32[]{:S(2)}) collective-permute-start(bf16[2,320,128]{2,1,0:T(8,128)(2,1)S(1)} %bitcast.91), channel_id=1, source_target_pairs={{0,64},{64,128},{128,192},{192,0},{1,65},{65,129},{129,193},{193,1... | collective-permute-start | bytes 491528 | tf_op jit(solution)/shard_map/ppermute | solution.py:44
  13.0 9.3 %collective-permute-start.24 = (bf16[2,320,128]{2,1,0:T(8,128)(2,1)S(1)}, bf16[2,320,128]{2,1,0:T(8,128)(2,1)S(1)}, u32[]{:S(2)}, u32[]{:S(2)}) collective-permute-start(bf16[2,320,128]{2,1,0:T(8,128)(2,1)S(1)} %bitcast.90), channel_id=1, source_target_pairs={{0,128},{64,192},{128,0},{192,64},{1,129},{65,193},{129,1},{193,65... | collective-permute-start | bytes 491528 | tf_op jit(solution)/shard_map/ppermute | solution.py:44
  16.0 6.4 %collective-permute-start.25 = (bf16[2,320,128]{2,1,0:T(8,128)(2,1)S(1)}, bf16[2,320,128]{2,1,0:T(8,128)(2,1)S(1)}, u32[]{:S(2)}, u32[]{:S(2)}) collective-permute-start(bf16[2,320,128]{2,1,0:T(8,128)(2,1)S(1)} %bitcast.92), channel_id=1, source_target_pairs={{0,192},{64,0},{128,64},{192,128},{1,193},{65,1},{129,65},{193,129... | collective-permute-start | bytes 491528 | tf_op jit(solution)/shard_map/ppermute | solution.py:44
  17.5 10.9 %collective-permute-start.3 = (bf16[4,30,8,128]{3,2,1,0:T(8,128)(2,1)S(1)}, bf16[4,30,8,128]{3,2,1,0:T(8,128)(2,1)S(1)}, u32[]{:S(2)}, u32[]{:S(2)}) collective-permute-start(bf16[4,30,8,128]{3,2,1,0:T(8,128)(2,1)S(1)} %pad_maximum_fusion.2.refs_0_), channel_id=1, source_target_pairs={{0,2},{1,3},{2,4},{3,5},{4,6},{5,7},{6,8},{7,9},{8,10},{9,11},{10,... | collective-permute-start | bytes 737288 | tf_op jit(solution)/shard_map/ppermute | solution.py:36
  19.5 8.4 %collective-permute-start.4 = (bf16[4,30,8,128]{3,2,1,0:T(8,128)(2,1)S(1)}, bf16[4,30,8,128]{3,2,1,0:T(8,128)(2,1)S(1)}, u32[]{:S(2)}, u32[]{:S(2)}) collective-permute-start(bf16[4,30,8,128]{3,2,1,0:T(8,128)(2,1)S(1)} %pad_maximum_fusion.2.refs_0_), channel_id=1, source_target_pairs={{0,14},{1,15},{2,0},{3,1},{4,2},{5,3},{6,4},{7,5},{8,6},{9,7},{10,... | collective-permute-start | bytes 737288 | tf_op jit(solution)/shard_map/ppermute | solution.py:36
  19.7 10.5 %collective-permute-start.11 = (bf16[4,30,8,128]{3,2,1,0:T(8,128)(2,1)S(1)}, bf16[4,30,8,128]{3,2,1,0:T(8,128)(2,1)S(1)}, u32[]{:S(2)}, u32[]{:S(2)}) collective-permute-start(bf16[4,30,8,128]{3,2,1,0:T(8,128)(2,1)S(1)} %pad_maximum_fusion.2.refs_0_), channel_id=1, source_target_pairs={{0,1},{1,0},{2,3},{3,2},{4,5},{5,4},{6,7},{7,6},{8,9},{9,8},{10,11... | collective-permute-start | bytes 737288 | tf_op jit(solution)/shard_map/ppermute | solution.py:40
  22.4 8.3 %collective-permute-start.27 = (bf16[4,320,128]{2,1,0:T(8,128)(2,1)S(1)}, bf16[4,320,128]{2,1,0:T(8,128)(2,1)S(1)}, u32[]{:S(2)}, u32[]{:S(2)}) collective-permute-start(bf16[4,320,128]{2,1,0:T(8,128)(2,1)S(1)} %pad_maximum_fusion.1), channel_id=1, source_target_pairs={{1,0},{2,1},{3,2},{4,3},{5,4},{6,5},{7,6},{8,7},{9,8},{10,9},{11,1... | collective-permute-start | bytes 983048 | tf_op jit(solution)/shard_map/ppermute | solution.py:214
  26.0 8.4 %collective-permute-start.26 = (bf16[4,320,128]{2,1,0:T(8,128)(2,1)S(1)}, bf16[4,320,128]{2,1,0:T(8,128)(2,1)S(1)}, u32[]{:S(2)}, u32[]{:S(2)}) collective-permute-start(bf16[4,320,128]{2,1,0:T(8,128)(2,1)S(1)} %pad_maximum_fusion), channel_id=1, source_target_pairs={{0,1},{1,2},{2,3},{3,4},{4,5},{5,6},{6,7},{7,8},{8,9},{9,10},{10,1... | collective-permute-start | bytes 983048 | tf_op jit(solution)/shard_map/ppermute | solution.py:211
  27.9 12.1 %collective-permute-start.6 = (bf16[4,30,8,128]{3,2,1,0:T(8,128)(2,1)S(1)}, bf16[4,30,8,128]{3,2,1,0:T(8,128)(2,1)S(1)}, u32[]{:S(2)}, u32[]{:S(2)}) collective-permute-start(bf16[4,30,8,128]{3,2,1,0:T(8,128)(2,1)S(1)} %collective-permute-done.4.refs_2_), channel_id=1, source_target_pairs={{0,14},{1,15},{2,0},{3,1},{4,2},{5,3},{6,4},{7,5},{8,6},{9,7},{10,... | collective-permute-start | bytes 737288 | tf_op jit(solution)/shard_map/ppermute | solution.py:36
  28.4 14.8 %collective-permute-start.5 = (bf16[4,30,8,128]{3,2,1,0:T(8,128)(2,1)S(1)}, bf16[4,30,8,128]{3,2,1,0:T(8,128)(2,1)S(1)}, u32[]{:S(2)}, u32[]{:S(2)}) collective-permute-start(bf16[4,30,8,128]{3,2,1,0:T(8,128)(2,1)S(1)} %collective-permute-done.3.refs_1_), channel_id=1, source_target_pairs={{0,2},{1,3},{2,4},{3,5},{4,6},{5,7},{6,8},{7,9},{8,10},{9,11},{10,... | collective-permute-start | bytes 737288 | tf_op jit(solution)/shard_map/ppermute | solution.py:36
  30.2 13.2 %collective-permute-start.13 = (bf16[4,30,8,128]{3,2,1,0:T(8,128)(2,1)S(1)}, bf16[4,30,8,128]{3,2,1,0:T(8,128)(2,1)S(1)}, u32[]{:S(2)}, u32[]{:S(2)}) collective-permute-start(bf16[4,30,8,128]{3,2,1,0:T(8,128)(2,1)S(1)} %collective-permute-done.4.refs_2_), channel_id=1, source_target_pairs={{0,1},{1,0},{2,3},{3,2},{4,5},{5,4},{6,7},{7,6},{8,9},{9,8},{10,11... | collective-permute-start | bytes 737288 | tf_op jit(solution)/shard_map/ppermute | solution.py:40
  30.7 58.9 %collective-permute-start.33 = (bf16[160,512]{1,0:T(8,128)(2,1)}, bf16[160,512]{1,0:T(8,128)(2,1)}, u32[]{:S(2)}, u32[]{:S(2)}) collective-permute-start(bf16[160,512]{1,0:T(8,128)(2,1)} %bitcast.1), channel_id=1, source_target_pairs={{0,192},{64,0},{128,64},{192,128},{1,193},{65,1},{129,65},{193,129... | collective-permute-start | bytes 491528 | tf_op jit(solution)/shard_map/ppermute | solution.py:44
  34.4 9.8 %collective-permute-start.12 = (bf16[4,30,8,128]{3,2,1,0:T(8,128)(2,1)S(1)}, bf16[4,30,8,128]{3,2,1,0:T(8,128)(2,1)S(1)}, u32[]{:S(2)}, u32[]{:S(2)}) collective-permute-start(bf16[4,30,8,128]{3,2,1,0:T(8,128)(2,1)S(1)} %collective-permute-done.3.refs_1_), channel_id=1, source_target_pairs={{0,1},{1,0},{2,3},{3,2},{4,5},{5,4},{6,7},{7,6},{8,9},{9,8},{10,11... | collective-permute-start | bytes 737288 | tf_op jit(solution)/shard_map/ppermute | solution.py:40
  40.0 12.6 %collective-permute-start.8 = (bf16[4,30,8,128]{3,2,1,0:T(8,128)(2,1)S(1)}, bf16[4,30,8,128]{3,2,1,0:T(8,128)(2,1)S(1)}, u32[]{:S(2)}, u32[]{:S(2)}) collective-permute-start(bf16[4,30,8,128]{3,2,1,0:T(8,128)(2,1)S(1)} %collective-permute-done.6.refs_4_), channel_id=1, source_target_pairs={{0,14},{1,15},{2,0},{3,1},{4,2},{5,3},{6,4},{7,5},{8,6},{9,7},{10,... | collective-permute-start | bytes 737288 | tf_op jit(solution)/shard_map/ppermute | solution.py:36
  43.2 9.4 %collective-permute-start.7 = (bf16[4,30,8,128]{3,2,1,0:T(8,128)(2,1)S(1)}, bf16[4,30,8,128]{3,2,1,0:T(8,128)(2,1)S(1)}, u32[]{:S(2)}, u32[]{:S(2)}) collective-permute-start(bf16[4,30,8,128]{3,2,1,0:T(8,128)(2,1)S(1)} %collective-permute-done.5.refs_3_), channel_id=1, source_target_pairs={{0,2},{1,3},{2,4},{3,5},{4,6},{5,7},{6,8},{7,9},{8,10},{9,11},{10,... | collective-permute-start | bytes 737288 | tf_op jit(solution)/shard_map/ppermute | solution.py:36
  43.3 47.4 %collective-permute-start.31 = (bf16[160,512]{1,0:T(8,128)(2,1)}, bf16[160,512]{1,0:T(8,128)(2,1)}, u32[]{:S(2)}, u32[]{:S(2)}) collective-permute-start(bf16[160,512]{1,0:T(8,128)(2,1)} %bitcast.1), channel_id=1, source_target_pairs={{0,64},{64,128},{128,192},{192,0},{1,65},{65,129},{129,193},{193,1... | collective-permute-start | bytes 491528 | tf_op jit(solution)/shard_map/ppermute | solution.py:44
  44.2 8.6 %collective-permute-start.15 = (bf16[4,30,8,128]{3,2,1,0:T(8,128)(2,1)S(1)}, bf16[4,30,8,128]{3,2,1,0:T(8,128)(2,1)S(1)}, u32[]{:S(2)}, u32[]{:S(2)}) collective-permute-start(bf16[4,30,8,128]{3,2,1,0:T(8,128)(2,1)S(1)} %collective-permute-done.6.refs_4_), channel_id=1, source_target_pairs={{0,1},{1,0},{2,3},{3,2},{4,5},{5,4},{6,7},{7,6},{8,9},{9,8},{10,11... | collective-permute-start | bytes 737288 | tf_op jit(solution)/shard_map/ppermute | solution.py:40
  52.6 7.1 %collective-permute-start.9 = (bf16[2,30,8,128]{3,2,1,0:T(8,128)(2,1)S(1)}, bf16[2,30,8,128]{3,2,1,0:T(8,128)(2,1)S(1)}, u32[]{:S(2)}, u32[]{:S(2)}) collective-permute-start(bf16[2,30,8,128]{3,2,1,0:T(8,128)(2,1)S(1)} %slice.137), channel_id=1, source_target_pairs={{0,2},{1,3},{2,4},{3,5},{4,6},{5,7},{6,8},{7,9},{8,10},{9,11},{10,... | collective-permute-start | bytes 368648 | tf_op jit(solution)/shard_map/ppermute | solution.py:36
  52.8 6.3 %collective-permute-start.10 = (bf16[2,30,8,128]{3,2,1,0:T(8,128)(2,1)S(1)}, bf16[2,30,8,128]{3,2,1,0:T(8,128)(2,1)S(1)}, u32[]{:S(2)}, u32[]{:S(2)}) collective-permute-start(bf16[2,30,8,128]{3,2,1,0:T(8,128)(2,1)S(1)} %slice.139), channel_id=1, source_target_pairs={{0,14},{1,15},{2,0},{3,1},{4,2},{5,3},{6,4},{7,5},{8,6},{9,7},{10,... | collective-permute-start | bytes 368648 | tf_op jit(solution)/shard_map/ppermute | solution.py:36
  56.5 5.7 %collective-permute-start.17 = (bf16[4,30,8,128]{3,2,1,0:T(8,128)(2,1)S(1)}, bf16[4,30,8,128]{3,2,1,0:T(8,128)(2,1)S(1)}, u32[]{:S(2)}, u32[]{:S(2)}) collective-permute-start(bf16[4,30,8,128]{3,2,1,0:T(8,128)(2,1)S(1)} %collective-permute-done.8.refs_6_), channel_id=1, source_target_pairs={{0,1},{1,0},{2,3},{3,2},{4,5},{5,4},{6,7},{7,6},{8,9},{9,8},{10,11... | collective-permute-start | bytes 737288 | tf_op jit(solution)/shard_map/ppermute | solution.py:40
  63.7 24.0 %collective-permute-start.20 = (f32[2,512]{1,0:T(2,128)S(1)}, f32[2,512]{1,0:T(2,128)S(1)}, u32[]{:S(2)}, u32[]{:S(2)}) collective-permute-start(f32[2,512]{1,0:T(2,128)S(1)} %add.294), channel_id=1, source_target_pairs={{0,64},{64,128},{128,192},{192,0},{1,65},{65,129},{129,193},{193,1... | collective-permute-start | bytes 12296 | tf_op jit(solution)/shard_map/ppermute | solution.py:44
  65.7 23.3 %collective-permute-start.21 = (f32[2,512]{1,0:T(2,128)S(1)}, f32[2,512]{1,0:T(2,128)S(1)}, u32[]{:S(2)}, u32[]{:S(2)}) collective-permute-start(f32[2,512]{1,0:T(2,128)S(1)} %add.294), channel_id=1, source_target_pairs={{0,128},{64,192},{128,0},{192,64},{1,129},{65,193},{129,1},{193,65... | collective-permute-start | bytes 12296 | tf_op jit(solution)/shard_map/ppermute | solution.py:44
  67.5 21.5 %collective-permute-start.22 = (f32[2,512]{1,0:T(2,128)S(1)}, f32[2,512]{1,0:T(2,128)S(1)}, u32[]{:S(2)}, u32[]{:S(2)}) collective-permute-start(f32[2,512]{1,0:T(2,128)S(1)} %add.294), channel_id=1, source_target_pairs={{0,192},{64,0},{128,64},{192,128},{1,193},{65,1},{129,65},{193,129... | collective-permute-start | bytes 12296 | tf_op jit(solution)/shard_map/ppermute | solution.py:44
  87.8 7.6 %collective-permute-start.32 = (bf16[160,512]{1,0:T(8,128)(2,1)}, bf16[160,512]{1,0:T(8,128)(2,1)S(1)}, u32[]{:S(2)}, u32[]{:S(2)}) collective-permute-start(bf16[160,512]{1,0:T(8,128)(2,1)} %bitcast.1), channel_id=1, source_target_pairs={{0,128},{64,192},{128,0},{192,64},{1,129},{65,193},{129,1},{193,65... | collective-permute-start | bytes 491528 | tf_op jit(solution)/shard_map/ppermute | solution.py:44
  121.5 7.2 %collective-permute-start.34 = (f32[8,128]{1,0:T(8,128)}, f32[8,128]{1,0:T(8,128)S(1)}, u32[]{:S(2)}, u32[]{:S(2)}) collective-permute-start(f32[8,128]{1,0:T(8,128)} %reduce_sum.356), channel_id=1, source_target_pairs={{0,64},{64,128},{128,192},{192,0},{1,65},{65,129},{129,193},{193,1... | collective-permute-start | bytes 12296 | tf_op jit(solution)/shard_map/ppermute | solution.py:44
  121.8 8.0 %collective-permute-start.35 = (f32[8,128]{1,0:T(8,128)}, f32[8,128]{1,0:T(8,128)S(1)}, u32[]{:S(2)}, u32[]{:S(2)}) collective-permute-start(f32[8,128]{1,0:T(8,128)} %reduce_sum.356), channel_id=1, source_target_pairs={{0,128},{64,192},{128,0},{192,64},{1,129},{65,193},{129,1},{193,65... | collective-permute-start | bytes 12296 | tf_op jit(solution)/shard_map/ppermute | solution.py:44
  124.9 12.2 %collective-permute-start.29 = (f32[160,512]{1,0:T(8,128)S(1)}, f32[160,512]{1,0:T(8,128)S(1)}, u32[]{:S(2)}, u32[]{:S(2)}) collective-permute-start(f32[160,512]{1,0:T(8,128)S(1)} %get-tuple-element.28), channel_id=1, source_target_pairs={{0,128},{64,192},{128,0},{192,64},{1,129},{65,193},{129,1},{193,65... | collective-permute-start | bytes 983048 | tf_op jit(solution)/shard_map/ppermute | solution.py:44
  127.7 13.1 %collective-permute-start.30 = (f32[160,512]{1,0:T(8,128)S(1)}, f32[160,512]{1,0:T(8,128)S(1)}, u32[]{:S(2)}, u32[]{:S(2)}) collective-permute-start(f32[160,512]{1,0:T(8,128)S(1)} %get-tuple-element.30), channel_id=1, source_target_pairs={{0,192},{64,0},{128,64},{192,128},{1,193},{65,1},{129,65},{193,129... | collective-permute-start | bytes 983048 | tf_op jit(solution)/shard_map/ppermute | solution.py:44
  128.8 13.8 %collective-permute-start.28 = (f32[160,512]{1,0:T(8,128)S(1)}, f32[160,512]{1,0:T(8,128)S(1)}, u32[]{:S(2)}, u32[]{:S(2)}) collective-permute-start(f32[160,512]{1,0:T(8,128)S(1)} %get-tuple-element.26), channel_id=1, source_target_pairs={{0,64},{64,128},{128,192},{192,0},{1,65},{65,129},{129,193},{193,1... | collective-permute-start | bytes 983048 | tf_op jit(solution)/shard_map/ppermute | solution.py:44
  (31 other events, 69.5 us)

commit v2 on v1

v2 whole, which is shorter than its diff:
```python
import functools

import jax
import jax.numpy as jnp
from jax import lax
from jax.experimental import pallas as pl
from jax.experimental.pallas import tpu as pltpu
from jax.sharding import Mesh
from jax.sharding import PartitionSpec as P

GROUPS = 32
XS, YS, ZS, CS = 4, 4, 8, 2
ROWS = YS * ZS * CS
FRAMES = XS
SIZES = {"x": XS, "y": YS, "z": ZS, "c": CS}
ROW_AXES = ("y", "z", "c")
TAPS = 9
PLANES = 3 * TAPS
UNITS = ((0, 1, 2, 3), (0, 1, 2), (0, 1))
VMEM = pl.BlockSpec(memory_space=pltpu.VMEM)


def send(value, axis, step):
    size = SIZES[axis]
    return lax.ppermute(value, axis, [(i, (i + step) % size) for i in range(size)])


def pool_kernel(msg0, msg1, msg2, msg3, low, high, out2, out1, out0, sums, pooled):
    cells = out2.shape[1] // FRAMES
    fine = 2 * cells
    place = lax.axis_index("x")
    zero = jnp.zeros((8, 128), jnp.float32)
    for band in range(3):
        sums[band, 0:8] = zero
        sums[band, 8 + fine : 16 + fine] = zero
    for k, msg in enumerate((msg0, msg1, msg2, msg3)):
        frame = lax.rem(place + FRAMES - k, FRAMES)
        upper = msg[0:fine].astype(jnp.float32)
        lower = msg[fine : 2 * fine].astype(jnp.float32)
        sums[0, 8 : 8 + fine] = lower + high[k].astype(jnp.float32)
        sums[1, 8 : 8 + fine] = upper + lower
        sums[2, 8 : 8 + fine] = low[k].astype(jnp.float32) + upper
        for band in range(3):
            at = sums.at[band]
            before = at[pl.ds(7, cells, stride=2), :]
            even = at[pl.ds(8, cells, stride=2), :]
            odd = at[pl.ds(9, cells, stride=2), :]
            after = at[pl.ds(10, cells, stride=2), :]
            pooled[frame, band * 3 + 0] = odd + after
            pooled[frame, band * 3 + 1] = even + odd
            pooled[frame, band * 3 + 2] = before + even
    for tap in range(TAPS):
        lanes = slice(tap * 128, tap * 128 + 128)

        def put(out, unit, value):
            head = value.astype(jnp.bfloat16)
            tail = (value - head.astype(jnp.float32)).astype(jnp.bfloat16)
            out[0, unit * cells : (unit + 1) * cells, lanes] = head
            out[1, unit * cells : (unit + 1) * cells, lanes] = tail

        p0, p1, p2, p3 = (pooled[t, tap] for t in range(FRAMES))
        put(out2, 0, p0)
        put(out2, 1, p1)
        put(out2, 2, p2)
        put(out2, 3, p3)
        p01 = p0 + p1
        put(out1, 0, p01)
        put(out1, 1, p2)
        put(out1, 2, p3)
        put(out0, 0, p01 + p2)
        put(out0, 1, p3)


def pool(msgs, low, high):
    cells = low.shape[1] // 2
    shapes = [
        jax.ShapeDtypeStruct((2, len(units) * cells, TAPS * 128), jnp.bfloat16) for units in UNITS
    ]
    return pl.pallas_call(
        pool_kernel,
        out_shape=shapes,
        in_specs=[VMEM] * 6,
        out_specs=[VMEM] * 3,
        scratch_shapes=[
            pltpu.VMEM((3, 2 * cells + 16, 128), jnp.float32),
            pltpu.VMEM((FRAMES, TAPS, cells, 128), jnp.float32),
        ],
        compiler_params=pltpu.CompilerParams(vmem_limit_bytes=12 << 20),
        cost_estimate=pl.CostEstimate(flops=20_000_000, bytes_accessed=9_000_000, transcendentals=0),
    )(*msgs, low, high)


def product_kernel(*refs):
    pieces = refs[: CS * YS]
    left2, left1, left0 = refs[CS * YS : CS * YS + 3]
    outs = refs[CS * YS + 3 : CS * YS + 7]
    weights, acc, sems = refs[CS * YS + 7 :]
    y, c = lax.axis_index("y"), lax.axis_index("c")
    cells = outs[0].shape[0]
    copies = []
    for side in range(CS):
        core = c if side == 0 else 1 - c
        for step in range(YS):
            piece = pieces[side * YS + step]
            source_y = lax.rem(y + YS - step, YS)
            for z in range(ZS):
                row = pl.multiple_of(source_y * (ZS * CS * 8) + z * (CS * 8) + core * 8, 8)
                copies.append(
                    pltpu.make_async_copy(
                        piece.at[z, 0:PLANES],
                        weights.at[:, pl.ds(row, 8), :],
                        sems.at[len(copies)],
                    )
                )
    for copy in copies:
        copy.start()
    for copy in copies:
        copy.wait()
    for n in range(acc.shape[1] // 256):
        cols = slice(n * 256, n * 256 + 256)
        for tap, left in ((2, left2), (1, left1), (0, left0)):
            right = jnp.concatenate(
                [weights[tap * TAPS + t, cols, :] for t in range(TAPS)], axis=1
            )
            total = None
            for half in range(2):
                part = lax.dot_general(
                    left[half], right, (((1,), (1,)), ((), ())), preferred_element_type=jnp.float32
                )
                total = part if total is None else total + part
            if tap == 2:
                acc[:, cols] = total
            else:
                acc[0 : total.shape[0], cols] += total
    place = lax.axis_index("x")
    for k, out in enumerate(outs):
        frame = lax.rem(place + FRAMES - k, FRAMES)
        out[...] = acc[pl.ds(pl.multiple_of(frame * cells, 8), cells), :]


def product(pieces, lefts, channels):
    cells = lefts[0].shape[1] // FRAMES
    return pl.pallas_call(
        product_kernel,
        out_shape=[jax.ShapeDtypeStruct((cells, channels), jnp.float32)] * FRAMES,
        in_specs=[pl.BlockSpec(memory_space=pl.ANY)] * len(pieces) + [VMEM] * 3,
        out_specs=[VMEM] * FRAMES,
        scratch_shapes=[
            pltpu.VMEM((PLANES, channels, 128), jnp.bfloat16),
            pltpu.VMEM((FRAMES * cells, channels), jnp.float32),
            pltpu.SemaphoreType.DMA((CS * YS * ZS,)),
        ],
        compiler_params=pltpu.CompilerParams(vmem_limit_bytes=14 << 20),
        cost_estimate=pl.CostEstimate(
            flops=3_400_000_000, bytes_accessed=11_000_000, transcendentals=0
        ),
    )(*pieces, *lefts)


def sums_kernel(part0, part1, part2, part3, msg0, msg1, msg2, msg3, chan, out):
    cells, channels = part0.shape
    offset = msg0.shape[0] - 4 * cells
    for q in range(channels // 128):
        lanes = slice(q * 128, q * 128 + 128)
        mean, inv, gain, bias = (chan[r : r + 1, lanes] for r in range(4))
        first = jnp.zeros((8, 128), jnp.float32)
        second = jnp.zeros((8, 128), jnp.float32)
        for part, msg in ((part0, msg0), (part1, msg1), (part2, msg2), (part3, msg3)):
            start = offset + q * cells
            features = msg[start : start + cells].astype(jnp.float32)
            normed = (features - mean) * inv
            pre = normed * gain + bias
            sigmoid_pre = 1.0 / (1.0 + jnp.exp(-pre))
            act = part[:, lanes] * (sigmoid_pre * (1.0 + pre * (1.0 - sigmoid_pre)))
            first = first + act.reshape(cells // 8, 8, 128).sum(axis=0)
            second = second + (act * normed).reshape(cells // 8, 8, 128).sum(axis=0)
        out[q : q + 1] = jnp.sum(first, axis=0, keepdims=True)
        out[4 + q : 5 + q] = jnp.sum(second, axis=0, keepdims=True)


def partial_sums(parts, msgs, chan):
    return pl.pallas_call(
        sums_kernel,
        out_shape=jax.ShapeDtypeStruct((8, 128), jnp.float32),
        in_specs=[VMEM] * 9,
        out_specs=VMEM,
        compiler_params=pltpu.CompilerParams(vmem_limit_bytes=6 << 20),
        cost_estimate=pl.CostEstimate(
            flops=6_000_000, bytes_accessed=2_600_000, transcendentals=330_000
        ),
    )(*parts, *msgs, chan)


def three_parts(value):
    head = lax.reduce_precision(value, 8, 7)
    rest = value - head
    middle = lax.reduce_precision(rest, 8, 7)
    return [part.astype(jnp.bfloat16) for part in (head, middle, rest - middle)]


def on_device(latent, norm_gain, norm_bias, conv_weight, cotangent):
    place = lax.axis_index("x")
    cells, channels = latent.shape[2], latent.shape[3]
    fine_cols = cotangent.shape[2]
    per_group = channels // GROUPS
    cell_count = FRAMES * ROWS * cells

    split = cotangent[0].reshape(2 * fine_cols, FRAMES, 128).transpose(1, 0, 2)
    shared = latent[0, 0].reshape(cells, 4, 128).transpose(1, 0, 2).reshape(4 * cells, 128)
    msgs = []
    for step in range(FRAMES):
        chunk = lax.dynamic_index_in_dim(split, lax.rem(place + step, FRAMES), 0, keepdims=False)
        msgs.append(jnp.concatenate([chunk, shared], axis=0))
    msgs = [msg if step == 0 else send(msg, "x", step) for step, msg in enumerate(msgs)]

    own = latent[0, 0].astype(jnp.float32)
    stats = jnp.stack([jnp.sum(own, axis=0), jnp.sum(own * own, axis=0)])
    parts = jnp.stack([part.reshape(8, 128) for part in three_parts(stats)])
    message = jnp.concatenate([conv_weight.reshape(PLANES, 8, 128), parts], axis=0)
    block = lax.all_to_all(
        jnp.broadcast_to(message[None], (ZS,) + message.shape), "z", 0, 0, tiled=True
    )
    pieces = [block] + [send(block, "y", step) for step in range(1, YS)]
    pieces = pieces + [send(piece, "c", 1) for piece in pieces]

    low = lax.ppermute(
        jnp.stack([msg[fine_cols : 2 * fine_cols] for msg in msgs]),
        ROW_AXES,
        [(i, i + 1) for i in range(ROWS - 1)],
    )
    high = lax.ppermute(
        jnp.stack([msg[:fine_cols] for msg in msgs]),
        ROW_AXES,
        [(i + 1, i) for i in range(ROWS - 1)],
    )
    lefts = pool(msgs, low, high)
    partial = product(pieces, lefts, channels)

    gathered = sum(
        jnp.sum(piece[:, PLANES:].astype(jnp.float32), axis=(0, 1)) for piece in pieces
    )
    total = gathered + sum(send(gathered, "x", step) for step in range(1, FRAMES))
    group = total.reshape(2, GROUPS, per_group).sum(axis=2) / (cell_count * per_group)
    group_mean = group[0]
    group_var = group[1] - group_mean * group_mean
    inv_std = lax.rsqrt(group_var + 1e-06)
    mean_chan = jnp.repeat(group_mean, per_group)
    inv_chan = jnp.repeat(inv_std, per_group)

    chan = jnp.stack([mean_chan, inv_chan, norm_gain, norm_bias])
    sums = partial_sums(partial, msgs, chan)
    sums = sums + sum(send(sums, "x", step) for step in range(1, FRAMES))
    up_grad = partial[0] + sum(
        send(partial[FRAMES - step], "x", step) for step in range(1, FRAMES)
    )
    sums = lax.all_to_all(
        jnp.broadcast_to(sums[None], (ROWS, 8, 128)), ROW_AXES, 0, 0, tiled=True
    ).sum(axis=0)
    sum_act, sum_scaled = sums.reshape(2, channels)

    gain_grad = sum_scaled / cell_count
    bias_grad = sum_act / cell_count
    scale = cell_count * per_group
    mean_q = (norm_gain * sum_act).reshape(GROUPS, per_group).sum(axis=1) / scale
    mean_qn = (norm_gain * sum_scaled).reshape(GROUPS, per_group).sum(axis=1) / scale
    normed = (own - mean_chan) * inv_chan
    pre = normed * norm_gain + norm_bias
    sigmoid_pre = jax.nn.sigmoid(pre)
    act_grad = up_grad * sigmoid_pre * (1.0 + pre * (1.0 - sigmoid_pre))
    latent_grad = inv_chan * (
        act_grad * norm_gain
        - jnp.repeat(mean_q, per_group)
        - normed * jnp.repeat(mean_qn, per_group)
    )
    return (latent_grad.reshape(1, 1, cells, channels), gain_grad, bias_grad)


def solution(mesh):
    fine = Mesh(mesh.devices.reshape(XS, YS, ZS, CS), ("x", "y", "z", "c"))
    image = P("x", ROW_AXES, None, None)
    return jax.shard_map(
        on_device,
        mesh=fine,
        in_specs=(image, P(), P(), P(None, None, None, ROW_AXES, "x"), image),
        out_specs=(image, P(), P()),
        check_vma=False,
    )
```

time: 147 us -> 116 us (0.79); the launches traced: 144 us -> 116 us
  blocking collectives: 22.8 us -> 0 us
  waiting for transfers between devices: 29.6 us -> 51.9 us
  local copies, waits for them, and re-layouts: 26.8 us -> 6.72 us
  other arithmetic: 10.3 us -> 3.32 us
  starting transfers between devices: 46.7 us -> 44.6 us
    all_to_all x1 -> x0, blocking collectives: 22.8 us -> none  [on_device(): lax.all_to_all(jnp.broadcast_to(sums, (ROWS, 8, 128)), 'rows', 0, 0, tile...]
    unnamed x56 -> x10, local copies, waits for them, and re-layouts: 22.8 us -> 0.07 us
    ppermute x37 -> x21, starting transfers between devices: 46.7 us -> 28.5 us  [the longest x19 23.2 us: send(): lax.ppermute(value, axis, [(i, (i + step) % size) for i in range(size)])]
    all_to_all x0 -> x2, starting transfers between devices: none -> 16.1 us  [the longest x1 8.57 us: on_device(): lax.all_to_all(jnp.broadcast_to(message[None], (ZS,) + message.shape), 'z...]
    ppermute x37 -> x21, waiting for transfers between devices: 29.6 us -> 45.2 us  [the longest x19 41.7 us: send(): lax.ppermute(value, axis, [(i, (i + step) % size) for i in range(size)])]
    all_to_all x0 -> x2, waiting for transfers between devices: none -> 6.61 us  [the longest x1 6.61 us: on_device(): lax.all_to_all(jnp.broadcast_to(sums[None], (ROWS, 8, 128)), ROW_AXES, 0,...]
    reduce_sum x21 -> x9, other arithmetic: 3.62 us -> 0.29 us  [the longest x8 0.22 us: on_device(): jnp.sum(piece[:, PLANES:].astype(jnp.float32), axis=(0, 1))]
    broadcast_in_dim x2, local copies, waits for them, and re-layouts: 0.03 us -> 1.56 us  [the longest x1 0.83 us: on_device(): jnp.broadcast_to(message[None], (ZS,) + message.shape)]
  transfers between devices with their start and end apart: 37 -> 23, of which waited for: 9 -> 12; matrix products, arithmetic and copies ran while one was open for 5% -> 2% of each run, Pallas kernels for 5% -> 6%
where the time goes in v2:
time: 116 us
  waiting for transfers between devices  51.9 us (45%)
  starting transfers between devices  44.6 us (38%)
  Pallas kernels  8.19 us (7%)
  local copies, waits for them, and re-layouts  6.72 us (6%)
  other arithmetic  3.32 us (3%)
    ppermute x19, waiting for transfers between devices, send(): lax.ppermute(value, axis, [(i, (i + step) % size) for i in range(size)])  41.7 us
    ppermute x19, starting transfers between devices, send(): lax.ppermute(value, axis, [(i, (i + step) % size) for i in range(size)])  23.2 us
    all_to_all x1, starting transfers between devices, on_device(): lax.all_to_all(jnp.broadcast_to(message[None], (ZS,) + message.shape), 'z...  8.57 us
    all_to_all x1, starting transfers between devices, on_device(): lax.all_to_all(jnp.broadcast_to(sums[None], (ROWS, 8, 128)), ROW_AXES, 0,...  7.53 us
    all_to_all x1, waiting for transfers between devices, on_device(): lax.all_to_all(jnp.broadcast_to(sums[None], (ROWS, 8, 128)), ROW_AXES, 0,...  6.61 us
    pallas_call x1, Pallas kernels, product(): pl.pallas_call(product_kernel, out_shape=[jax.ShapeDtypeStruct((cells, ch...  5.93 us
    ppermute x1, starting transfers between devices, on_device(): lax.ppermute(jnp.stack([msg[:fine_cols] for msg in msgs]), ROW_AXES, [(i...  3.36 us
  transfers between devices with their start and end apart: 23, of which 12 were waited for; matrix products, arithmetic and copies ran while one was open for 2% of the time, Pallas kernels for 6%

profile of v2, /device:TPU:32, one launch (start us, length us, event | category | flops | bytes accessed | tf_op | source)
XLA Modules:
  0.0 115.7 jit_solution(6529667975422249026)
XLA Ops:
  0.7 1.0 reshape_squeeze.7
  1.6 1.6 %reshape_squeeze.6 = bf16[640,4,128]{2,1,0:T(4,128)(2,1)S(1)} reshape(bf16[1,2,320,512]{3,2,1,0:T(8,128)(2,1)} %param.9) | data formatting | bytes 1310720 | tf_op jit(solution)/shard_map/reshape;squeeze | solution.py:208
  3.3 1.4 %constant_dynamic-slice_fusion = (bf16[640,1,128]{2,1,0:T(2,128)(2,1)S(1)}, bf16[640,1,128]{2,1,0:T(2,128)(2,1)S(1)}, bf16[640,1,128]{2,1,0:T(2,128)(2,1)S(1)}, bf16[640,1,128]{2,1,0:T(2,128)(2,1)S(1)}) fusion(bf16[640,4,128]{2,1,0:T(4,128)(2,1)S(1)} %reshape_squeeze.6, s32[]{:T(128)S(6)} %select_n.16, s32[]{:T(128)S(6)} %select_n.15, s32[]{:T(128)S(6)} %select_n.14, ...), kind=kLoop, calls=%fused_computation.61 | loop fusion | bytes 1310736 | tf_op jit(solution)/shard_map/dynamic-slice.3
  4.8 0.9 pad_maximum_fusion
  5.7 2.8 %collective-permute-start.12 = (bf16[1280,128]{1,0:T(8,128)(2,1)}, bf16[1280,128]{1,0:T(8,128)(2,1)S(1)}, u32[]{:S(2)}, u32[]{:S(2)}) collective-permute-start(bf16[1280,128]{1,0:T(8,128)(2,1)} %get-tuple-element.31), channel_id=1, source_target_pairs={{0,192},{64,0},{128,64},{192,128},{1,193},{65,1},{129,65},{193,129... | collective-permute-start | bytes 983048 | tf_op jit(solution)/shard_map/ppermute | solution.py:25
  8.6 0.8 broadcast_in_dim.31
  9.4 8.6 %all-to-all-start = ((bf16[8,30,8,128]{3,2,1,0:T(8,128)(2,1)}), bf16[8,30,8,128]{3,2,1,0:T(8,128)(2,1)S(1)}, u32[]{:S(2)}, u32[]{:S(2)}) async-start(bf16[8,30,8,128]{3,2,1,0:T(8,128)(2,1)} %broadcast_in_dim.31), calls=%async_computation | async-start | bytes 983040 | tf_op jit(solution)/shard_map/all_to_all | solution.py:220
  18.0 2.3 %collective-permute-start.11 = (bf16[1280,128]{1,0:T(8,128)(2,1)S(1)}, bf16[1280,128]{1,0:T(8,128)(2,1)S(1)}, u32[]{:S(2)}, u32[]{:S(2)}) collective-permute-start(bf16[1280,128]{1,0:T(8,128)(2,1)S(1)} %get-tuple-element.33), channel_id=1, source_target_pairs={{0,128},{64,192},{128,0},{192,64},{1,129},{65,193},{129,1},{193,65... | collective-permute-start | bytes 983048 | tf_op jit(solution)/shard_map/ppermute | solution.py:25
  20.4 13.7 %collective-permute-done.11.msg2 = bf16[1280,128]{1,0:T(8,128)(2,1)S(1)} collective-permute-done((bf16[1280,128]{1,0:T(8,128)(2,1)S(1)}, bf16[1280,128]{1,0:T(8,128)(2,1)S(1)}, u32[]{:S(2)}, u32[]{:S(2)}) %collective-permute-start.11) | collective-permute-done | bytes 327712 | tf_op jit(solution)/shard_map/ppermute | solution.py:25
  34.0 0.8 collective-permute-done.10.msg1
  34.9 3.1 %collective-permute-start.2 = (bf16[8,30,8,128]{3,2,1,0:T(8,128)(2,1)S(1)}, bf16[8,30,8,128]{3,2,1,0:T(8,128)(2,1)S(1)}, u32[]{:S(2)}, u32[]{:S(2)}) collective-permute-start(bf16[8,30,8,128]{3,2,1,0:T(8,128)(2,1)S(1)} %all-to-all-done.refs_0_), channel_id=1, source_target_pairs={{0,48},{16,0},{32,16},{48,32},{1,49},{17,1},{33,17},{49,33},{2,50}... | collective-permute-start | bytes 1474568 | tf_op jit(solution)/shard_map/ppermute | solution.py:25
  38.0 1.9 %collective-permute-start.13 = (bf16[4,320,128]{2,1,0:T(8,128)(2,1)S(1)}, bf16[4,320,128]{2,1,0:T(8,128)(2,1)S(1)}, u32[]{:S(2)}, u32[]{:S(2)}) collective-permute-start(bf16[4,320,128]{2,1,0:T(8,128)(2,1)S(1)} %pad_maximum_fusion.4), channel_id=1, source_target_pairs={{0,1},{1,2},{2,3},{3,4},{4,5},{5,6},{6,7},{7,8},{8,9},{9,10},{10,1... | collective-permute-start | bytes 983048 | tf_op jit(solution)/shard_map/ppermute | solution.py:226
  40.7 3.4 %collective-permute-start.14 = (bf16[4,320,128]{2,1,0:T(8,128)(2,1)S(1)}, bf16[4,320,128]{2,1,0:T(8,128)(2,1)S(1)}, u32[]{:S(2)}, u32[]{:S(2)}) collective-permute-start(bf16[4,320,128]{2,1,0:T(8,128)(2,1)S(1)} %pad_maximum_fusion.5), channel_id=1, source_target_pairs={{1,0},{2,1},{3,2},{4,3},{5,4},{6,5},{7,6},{8,7},{9,8},{10,9},{11,1... | collective-permute-start | bytes 983048 | tf_op jit(solution)/shard_map/ppermute | solution.py:231
  44.1 1.0 collective-permute-start
  45.1 1.3 %collective-permute-done.13.low = bf16[4,320,128]{2,1,0:T(8,128)(2,1)S(1)} collective-permute-done((bf16[4,320,128]{2,1,0:T(8,128)(2,1)S(1)}, bf16[4,320,128]{2,1,0:T(8,128)(2,1)S(1)}, u32[]{:S(2)}, u32[]{:S(2)}) %collective-permute-start.13) | collective-permute-done | bytes 327712 | tf_op jit(solution)/shard_map/ppermute | solution.py:226
  46.4 2.2 %collective-permute-done.14.high = bf16[4,320,128]{2,1,0:T(8,128)(2,1)S(1)} collective-permute-done((bf16[4,320,128]{2,1,0:T(8,128)(2,1)S(1)}, bf16[4,320,128]{2,1,0:T(8,128)(2,1)S(1)}, u32[]{:S(2)}, u32[]{:S(2)}) %collective-permute-start.14) | collective-permute-done | bytes 327712 | tf_op jit(solution)/shard_map/ppermute | solution.py:231
  48.7 1.5 %shard_map.76 = (bf16[2,640,1152]{2,1,0:T(8,128)(2,1)S(1)}, bf16[2,480,1152]{2,1,0:T(8,128)(2,1)S(1)}, bf16[2,320,1152]{2,1,0:T(8,128)(2,1)S(1)}) custom-call(bf16[1280,128]{1,0:T(8,128)(2,1)S(1)} %get-tuple-element.34.msg0, bf16[1280,128]{1,0:T(8,128)(2,1)S(1)} %collective-permute-done.10.msg1, bf16[1280,128]{1,0:T(8,128)(2,1)S(1)} %collective-permute-done.11.msg2, ...), custom_call_target="tpu_custom_call" | custom-call | flops 20000000 | bytes 9000000 | tf_op jit(solution)/shard_map/pallas_call | solution.py:79
  50.1 6.2 %collective-permute-done.2.refs_3_ = bf16[8,30,8,128]{3,2,1,0:T(8,128)(2,1)S(1)} collective-permute-done((bf16[8,30,8,128]{3,2,1,0:T(8,128)(2,1)S(1)}, bf16[8,30,8,128]{3,2,1,0:T(8,128)(2,1)S(1)}, u32[]{:S(2)}, u32[]{:S(2)}) %collective-permute-start.2) | collective-permute-done | bytes 491552 | tf_op jit(solution)/shard_map/ppermute | solution.py:25
  57.0 9.2 %collective-permute-done.refs_1_ = bf16[8,30,8,128]{3,2,1,0:T(8,128)(2,1)S(1)} collective-permute-done((bf16[8,30,8,128]{3,2,1,0:T(8,128)(2,1)S(1)}, bf16[8,30,8,128]{3,2,1,0:T(8,128)(2,1)S(1)}, u32[]{:S(2)}, u32[]{:S(2)}) %collective-permute-start) | collective-permute-done | bytes 491552 | tf_op jit(solution)/shard_map/ppermute | solution.py:25
  66.4 1.7 %collective-permute-done.4.refs_5_ = bf16[8,30,8,128]{3,2,1,0:T(8,128)(2,1)S(1)} collective-permute-done((bf16[8,30,8,128]{3,2,1,0:T(8,128)(2,1)S(1)}, bf16[8,30,8,128]{3,2,1,0:T(8,128)(2,1)S(1)}, u32[]{:S(2)}, u32[]{:S(2)}) %collective-permute-start.4) | collective-permute-done | bytes 491552 | tf_op jit(solution)/shard_map/ppermute | solution.py:25
  68.2 2.0 %collective-permute-start.7 = (f32[8,128]{1,0:T(8,128)S(1)}, f32[8,128]{1,0:T(8,128)S(1)}, u32[]{:S(2)}, u32[]{:S(2)}) collective-permute-start(f32[8,128]{1,0:T(8,128)S(1)} %add_add_fusion.2), channel_id=1, source_target_pairs={{0,64},{64,128},{128,192},{192,0},{1,65},{65,129},{129,193},{193,1... | collective-permute-start | bytes 12296 | tf_op jit(solution)/shard_map/ppermute | solution.py:25
  70.8 5.9 %shard_map.77 = (f32[160,512]{1,0:T(8,128)S(1)}, f32[160,512]{1,0:T(8,128)S(1)}, f32[160,512]{1,0:T(8,128)S(1)}, f32[160,512]{1,0:T(8,128)S(1)}) custom-call(bf16[8,30,8,128]{3,2,1,0:T(8,128)(2,1)S(1)} %all-to-all-done.refs_0_, bf16[8,30,8,128]{3,2,1,0:T(8,128)(2,1)S(1)} %collective-permute-done.refs_1_, ...), custom_call_target="tpu_custom_call" | custom-call | flops 3400000000 | bytes 11000000 | tf_op jit(solution)/shard_map/pallas_call | solution.py:143
  78.1 2.1 %collective-permute-start.20 = (f32[8,128]{1,0:T(8,128)S(1)}, f32[8,128]{1,0:T(8,128)S(1)}, u32[]{:S(2)}, u32[]{:S(2)}) collective-permute-start(f32[8,128]{1,0:T(8,128)S(1)} %shard_map.78), channel_id=1, source_target_pairs={{0,192},{64,0},{128,64},{192,128},{1,193},{65,1},{129,65},{193,129... | collective-permute-start | bytes 12296 | tf_op jit(solution)/shard_map/ppermute | solution.py:25
  80.3 2.9 %collective-permute-start.19 = (f32[8,128]{1,0:T(8,128)S(1)}, f32[8,128]{1,0:T(8,128)S(1)}, u32[]{:S(2)}, u32[]{:S(2)}) collective-permute-start(f32[8,128]{1,0:T(8,128)S(1)} %shard_map.78), channel_id=1, source_target_pairs={{0,128},{64,192},{128,0},{192,64},{1,129},{65,193},{129,1},{193,65... | collective-permute-start | bytes 12296 | tf_op jit(solution)/shard_map/ppermute | solution.py:25
  83.2 1.9 %collective-permute-done.18 = f32[8,128]{1,0:T(8,128)S(1)} collective-permute-done((f32[8,128]{1,0:T(8,128)S(1)}, f32[8,128]{1,0:T(8,128)S(1)}, u32[]{:S(2)}, u32[]{:S(2)}) %collective-permute-start.18) | collective-permute-done | bytes 4128 | tf_op jit(solution)/shard_map/ppermute | solution.py:25
  86.1 7.5 %all-to-all-start.1 = ((f32[64,8,128]{2,1,0:T(8,128)}), f32[64,8,128]{2,1,0:T(8,128)S(1)}, u32[]{:S(2)}, u32[]{:S(2)}) async-start(f32[64,8,128]{2,1,0:T(8,128)} %broadcast_in_dim.36), calls=%async_computation.1 | async-start | bytes 524288 | tf_op jit(solution)/shard_map/all_to_all | solution.py:256
  93.7 3.3 %collective-permute-start.17 = (f32[160,512]{1,0:T(8,128)S(1)}, f32[160,512]{1,0:T(8,128)S(1)}, u32[]{:S(2)}, u32[]{:S(2)}) collective-permute-start(f32[160,512]{1,0:T(8,128)S(1)} %get-tuple-element.16.part1), channel_id=1, source_target_pairs={{0,192},{64,0},{128,64},{192,128},{1,193},{65,1},{129,65},{193,129... | collective-permute-start | bytes 983048 | tf_op jit(solution)/shard_map/ppermute | solution.py:25
  97.0 1.7 %collective-permute-start.16 = (f32[160,512]{1,0:T(8,128)S(1)}, f32[160,512]{1,0:T(8,128)S(1)}, u32[]{:S(2)}, u32[]{:S(2)}) collective-permute-start(f32[160,512]{1,0:T(8,128)S(1)} %get-tuple-element.15.part2), channel_id=1, source_target_pairs={{0,128},{64,192},{128,0},{192,64},{1,129},{65,193},{129,1},{193,65... | collective-permute-start | bytes 983048 | tf_op jit(solution)/shard_map/ppermute | solution.py:25
  98.8 6.6 %all-to-all-done.1 = f32[64,8,128]{2,1,0:T(8,128)S(1)} async-done(((f32[64,8,128]{2,1,0:T(8,128)}), f32[64,8,128]{2,1,0:T(8,128)S(1)}, u32[]{:S(2)}, u32[]{:S(2)}) %all-to-all-start.1) | async-done | bytes 262176 | tf_op jit(solution)/shard_map/all_to_all | solution.py:256
  106.8 4.5 %collective-permute-done.17 = f32[160,512]{1,0:T(8,128)S(1)} collective-permute-done((f32[160,512]{1,0:T(8,128)S(1)}, f32[160,512]{1,0:T(8,128)S(1)}, u32[]{:S(2)}, u32[]{:S(2)}) %collective-permute-start.17) | collective-permute-done | bytes 327712 | tf_op jit(solution)/shard_map/ppermute | solution.py:25
  111.3 3.4 %collective-permute-done.15 = f32[160,512]{1,0:T(8,128)S(1)} collective-permute-done((f32[160,512]{1,0:T(8,128)S(1)}, f32[160,512]{1,0:T(8,128)S(1)}, u32[]{:S(2)}, u32[]{:S(2)}) %collective-permute-start.15) | collective-permute-done | bytes 327712 | tf_op jit(solution)/shard_map/ppermute | solution.py:25
  114.7 1.0 fusion.18
  (83 shorter events, 6.6 us)
Async XLA Ops:
  4.7 3.8 %copy-start = (bf16[1,1,160,512]{3,2,1,0:T(8,128)(2,1)S(1)}, bf16[1,1,160,512]{3,2,1,0:T(8,128)(2,1)}, u32[]{:S(2)}) copy-start(bf16[1,1,160,512]{3,2,1,0:T(8,128)(2,1)} %param.5) | copy-start | bytes 491524
  4.7 3.9 %copy-start.1 = (bf16[3,3,3,8,128]{4,3,2,1,0:T(8,128)(2,1)S(1)}, bf16[3,3,3,8,128]{4,3,2,1,0:T(8,128)(2,1)}, u32[]{:S(2)}) copy-start(bf16[3,3,3,8,128]{4,3,2,1,0:T(8,128)(2,1)} %param.8) | copy-start | bytes 165892
  5.7 14.6 %collective-permute-start.12 = (bf16[1280,128]{1,0:T(8,128)(2,1)}, bf16[1280,128]{1,0:T(8,128)(2,1)S(1)}, u32[]{:S(2)}, u32[]{:S(2)}) collective-permute-start(bf16[1280,128]{1,0:T(8,128)(2,1)} %get-tuple-element.31), channel_id=1, source_target_pairs={{0,192},{64,0},{128,64},{192,128},{1,193},{65,1},{129,65},{193,129... | collective-permute-start | bytes 983048 | tf_op jit(solution)/shard_map/ppermute | solution.py:25
  9.4 25.4 %all-to-all-start = ((bf16[8,30,8,128]{3,2,1,0:T(8,128)(2,1)}), bf16[8,30,8,128]{3,2,1,0:T(8,128)(2,1)S(1)}, u32[]{:S(2)}, u32[]{:S(2)}) async-start(bf16[8,30,8,128]{3,2,1,0:T(8,128)(2,1)} %broadcast_in_dim.31), calls=%async_computation | async-start | bytes 983040 | tf_op jit(solution)/shard_map/all_to_all | solution.py:220
  18.0 16.8 %collective-permute-start.10 = (bf16[1280,128]{1,0:T(8,128)(2,1)S(1)}, bf16[1280,128]{1,0:T(8,128)(2,1)S(1)}, u32[]{:S(2)}, u32[]{:S(2)}) collective-permute-start(bf16[1280,128]{1,0:T(8,128)(2,1)S(1)} %get-tuple-element.32), channel_id=1, source_target_pairs={{0,64},{64,128},{128,192},{192,0},{1,65},{65,129},{129,193},{193,1... | collective-permute-start | bytes 983048 | tf_op jit(solution)/shard_map/ppermute | solution.py:25
  18.0 16.0 %collective-permute-start.11 = (bf16[1280,128]{1,0:T(8,128)(2,1)S(1)}, bf16[1280,128]{1,0:T(8,128)(2,1)S(1)}, u32[]{:S(2)}, u32[]{:S(2)}) collective-permute-start(bf16[1280,128]{1,0:T(8,128)(2,1)S(1)} %get-tuple-element.33), channel_id=1, source_target_pairs={{0,128},{64,192},{128,0},{192,64},{1,129},{65,193},{129,1},{193,65... | collective-permute-start | bytes 983048 | tf_op jit(solution)/shard_map/ppermute | solution.py:25
  34.9 21.5 %collective-permute-start.2 = (bf16[8,30,8,128]{3,2,1,0:T(8,128)(2,1)S(1)}, bf16[8,30,8,128]{3,2,1,0:T(8,128)(2,1)S(1)}, u32[]{:S(2)}, u32[]{:S(2)}) collective-permute-start(bf16[8,30,8,128]{3,2,1,0:T(8,128)(2,1)S(1)} %all-to-all-done.refs_0_), channel_id=1, source_target_pairs={{0,48},{16,0},{32,16},{48,32},{1,49},{17,1},{33,17},{49,33},{2,50}... | collective-permute-start | bytes 1474568 | tf_op jit(solution)/shard_map/ppermute | solution.py:25
  38.0 8.4 %collective-permute-start.13 = (bf16[4,320,128]{2,1,0:T(8,128)(2,1)S(1)}, bf16[4,320,128]{2,1,0:T(8,128)(2,1)S(1)}, u32[]{:S(2)}, u32[]{:S(2)}) collective-permute-start(bf16[4,320,128]{2,1,0:T(8,128)(2,1)S(1)} %pad_maximum_fusion.4), channel_id=1, source_target_pairs={{0,1},{1,2},{2,3},{3,4},{4,5},{5,6},{6,7},{7,8},{8,9},{9,10},{10,1... | collective-permute-start | bytes 983048 | tf_op jit(solution)/shard_map/ppermute | solution.py:226
  40.0 16.4 %collective-permute-start.1 = (bf16[8,30,8,128]{3,2,1,0:T(8,128)(2,1)S(1)}, bf16[8,30,8,128]{3,2,1,0:T(8,128)(2,1)S(1)}, u32[]{:S(2)}, u32[]{:S(2)}) collective-permute-start(bf16[8,30,8,128]{3,2,1,0:T(8,128)(2,1)S(1)} %all-to-all-done.refs_0_), channel_id=1, source_target_pairs={{0,32},{16,48},{32,0},{48,16},{1,33},{17,49},{33,1},{49,17},{2,34}... | collective-permute-start | bytes 1474568 | tf_op jit(solution)/shard_map/ppermute | solution.py:25
  40.7 7.9 %collective-permute-start.14 = (bf16[4,320,128]{2,1,0:T(8,128)(2,1)S(1)}, bf16[4,320,128]{2,1,0:T(8,128)(2,1)S(1)}, u32[]{:S(2)}, u32[]{:S(2)}) collective-permute-start(bf16[4,320,128]{2,1,0:T(8,128)(2,1)S(1)} %pad_maximum_fusion.5), channel_id=1, source_target_pairs={{1,0},{2,1},{3,2},{4,3},{5,4},{6,5},{7,6},{8,7},{9,8},{10,9},{11,1... | collective-permute-start | bytes 983048 | tf_op jit(solution)/shard_map/ppermute | solution.py:231
  44.1 22.1 %collective-permute-start = (bf16[8,30,8,128]{3,2,1,0:T(8,128)(2,1)S(1)}, bf16[8,30,8,128]{3,2,1,0:T(8,128)(2,1)S(1)}, u32[]{:S(2)}, u32[]{:S(2)}) collective-permute-start(bf16[8,30,8,128]{3,2,1,0:T(8,128)(2,1)S(1)} %all-to-all-done.refs_0_), channel_id=1, source_target_pairs={{0,16},{16,32},{32,48},{48,0},{1,17},{17,33},{33,49},{49,1},{2,18}... | collective-permute-start | bytes 1474568 | tf_op jit(solution)/shard_map/ppermute | solution.py:25
  46.4 19.8 %collective-permute-start.3 = (bf16[8,30,8,128]{3,2,1,0:T(8,128)(2,1)S(1)}, bf16[8,30,8,128]{3,2,1,0:T(8,128)(2,1)S(1)}, u32[]{:S(2)}, u32[]{:S(2)}) collective-permute-start(bf16[8,30,8,128]{3,2,1,0:T(8,128)(2,1)S(1)} %all-to-all-done.refs_0_), channel_id=1, source_target_pairs={{0,1},{1,0},{2,3},{3,2},{4,5},{5,4},{6,7},{7,6},{8,9},{9,8},{10,11... | collective-permute-start | bytes 1474568 | tf_op jit(solution)/shard_map/ppermute | solution.py:25
  56.4 9.9 %collective-permute-start.6 = (bf16[8,30,8,128]{3,2,1,0:T(8,128)(2,1)S(1)}, bf16[8,30,8,128]{3,2,1,0:T(8,128)(2,1)S(1)}, u32[]{:S(2)}, u32[]{:S(2)}) collective-permute-start(bf16[8,30,8,128]{3,2,1,0:T(8,128)(2,1)S(1)} %collective-permute-done.2.refs_3_), channel_id=1, source_target_pairs={{0,1},{1,0},{2,3},{3,2},{4,5},{5,4},{6,7},{7,6},{8,9},{9,8},{10,11... | collective-permute-start | bytes 1474568 | tf_op jit(solution)/shard_map/ppermute | solution.py:25
  56.4 9.9 %collective-permute-start.5 = (bf16[8,30,8,128]{3,2,1,0:T(8,128)(2,1)S(1)}, bf16[8,30,8,128]{3,2,1,0:T(8,128)(2,1)S(1)}, u32[]{:S(2)}, u32[]{:S(2)}) collective-permute-start(bf16[8,30,8,128]{3,2,1,0:T(8,128)(2,1)S(1)} %collective-permute-done.1.refs_2_), channel_id=1, source_target_pairs={{0,1},{1,0},{2,3},{3,2},{4,5},{5,4},{6,7},{7,6},{8,9},{9,8},{10,11... | collective-permute-start | bytes 1474568 | tf_op jit(solution)/shard_map/ppermute | solution.py:25
  66.2 1.9 %collective-permute-start.4 = (bf16[8,30,8,128]{3,2,1,0:T(8,128)(2,1)S(1)}, bf16[8,30,8,128]{3,2,1,0:T(8,128)(2,1)S(1)}, u32[]{:S(2)}, u32[]{:S(2)}) collective-permute-start(bf16[8,30,8,128]{3,2,1,0:T(8,128)(2,1)S(1)} %collective-permute-done.refs_1_), channel_id=1, source_target_pairs={{0,1},{1,0},{2,3},{3,2},{4,5},{5,4},{6,7},{7,6},{8,9},{9,8},{10,11... | collective-permute-start | bytes 1474568 | tf_op jit(solution)/shard_map/ppermute | solution.py:25
  68.1 8.7 %collective-permute-start.9 = (f32[8,128]{1,0:T(8,128)S(1)}, f32[8,128]{1,0:T(8,128)S(1)}, u32[]{:S(2)}, u32[]{:S(2)}) collective-permute-start(f32[8,128]{1,0:T(8,128)S(1)} %add_add_fusion.2), channel_id=1, source_target_pairs={{0,192},{64,0},{128,64},{192,128},{1,193},{65,1},{129,65},{193,129... | collective-permute-start | bytes 12296 | tf_op jit(solution)/shard_map/ppermute | solution.py:25
  68.2 8.6 %collective-permute-start.7 = (f32[8,128]{1,0:T(8,128)S(1)}, f32[8,128]{1,0:T(8,128)S(1)}, u32[]{:S(2)}, u32[]{:S(2)}) collective-permute-start(f32[8,128]{1,0:T(8,128)S(1)} %add_add_fusion.2), channel_id=1, source_target_pairs={{0,64},{64,128},{128,192},{192,0},{1,65},{65,129},{129,193},{193,1... | collective-permute-start | bytes 12296 | tf_op jit(solution)/shard_map/ppermute | solution.py:25
  70.2 6.6 %collective-permute-start.8 = (f32[8,128]{1,0:T(8,128)S(1)}, f32[8,128]{1,0:T(8,128)S(1)}, u32[]{:S(2)}, u32[]{:S(2)}) collective-permute-start(f32[8,128]{1,0:T(8,128)S(1)} %add_add_fusion.2), channel_id=1, source_target_pairs={{0,128},{64,192},{128,0},{192,64},{1,129},{65,193},{129,1},{193,65... | collective-permute-start | bytes 12296 | tf_op jit(solution)/shard_map/ppermute | solution.py:25
  70.8 6.5 %copy-start.2 = (f32[512]{0:T(512)S(1)}, f32[512]{0:T(512)}, u32[]{:S(2)}) copy-start(f32[512]{0:T(512)} %param.6) | copy-start | bytes 6148
  70.8 6.5 %copy-start.3 = (f32[512]{0:T(512)S(1)}, f32[512]{0:T(512)}, u32[]{:S(2)}) copy-start(f32[512]{0:T(512)} %param.7) | copy-start | bytes 6148
  78.1 5.0 %collective-permute-start.20 = (f32[8,128]{1,0:T(8,128)S(1)}, f32[8,128]{1,0:T(8,128)S(1)}, u32[]{:S(2)}, u32[]{:S(2)}) collective-permute-start(f32[8,128]{1,0:T(8,128)S(1)} %shard_map.78), channel_id=1, source_target_pairs={{0,192},{64,0},{128,64},{192,128},{1,193},{65,1},{129,65},{193,129... | collective-permute-start | bytes 12296 | tf_op jit(solution)/shard_map/ppermute | solution.py:25
  80.3 4.8 %collective-permute-start.18 = (f32[8,128]{1,0:T(8,128)S(1)}, f32[8,128]{1,0:T(8,128)S(1)}, u32[]{:S(2)}, u32[]{:S(2)}) collective-permute-start(f32[8,128]{1,0:T(8,128)S(1)} %shard_map.78), channel_id=1, source_target_pairs={{0,64},{64,128},{128,192},{192,0},{1,65},{65,129},{129,193},{193,1... | collective-permute-start | bytes 12296 | tf_op jit(solution)/shard_map/ppermute | solution.py:25
  80.3 5.1 %collective-permute-start.19 = (f32[8,128]{1,0:T(8,128)S(1)}, f32[8,128]{1,0:T(8,128)S(1)}, u32[]{:S(2)}, u32[]{:S(2)}) collective-permute-start(f32[8,128]{1,0:T(8,128)S(1)} %shard_map.78), channel_id=1, source_target_pairs={{0,128},{64,192},{128,0},{192,64},{1,129},{65,193},{129,1},{193,65... | collective-permute-start | bytes 12296 | tf_op jit(solution)/shard_map/ppermute | solution.py:25
  86.1 19.3 %all-to-all-start.1 = ((f32[64,8,128]{2,1,0:T(8,128)}), f32[64,8,128]{2,1,0:T(8,128)S(1)}, u32[]{:S(2)}, u32[]{:S(2)}) async-start(f32[64,8,128]{2,1,0:T(8,128)} %broadcast_in_dim.36), calls=%async_computation.1 | async-start | bytes 524288 | tf_op jit(solution)/shard_map/all_to_all | solution.py:256
  93.7 17.6 %collective-permute-start.17 = (f32[160,512]{1,0:T(8,128)S(1)}, f32[160,512]{1,0:T(8,128)S(1)}, u32[]{:S(2)}, u32[]{:S(2)}) collective-permute-start(f32[160,512]{1,0:T(8,128)S(1)} %get-tuple-element.16.part1), channel_id=1, source_target_pairs={{0,192},{64,0},{128,64},{192,128},{1,193},{65,1},{129,65},{193,129... | collective-permute-start | bytes 983048 | tf_op jit(solution)/shard_map/ppermute | solution.py:25
  97.0 17.7 %collective-permute-start.15 = (f32[160,512]{1,0:T(8,128)S(1)}, f32[160,512]{1,0:T(8,128)S(1)}, u32[]{:S(2)}, u32[]{:S(2)}) collective-permute-start(f32[160,512]{1,0:T(8,128)S(1)} %get-tuple-element.14.part3), channel_id=1, source_target_pairs={{0,64},{64,128},{128,192},{192,0},{1,65},{65,129},{129,193},{193,1... | collective-permute-start | bytes 983048 | tf_op jit(solution)/shard_map/ppermute | solution.py:25
  97.0 17.7 %collective-permute-start.16 = (f32[160,512]{1,0:T(8,128)S(1)}, f32[160,512]{1,0:T(8,128)S(1)}, u32[]{:S(2)}, u32[]{:S(2)}) collective-permute-start(f32[160,512]{1,0:T(8,128)S(1)} %get-tuple-element.15.part2), channel_id=1, source_target_pairs={{0,128},{64,192},{128,0},{192,64},{1,129},{65,193},{129,1},{193,65... | collective-permute-start | bytes 983048 | tf_op jit(solution)/shard_map/ppermute | solution.py:25

commit v3 on v2

v3 whole, which is shorter than its diff:
```python
import functools

import jax
import jax.numpy as jnp
from jax import lax
from jax.experimental import pallas as pl
from jax.experimental.pallas import tpu as pltpu
from jax.sharding import Mesh
from jax.sharding import PartitionSpec as P

GROUPS = 32
XS, YS, ZS, CS = 4, 4, 8, 2
ROWS = YS * ZS * CS
FRAMES = XS
SIZES = {"x": XS, "y": YS, "z": ZS, "c": CS}
ROW_AXES = ("y", "z", "c")
TAPS = 9
PLANES = 3 * TAPS
UNITS = ((0, 1, 2, 3), (0, 1, 2), (0, 1))
VMEM = pl.BlockSpec(memory_space=pltpu.VMEM)


def send(value, axis, step):
    size = SIZES[axis]
    return lax.ppermute(value, axis, [(i, (i + step) % size) for i in range(size)])


def pool_kernel(msg0, msg1, msg2, msg3, low, high, out2, out1, out0, sums, pooled):
    cells = out2.shape[1] // FRAMES
    fine = 2 * cells
    place = lax.axis_index("x")
    zero = jnp.zeros((8, 128), jnp.float32)
    for band in range(3):
        sums[band, 0:8] = zero
        sums[band, 8 + fine : 16 + fine] = zero
    for k, msg in enumerate((msg0, msg1, msg2, msg3)):
        frame = lax.rem(place + FRAMES - k, FRAMES)
        upper = msg[0].astype(jnp.float32)
        lower = msg[1].astype(jnp.float32)
        sums[0, 8 : 8 + fine] = lower + high[k].astype(jnp.float32)
        sums[1, 8 : 8 + fine] = upper + lower
        sums[2, 8 : 8 + fine] = low[k].astype(jnp.float32) + upper
        for band in range(3):
            at = sums.at[band]
            before = at[pl.ds(7, cells, stride=2), :]
            even = at[pl.ds(8, cells, stride=2), :]
            odd = at[pl.ds(9, cells, stride=2), :]
            after = at[pl.ds(10, cells, stride=2), :]
            pooled[frame, band * 3 + 0] = odd + after
            pooled[frame, band * 3 + 1] = even + odd
            pooled[frame, band * 3 + 2] = before + even
    for tap in range(TAPS):
        lanes = slice(tap * 128, tap * 128 + 128)

        def put(out, unit, value):
            head = value.astype(jnp.bfloat16)
            tail = (value - head.astype(jnp.float32)).astype(jnp.bfloat16)
            out[0, unit * cells : (unit + 1) * cells, lanes] = head
            out[1, unit * cells : (unit + 1) * cells, lanes] = tail

        p0, p1, p2, p3 = (pooled[t, tap] for t in range(FRAMES))
        put(out2, 0, p0)
        put(out2, 1, p1)
        put(out2, 2, p2)
        put(out2, 3, p3)
        p01 = p0 + p1
        put(out1, 0, p01)
        put(out1, 1, p2)
        put(out1, 2, p3)
        put(out0, 0, p01 + p2)
        put(out0, 1, p3)


def pool(msgs, low, high):
    cells = low.shape[1] // 2
    shapes = [
        jax.ShapeDtypeStruct((2, len(units) * cells, TAPS * 128), jnp.bfloat16) for units in UNITS
    ]
    return pl.pallas_call(
        pool_kernel,
        out_shape=shapes,
        in_specs=[VMEM] * 6,
        out_specs=[VMEM] * 3,
        scratch_shapes=[
            pltpu.VMEM((3, 2 * cells + 16, 128), jnp.float32),
            pltpu.VMEM((FRAMES, TAPS, cells, 128), jnp.float32),
        ],
        compiler_params=pltpu.CompilerParams(vmem_limit_bytes=12 << 20),
        cost_estimate=pl.CostEstimate(flops=20_000_000, bytes_accessed=9_000_000, transcendentals=0),
    )(*msgs, low, high)


def split_kernel(cot, out0, out1, out2, out3, sems):
    place = lax.axis_index("x")
    copies = []
    for k, out in enumerate((out0, out1, out2, out3)):
        first = pl.multiple_of(lax.rem(place + k, FRAMES) * 128, 128)
        copies.append(pltpu.make_async_copy(cot.at[0, :, :, pl.ds(first, 128)], out, sems.at[k]))
    for copy in copies:
        copy.start()
    for copy in copies:
        copy.wait()


def split(cotangent):
    shape = jax.ShapeDtypeStruct(cotangent.shape[1:3] + (128,), cotangent.dtype)
    return pl.pallas_call(
        split_kernel,
        out_shape=[shape] * FRAMES,
        in_specs=[pl.BlockSpec(memory_space=pl.ANY)],
        out_specs=[VMEM] * FRAMES,
        scratch_shapes=[pltpu.SemaphoreType.DMA((FRAMES,))],
        compiler_params=pltpu.CompilerParams(vmem_limit_bytes=2 << 20),
        cost_estimate=pl.CostEstimate(flops=0, bytes_accessed=1_300_000, transcendentals=0),
    )(cotangent)


def message_kernel(latent, weight, out, stats):
    channels = latent.shape[1]
    for q in range(channels // 128):
        values = latent[:, q * 128 : q * 128 + 128].astype(jnp.float32)
        stats[q : q + 1] = jnp.sum(values, axis=0, keepdims=True)
        stats[4 + q : 5 + q] = jnp.sum(values * values, axis=0, keepdims=True)
    total = stats[...]
    head = total.astype(jnp.bfloat16)
    rest = total - head.astype(jnp.float32)
    middle = rest.astype(jnp.bfloat16)
    last = (rest - middle.astype(jnp.float32)).astype(jnp.bfloat16)
    for z in range(ZS):
        out[z, 0:PLANES] = weight[...]
        out[z, PLANES] = head
        out[z, PLANES + 1] = middle
        out[z, PLANES + 2] = last


def message(latent, weight):
    return pl.pallas_call(
        message_kernel,
        out_shape=jax.ShapeDtypeStruct((ZS, PLANES + 3, 8, 128), jnp.bfloat16),
        in_specs=[VMEM] * 2,
        out_specs=VMEM,
        scratch_shapes=[pltpu.VMEM((8, 128), jnp.float32)],
        compiler_params=pltpu.CompilerParams(vmem_limit_bytes=3 << 20),
        cost_estimate=pl.CostEstimate(flops=250_000, bytes_accessed=720_000, transcendentals=0),
    )(latent, weight)


def rims_kernel(msg0, msg1, msg2, msg3, first, last):
    for k, msg in enumerate((msg0, msg1, msg2, msg3)):
        first[k] = msg[0]
        last[k] = msg[1]


def rims(msgs):
    shape = jax.ShapeDtypeStruct((FRAMES,) + msgs[0].shape[1:], jnp.bfloat16)
    return pl.pallas_call(
        rims_kernel,
        out_shape=[shape] * 2,
        in_specs=[VMEM] * FRAMES,
        out_specs=[VMEM] * 2,
        compiler_params=pltpu.CompilerParams(vmem_limit_bytes=3 << 20),
        cost_estimate=pl.CostEstimate(flops=0, bytes_accessed=1_300_000, transcendentals=0),
    )(*msgs)


def product_kernel(steps, aliased, *refs):
    count = CS * len(steps)
    pieces = refs[:count]
    left2, left1, left0 = refs[count : count + 3]
    skip = count + 3 + (FRAMES if aliased else 0)
    outs = refs[skip : skip + FRAMES]
    weights, acc, sems = refs[skip + FRAMES :]
    y, c = lax.axis_index("y"), lax.axis_index("c")
    cells = outs[0].shape[1]
    copies = []
    for index, step in enumerate(steps):
        for side in range(CS):
            core = c if side == 0 else 1 - c
            piece = pieces[index * CS + side]
            for z in range(ZS):
                row = pl.multiple_of(index * 128 + z * (CS * 8) + core * 8, 8)
                copies.append(
                    pltpu.make_async_copy(
                        piece.at[z, 0:PLANES],
                        weights.at[:, pl.ds(row, 8), :],
                        sems.at[len(copies)],
                    )
                )
    for copy in copies:
        copy.start()
    for copy in copies:
        copy.wait()
    for tap, left in ((2, left2), (1, left1), (0, left0)):
        right = jnp.concatenate([weights[tap * TAPS + t] for t in range(TAPS)], axis=1)
        total = None
        for half in range(2):
            part = lax.dot_general(
                left[half], right, (((1,), (1,)), ((), ())), preferred_element_type=jnp.float32
            )
            total = part if total is None else total + part
        if tap == 2:
            acc[...] = total
        else:
            acc[0 : total.shape[0]] += total
    place = lax.axis_index("x")
    for index, step in enumerate(steps):
        source_y = lax.rem(y + YS - step, YS)
        lanes = slice(index * 128, index * 128 + 128)
        for k, out in enumerate(outs):
            frame = lax.rem(place + FRAMES - k, FRAMES)
            out[source_y] = acc[pl.ds(pl.multiple_of(frame * cells, 8), cells), lanes]


def product(pieces, steps, lefts, before):
    cells = lefts[0].shape[1] // FRAMES
    aliased = before is not None
    inputs = [*pieces, *lefts, *(before if aliased else [])]
    return pl.pallas_call(
        functools.partial(product_kernel, steps, aliased),
        out_shape=[jax.ShapeDtypeStruct((YS, cells, 128), jnp.float32)] * FRAMES,
        in_specs=[pl.BlockSpec(memory_space=pl.ANY)] * len(pieces)
        + [VMEM] * (len(inputs) - len(pieces)),
        out_specs=[VMEM] * FRAMES,
        scratch_shapes=[
            pltpu.VMEM((PLANES, len(steps) * 128, 128), jnp.bfloat16),
            pltpu.VMEM((FRAMES * cells, len(steps) * 128), jnp.float32),
            pltpu.SemaphoreType.DMA((CS * ZS * len(steps),)),
        ],
        input_output_aliases={len(pieces) + 3 + k: k for k in range(FRAMES)} if aliased else {},
        compiler_params=pltpu.CompilerParams(vmem_limit_bytes=12 << 20),
        cost_estimate=pl.CostEstimate(
            flops=1_700_000_000, bytes_accessed=9_000_000, transcendentals=0
        ),
    )(*inputs)


def slope(features, chan, lanes):
    mean, inv, gain, bias = (chan[r : r + 1, lanes] for r in range(4))
    normed = (features.astype(jnp.float32) - mean) * inv
    pre = normed * gain + bias
    sigmoid_pre = 1.0 / (1.0 + jnp.exp(-pre))
    return normed, sigmoid_pre * (1.0 + pre * (1.0 - sigmoid_pre))


def sums_kernel(part0, part1, part2, part3, lat0, lat1, lat2, lat3, chan, out):
    cells, channels = lat0.shape
    for q in range(channels // 128):
        lanes = slice(q * 128, q * 128 + 128)
        first = jnp.zeros((8, 128), jnp.float32)
        second = jnp.zeros((8, 128), jnp.float32)
        for part, lat in ((part0, lat0), (part1, lat1), (part2, lat2), (part3, lat3)):
            normed, gate = slope(lat[:, lanes], chan, lanes)
            act = part[q] * gate
            first = first + act.reshape(cells // 8, 8, 128).sum(axis=0)
            second = second + (act * normed).reshape(cells // 8, 8, 128).sum(axis=0)
        out[q : q + 1] = jnp.sum(first, axis=0, keepdims=True)
        out[4 + q : 5 + q] = jnp.sum(second, axis=0, keepdims=True)


def partial_sums(parts, lats, chan):
    return pl.pallas_call(
        sums_kernel,
        out_shape=jax.ShapeDtypeStruct((8, 128), jnp.float32),
        in_specs=[VMEM] * 9,
        out_specs=VMEM,
        compiler_params=pltpu.CompilerParams(vmem_limit_bytes=4 << 20),
        cost_estimate=pl.CostEstimate(
            flops=6_000_000, bytes_accessed=2_600_000, transcendentals=330_000
        ),
    )(*parts, *lats, chan)


def final_kernel(count, sum0, sum1, sum2, sum3, part0, part1, part2, part3, lat, chan, grad, sums):
    cells, channels = lat.shape
    per_group = channels // GROUPS
    total = (sum0[...] + sum1[...] + (sum2[...] + sum3[...])) / count
    sums[...] = total
    row = lax.broadcasted_iota(jnp.int32, (128, 128), 0) // per_group
    col = lax.broadcasted_iota(jnp.int32, (128, 128), 1) // per_group
    same = jnp.where(row == col, 1.0, 0.0)
    gains = jnp.concatenate([chan[2:3, q * 128 : q * 128 + 128] for q in range(4)] * 2, axis=0)
    means = lax.dot_general(
        total * gains,
        same,
        (((1,), (0,)), ((), ())),
        precision=lax.Precision.HIGHEST,
        preferred_element_type=jnp.float32,
    ) / per_group
    for q in range(channels // 128):
        lanes = slice(q * 128, q * 128 + 128)
        normed, gate = slope(lat[:, lanes], chan, lanes)
        up_grad = part0[q] + part1[q] + (part2[q] + part3[q])
        grad[:, lanes] = chan[1:2, lanes] * (
            up_grad * gate * chan[2:3, lanes]
            - means[q : q + 1]
            - normed * means[4 + q : 5 + q]
        )


def final(count, sums, parts, lat, chan):
    return pl.pallas_call(
        functools.partial(final_kernel, count),
        out_shape=[
            jax.ShapeDtypeStruct(lat.shape, jnp.float32),
            jax.ShapeDtypeStruct((8, 128), jnp.float32),
        ],
        in_specs=[VMEM] * 10,
        out_specs=[VMEM] * 2,
        compiler_params=pltpu.CompilerParams(vmem_limit_bytes=4 << 20),
        cost_estimate=pl.CostEstimate(
            flops=2_000_000, bytes_accessed=1_900_000, transcendentals=82_000
        ),
    )(*sums, *parts, lat, chan)


def on_device(latent, norm_gain, norm_bias, conv_weight, cotangent):
    cells, channels = latent.shape[2], latent.shape[3]
    per_group = channels // GROUPS
    cell_count = FRAMES * ROWS * cells
    own = latent[0, 0]

    block = lax.all_to_all(
        message(own, conv_weight.reshape(PLANES, 8, 128)), "z", 0, 0, tiled=True
    )

    msgs = [
        msg if step == 0 else send(msg, "x", step) for step, msg in enumerate(split(cotangent))
    ]
    block, msgs = lax.optimization_barrier((block, msgs))
    pieces = [block] + [send(block, "y", step) for step in range(1, YS)]
    first, last = rims(msgs)
    low = lax.ppermute(last, ROW_AXES, [(i, i + 1) for i in range(ROWS - 1)])
    high = lax.ppermute(first, ROW_AXES, [(i + 1, i) for i in range(ROWS - 1)])
    late, _ = lax.optimization_barrier((own, first))
    lats = [own] + [send(late, "x", step) for step in range(1, FRAMES)]
    lefts = pool(msgs, low, high)
    others = [send(piece, "c", 1) for piece in pieces]
    partial = None
    for steps in ((0, 3), (2, 1)):
        chosen = [piece for step in steps for piece in (pieces[step], others[step])]
        partial = product(chosen, steps, lefts, partial)

    gathered = sum(
        jnp.sum(piece[:, PLANES:].astype(jnp.float32), axis=(0, 1)) for piece in pieces + others
    )
    total = gathered + sum(send(gathered, "x", step) for step in range(1, FRAMES))
    group = total.reshape(2, GROUPS, per_group).sum(axis=2) / (cell_count * per_group)
    group_mean = group[0]
    group_var = group[1] - group_mean * group_mean
    inv_std = lax.rsqrt(group_var + 1e-06)
    chan = jnp.stack(
        [jnp.repeat(group_mean, per_group), jnp.repeat(inv_std, per_group), norm_gain, norm_bias]
    )

    sums = partial_sums(partial, lats, chan)
    parts = [partial[0]] + [send(partial[FRAMES - step], "x", step) for step in range(1, FRAMES)]
    sums = lax.all_to_all(
        jnp.broadcast_to(sums[None], (ROWS, 8, 128)), ROW_AXES, 0, 0, tiled=True
    ).sum(axis=0)
    sums = [sums] + [send(sums, "x", step) for step in range(1, FRAMES)]
    latent_grad, chan_grad = final(cell_count, sums, parts, own, chan)
    bias_grad, gain_grad = chan_grad.reshape(2, channels)
    return (latent_grad.reshape(1, 1, cells, channels), gain_grad, bias_grad)


def solution(mesh):
    fine = Mesh(mesh.devices.reshape(XS, YS, ZS, CS), ("x", "y", "z", "c"))
    image = P("x", ROW_AXES, None, None)
    return jax.shard_map(
        on_device,
        mesh=fine,
        in_specs=(image, P(), P(), P(None, None, None, ROW_AXES, "x"), image),
        out_specs=(image, P(), P()),
        check_vma=False,
    )
```

time: 116 us -> 105 us (0.905)
  waiting for transfers between devices: 51.9 us -> 34.1 us
  starting transfers between devices: 44.6 us -> 53.5 us
  other arithmetic: 3.32 us -> 0.42 us
  Pallas kernels: 8.19 us -> 10.6 us
  local copies, waits for them, and re-layouts: 6.72 us -> 4.52 us
    ppermute x19 -> x22, waiting for transfers between devices: 41.7 us -> 22.5 us  [send(): lax.ppermute(value, axis, [(i, (i + step) % size) for i in range(size)])]
    ppermute x19 -> x22, starting transfers between devices: 23.2 us -> 29.7 us  [send(): lax.ppermute(value, axis, [(i, (i + step) % size) for i in range(size)])]
    another operation x10 -> x3, local copies, waits for them, and re-layouts: 4.2 us -> 0.75 us  [the longest x1 0.58 us: on_device(): bias_grad, gain_grad = chan_grad.reshape(2, channels)]
    all_to_all x1, starting transfers between devices: 7.53 us -> 10.9 us  [on_device(): lax.all_to_all(jnp.broadcast_to(sums[None], (ROWS, 8, 128)), ROW_AXES, 0,...]
    all_to_all x1, waiting for transfers between devices: 0.01 us -> 2.92 us  [on_device(): lax.all_to_all(message(own, conv_weight.reshape(PLANES, 8, 128)), 'z', 0,...]
    unnamed x10 -> x12, local copies, waits for them, and re-layouts: 0.07 us -> 2.83 us
    pallas_call x1 -> x6, Pallas kernels: 5.93 us -> 8.34 us  [the longest x2 6.15 us: product(): pl.pallas_call(functools.partial(product_kernel, steps, aliased), out_sha...]
    ppermute x2, waiting for transfers between devices: 3.52 us -> 1.61 us  [the longest x1 1.61 us: on_device(): high = lax.ppermute(first, ROW_AXES, [(i + 1, i) for i in range(ROWS - 1)])]
  transfers between devices with their start and end apart: 23 -> 26, of which waited for: 12 -> 11; matrix products, arithmetic and copies ran while one was open for 2% -> 1% of each run, Pallas kernels for 6% -> 8%
where the time goes in v3:
time: 105 us; the launch traced here: 104 us
  starting transfers between devices  53.5 us (51%)
  waiting for transfers between devices  34.1 us (32%)
  Pallas kernels  10.6 us (10%)
  local copies, waits for them, and re-layouts  4.52 us (4%)
    ppermute x22, starting transfers between devices, send(): lax.ppermute(value, axis, [(i, (i + step) % size) for i in range(size)])  29.7 us
    ppermute x22, waiting for transfers between devices, send(): lax.ppermute(value, axis, [(i, (i + step) % size) for i in range(size)])  22.5 us
    all_to_all x1, starting transfers between devices, on_device(): lax.all_to_all(jnp.broadcast_to(sums[None], (ROWS, 8, 128)), ROW_AXES, 0,...  10.9 us
    all_to_all x1, starting transfers between devices, on_device(): lax.all_to_all(message(own, conv_weight.reshape(PLANES, 8, 128)), 'z', 0,...  8.57 us
    all_to_all x1, waiting for transfers between devices, on_device(): lax.all_to_all(jnp.broadcast_to(sums[None], (ROWS, 8, 128)), ROW_AXES, 0,...  7.03 us
    pallas_call x2, Pallas kernels, product(): pl.pallas_call(functools.partial(product_kernel, steps, aliased), out_sha...  6.15 us
    all_to_all x1, waiting for transfers between devices, on_device(): lax.all_to_all(message(own, conv_weight.reshape(PLANES, 8, 128)), 'z', 0,...  2.92 us
    unnamed x12, local copies, waits for them, and re-layouts  2.83 us
  transfers between devices with their start and end apart: 26, of which 11 were waited for; matrix products, arithmetic and copies ran while one was open for 1% of the time, Pallas kernels for 8%

profile of v3, /device:TPU:32, one launch (start us, length us, event | category | flops | bytes accessed | tf_op | source)
XLA Modules:
  0.0 103.9 jit_solution(11490041477580533836)
XLA Ops:
  0.6 0.9 copy-done
  2.4 0.9 shard_map.76
  3.3 8.6 %all-to-all-start = ((bf16[8,30,8,128]{3,2,1,0:T(8,128)(2,1)}), bf16[8,30,8,128]{3,2,1,0:T(8,128)(2,1)S(1)}, u32[]{:S(2)}, u32[]{:S(2)}) async-start(bf16[8,30,8,128]{3,2,1,0:T(8,128)(2,1)} %shard_map.76), calls=%async_computation | async-start | bytes 983040 | tf_op jit(solution)/shard_map/all_to_all | solution.py:322
  11.8 1.1 %copy-done.2 = bf16[1,2,320,512]{3,2,1,0:T(8,128)(2,1)S(1)} copy-done((bf16[1,2,320,512]{3,2,1,0:T(8,128)(2,1)S(1)}, bf16[1,2,320,512]{3,2,1,0:T(8,128)(2,1)}, u32[]{:S(2)}) %copy-start.2) | copy-done | bytes 655384
  13.1 1.6 %collective-permute-start = (bf16[2,320,128]{2,1,0:T(8,128)(2,1)S(1)}, bf16[2,320,128]{2,1,0:T(8,128)(2,1)S(1)}, u32[]{:S(2)}, u32[]{:S(2)}) collective-permute-start(bf16[2,320,128]{2,1,0:T(8,128)(2,1)S(1)} %get-tuple-element.29), channel_id=1, source_target_pairs={{0,64},{64,128},{128,192},{192,0},{1,65},{65,129},{129,193},{193,1... | collective-permute-start | bytes 491528 | tf_op jit(solution)/shard_map/ppermute | solution.py:25
  14.7 2.7 %collective-permute-start.1 = (bf16[2,320,128]{2,1,0:T(8,128)(2,1)S(1)}, bf16[2,320,128]{2,1,0:T(8,128)(2,1)S(1)}, u32[]{:S(2)}, u32[]{:S(2)}) collective-permute-start(bf16[2,320,128]{2,1,0:T(8,128)(2,1)S(1)} %get-tuple-element.30), channel_id=1, source_target_pairs={{0,128},{64,192},{128,0},{192,64},{1,129},{65,193},{129,1},{193,65... | collective-permute-start | bytes 491528 | tf_op jit(solution)/shard_map/ppermute | solution.py:25
  17.4 1.4 %collective-permute-start.2 = (bf16[2,320,128]{2,1,0:T(8,128)(2,1)S(1)}, bf16[2,320,128]{2,1,0:T(8,128)(2,1)S(1)}, u32[]{:S(2)}, u32[]{:S(2)}) collective-permute-start(bf16[2,320,128]{2,1,0:T(8,128)(2,1)S(1)} %get-tuple-element.31), channel_id=1, source_target_pairs={{0,192},{64,0},{128,64},{192,128},{1,193},{65,1},{129,65},{193,129... | collective-permute-start | bytes 491528 | tf_op jit(solution)/shard_map/ppermute | solution.py:25
  18.8 1.7 %collective-permute-done.msg1 = bf16[2,320,128]{2,1,0:T(8,128)(2,1)S(1)} collective-permute-done((bf16[2,320,128]{2,1,0:T(8,128)(2,1)S(1)}, bf16[2,320,128]{2,1,0:T(8,128)(2,1)S(1)}, u32[]{:S(2)}, u32[]{:S(2)}) %collective-permute-start) | collective-permute-done | bytes 163872 | tf_op jit(solution)/shard_map/ppermute | solution.py:25
  20.5 3.7 %collective-permute-done.1.msg2 = bf16[2,320,128]{2,1,0:T(8,128)(2,1)S(1)} collective-permute-done((bf16[2,320,128]{2,1,0:T(8,128)(2,1)S(1)}, bf16[2,320,128]{2,1,0:T(8,128)(2,1)S(1)}, u32[]{:S(2)}, u32[]{:S(2)}) %collective-permute-start.1) | collective-permute-done | bytes 163872 | tf_op jit(solution)/shard_map/ppermute | solution.py:25
  24.3 2.9 %all-to-all-done.refs_0_ = bf16[8,30,8,128]{3,2,1,0:T(8,128)(2,1)S(1)} async-done(((bf16[8,30,8,128]{3,2,1,0:T(8,128)(2,1)}), bf16[8,30,8,128]{3,2,1,0:T(8,128)(2,1)S(1)}, u32[]{:S(2)}, u32[]{:S(2)}) %all-to-all-start) | async-done | bytes 491552 | tf_op jit(solution)/shard_map/all_to_all | solution.py:322
  27.2 3.0 %collective-permute-start.10 = (bf16[8,30,8,128]{3,2,1,0:T(8,128)(2,1)S(1)}, bf16[8,30,8,128]{3,2,1,0:T(8,128)(2,1)S(1)}, u32[]{:S(2)}, u32[]{:S(2)}) collective-permute-start(bf16[8,30,8,128]{3,2,1,0:T(8,128)(2,1)S(1)} %all-to-all-done.refs_0_), channel_id=1, source_target_pairs={{0,48},{16,0},{32,16},{48,32},{1,49},{17,1},{33,17},{49,33},{2,50}... | collective-permute-start | bytes 1474568 | tf_op jit(solution)/shard_map/ppermute | solution.py:25
  30.9 2.4 %collective-permute-start.8 = (bf16[4,320,128]{2,1,0:T(8,128)(2,1)S(1)}, bf16[4,320,128]{2,1,0:T(8,128)(2,1)S(1)}, u32[]{:S(2)}, u32[]{:S(2)}) collective-permute-start(bf16[4,320,128]{2,1,0:T(8,128)(2,1)S(1)} %get-tuple-element.38), channel_id=1, source_target_pairs={{1,0},{2,1},{3,2},{4,3},{5,4},{6,5},{7,6},{8,7},{9,8},{10,9},{11,1... | collective-permute-start | bytes 983048 | tf_op jit(solution)/shard_map/ppermute | solution.py:333
  33.3 1.0 %collective-permute-start.5 = (bf16[8,30,8,128]{3,2,1,0:T(8,128)(2,1)S(1)}, bf16[8,30,8,128]{3,2,1,0:T(8,128)(2,1)S(1)}, u32[]{:S(2)}, u32[]{:S(2)}) collective-permute-start(bf16[8,30,8,128]{3,2,1,0:T(8,128)(2,1)S(1)} %all-to-all-done.refs_0_), channel_id=1, source_target_pairs={{0,16},{16,32},{32,48},{48,0},{1,17},{17,33},{33,49},{49,1},{2,18}... | collective-permute-start | bytes 1474568 | tf_op jit(solution)/shard_map/ppermute | solution.py:25
  34.3 1.9 %collective-permute-start.7 = (bf16[4,320,128]{2,1,0:T(8,128)(2,1)S(1)}, bf16[4,320,128]{2,1,0:T(8,128)(2,1)S(1)}, u32[]{:S(2)}, u32[]{:S(2)}) collective-permute-start(bf16[4,320,128]{2,1,0:T(8,128)(2,1)S(1)} %get-tuple-element.37), channel_id=1, source_target_pairs={{0,1},{1,2},{2,3},{3,4},{4,5},{5,6},{6,7},{7,8},{8,9},{9,10},{10,1... | collective-permute-start | bytes 983048 | tf_op jit(solution)/shard_map/ppermute | solution.py:332
  36.3 1.6 %collective-permute-done.8.high = bf16[4,320,128]{2,1,0:T(8,128)(2,1)S(1)} collective-permute-done((bf16[4,320,128]{2,1,0:T(8,128)(2,1)S(1)}, bf16[4,320,128]{2,1,0:T(8,128)(2,1)S(1)}, u32[]{:S(2)}, u32[]{:S(2)}) %collective-permute-start.8) | collective-permute-done | bytes 327712 | tf_op jit(solution)/shard_map/ppermute | solution.py:333
  37.9 10.1 %collective-permute-done.10.refs_2_ = bf16[8,30,8,128]{3,2,1,0:T(8,128)(2,1)S(1)} collective-permute-done((bf16[8,30,8,128]{3,2,1,0:T(8,128)(2,1)S(1)}, bf16[8,30,8,128]{3,2,1,0:T(8,128)(2,1)S(1)}, u32[]{:S(2)}, u32[]{:S(2)}) %collective-permute-start.10) | collective-permute-done | bytes 491552 | tf_op jit(solution)/shard_map/ppermute | solution.py:25
  48.0 1.6 %collective-permute-start.12 = (bf16[160,512]{1,0:T(8,128)(2,1)S(1)}, bf16[160,512]{1,0:T(8,128)(2,1)S(1)}, u32[]{:S(2)}, u32[]{:S(2)}) collective-permute-start(bf16[160,512]{1,0:T(8,128)(2,1)S(1)} %bitcast.20), channel_id=1, source_target_pairs={{0,64},{64,128},{128,192},{192,0},{1,65},{65,129},{129,193},{193,1... | collective-permute-start | bytes 491528 | tf_op jit(solution)/shard_map/ppermute | solution.py:25
  49.6 1.5 %shard_map.79 = (bf16[2,640,1152]{2,1,0:T(8,128)(2,1)S(1)}, bf16[2,480,1152]{2,1,0:T(8,128)(2,1)S(1)}, bf16[2,320,1152]{2,1,0:T(8,128)(2,1)S(1)}) custom-call(bf16[2,320,128]{2,1,0:T(8,128)(2,1)S(1)} %get-tuple-element.33.msg0, bf16[2,320,128]{2,1,0:T(8,128)(2,1)S(1)} %collective-permute-done.msg1, bf16[2,320,128]{2,1,0:T(8,128)(2,1)S(1)} %collective-permute-done.1.msg2, ...), custom_call_target="tpu_custom_call" | custom-call | flops 20000000 | bytes 9000000 | tf_op jit(solution)/shard_map/pallas_call | solution.py:79
  51.8 3.0 %collective-permute-start.13 = (bf16[160,512]{1,0:T(8,128)(2,1)S(1)}, bf16[160,512]{1,0:T(8,128)(2,1)S(1)}, u32[]{:S(2)}, u32[]{:S(2)}) collective-permute-start(bf16[160,512]{1,0:T(8,128)(2,1)S(1)} %bitcast.21), channel_id=1, source_target_pairs={{0,128},{64,192},{128,0},{192,64},{1,129},{65,193},{129,1},{193,65... | collective-permute-start | bytes 491528 | tf_op jit(solution)/shard_map/ppermute | solution.py:25
  55.6 2.2 %collective-permute-start.16 = (f32[8,128]{1,0:T(8,128)S(1)}, f32[8,128]{1,0:T(8,128)S(1)}, u32[]{:S(2)}, u32[]{:S(2)}) collective-permute-start(f32[8,128]{1,0:T(8,128)S(1)} %add_add_fusion.1), channel_id=1, source_target_pairs={{0,128},{64,192},{128,0},{192,64},{1,129},{65,193},{129,1},{193,65... | collective-permute-start | bytes 12296 | tf_op jit(solution)/shard_map/ppermute | solution.py:25
  57.9 1.4 %collective-permute-start.17 = (f32[8,128]{1,0:T(8,128)S(1)}, f32[8,128]{1,0:T(8,128)S(1)}, u32[]{:S(2)}, u32[]{:S(2)}) collective-permute-start(f32[8,128]{1,0:T(8,128)S(1)} %add_add_fusion.1), channel_id=1, source_target_pairs={{0,192},{64,0},{128,64},{192,128},{1,193},{65,1},{129,65},{193,129... | collective-permute-start | bytes 12296 | tf_op jit(solution)/shard_map/ppermute | solution.py:25
  59.3 3.1 %shard_map.80 = (f32[4,160,128]{2,1,0:T(8,128)S(1)}, f32[4,160,128]{2,1,0:T(8,128)S(1)}, f32[4,160,128]{2,1,0:T(8,128)S(1)}, f32[4,160,128]{2,1,0:T(8,128)S(1)}) custom-call(bf16[8,30,8,128]{3,2,1,0:T(8,128)(2,1)S(1)} %all-to-all-done.refs_0_, bf16[8,30,8,128]{3,2,1,0:T(8,128)(2,1)S(1)} %collective-permute-done.9.refs_1_, ...), custom_call_target="tpu_custom_call" | custom-call | flops 1700000000 | bytes 9000000 | tf_op jit(solution)/shard_map/pallas_call | solution.py:218
  62.4 3.1 %shard_map.81 = (f32[4,160,128]{2,1,0:T(8,128)S(1)}, f32[4,160,128]{2,1,0:T(8,128)S(1)}, f32[4,160,128]{2,1,0:T(8,128)S(1)}, f32[4,160,128]{2,1,0:T(8,128)S(1)}) custom-call(bf16[8,30,8,128]{3,2,1,0:T(8,128)(2,1)S(1)} %collective-permute-done.3.refs_0_, ...), custom_call_target="tpu_custom_call", output_to_operand_aliasing={{0}: (7, {}), {1}: (8, {}), {2}: (9, {}), {3}: (10, {})} | custom-call | flops 1700000000 | bytes 9000000 | tf_op jit(solution)/shard_map/pallas_call | solution.py:218
  66.6 4.4 %collective-permute-done.14.lat3 = bf16[160,512]{1,0:T(8,128)(2,1)S(1)} collective-permute-done((bf16[160,512]{1,0:T(8,128)(2,1)S(1)}, bf16[160,512]{1,0:T(8,128)(2,1)S(1)}, u32[]{:S(2)}, u32[]{:S(2)}) %collective-permute-start.14) | collective-permute-done | bytes 163872 | tf_op jit(solution)/shard_map/ppermute | solution.py:25
  72.5 10.9 %all-to-all-start.1 = ((f32[64,8,128]{2,1,0:T(8,128)}), f32[64,8,128]{2,1,0:T(8,128)S(1)}, u32[]{:S(2)}, u32[]{:S(2)}) async-start(f32[64,8,128]{2,1,0:T(8,128)} %broadcast_in_dim.14), calls=%async_computation.1 | async-start | bytes 524288 | tf_op jit(solution)/shard_map/all_to_all | solution.py:357
  84.1 2.6 %collective-permute-start.22 = (f32[4,160,128]{2,1,0:T(8,128)S(1)}, f32[4,160,128]{2,1,0:T(8,128)S(1)}, u32[]{:S(2)}, u32[]{:S(2)}) collective-permute-start(f32[4,160,128]{2,1,0:T(8,128)S(1)} %get-tuple-element.48.part2), channel_id=1, source_target_pairs={{0,128},{64,192},{128,0},{192,64},{1,129},{65,193},{129,1},{193,65... | collective-permute-start | bytes 983048 | tf_op jit(solution)/shard_map/ppermute | solution.py:25
  86.7 1.4 %collective-permute-start.23 = (f32[4,160,128]{2,1,0:T(8,128)S(1)}, f32[4,160,128]{2,1,0:T(8,128)S(1)}, u32[]{:S(2)}, u32[]{:S(2)}) collective-permute-start(f32[4,160,128]{2,1,0:T(8,128)S(1)} %get-tuple-element.47.part1), channel_id=1, source_target_pairs={{0,192},{64,0},{128,64},{192,128},{1,193},{65,1},{129,65},{193,129... | collective-permute-start | bytes 983048 | tf_op jit(solution)/shard_map/ppermute | solution.py:25
  88.1 7.0 %all-to-all-done.1 = f32[64,8,128]{2,1,0:T(8,128)S(1)} async-done(((f32[64,8,128]{2,1,0:T(8,128)}), f32[64,8,128]{2,1,0:T(8,128)S(1)}, u32[]{:S(2)}, u32[]{:S(2)}) %all-to-all-start.1) | async-done | bytes 262176 | tf_op jit(solution)/shard_map/all_to_all | solution.py:357
  95.9 2.6 %collective-permute-start.19 = (f32[8,128]{1,0:T(8,128)S(1)}, f32[8,128]{1,0:T(8,128)S(1)}, u32[]{:S(2)}, u32[]{:S(2)}) collective-permute-start(f32[8,128]{1,0:T(8,128)S(1)} %reduce_sum.99.sum0), channel_id=1, source_target_pairs={{0,128},{64,192},{128,0},{192,64},{1,129},{65,193},{129,1},{193,65... | collective-permute-start | bytes 12296 | tf_op jit(solution)/shard_map/ppermute | solution.py:25
  98.5 1.4 %collective-permute-start.20 = (f32[8,128]{1,0:T(8,128)S(1)}, f32[8,128]{1,0:T(8,128)S(1)}, u32[]{:S(2)}, u32[]{:S(2)}) collective-permute-start(f32[8,128]{1,0:T(8,128)S(1)} %reduce_sum.99.sum0), channel_id=1, source_target_pairs={{0,192},{64,0},{128,64},{192,128},{1,193},{65,1},{129,65},{193,129... | collective-permute-start | bytes 12296 | tf_op jit(solution)/shard_map/ppermute | solution.py:25
  99.9 1.7 %collective-permute-done.22.part2 = f32[4,160,128]{2,1,0:T(8,128)S(1)} collective-permute-done((f32[4,160,128]{2,1,0:T(8,128)S(1)}, f32[4,160,128]{2,1,0:T(8,128)S(1)}, u32[]{:S(2)}, u32[]{:S(2)}) %collective-permute-start.22) | collective-permute-done | bytes 327712 | tf_op jit(solution)/shard_map/ppermute | solution.py:25
  102.3 1.1 %shard_map.83 = (f32[160,512]{1,0:T(8,128)}, f32[8,128]{1,0:T(8,128)S(1)}) custom-call(f32[8,128]{1,0:T(8,128)S(1)} %reduce_sum.99.sum0, f32[8,128]{1,0:T(8,128)S(1)} %collective-permute-done.18.sum1, f32[8,128]{1,0:T(8,128)S(1)} %collective-permute-done.19.sum2, f32[8,128]{1,0:T(8,128)S(1)} %collective-permute-done.20.sum3, ...), custom_call_target="tpu_custom_call" | custom-call | flops 2000000 | bytes 1900000 | tf_op jit(solution)/shard_map/pallas_call | solution.py:301
  (63 shorter events, 8.5 us)
Async XLA Ops:
  0.6 0.9 copy-start
  1.5 0.8 copy-start.3
  2.4 45.6 %copy-start.1 = (bf16[1,1,160,512]{3,2,1,0:T(8,128)(2,1)S(1)}, bf16[1,1,160,512]{3,2,1,0:T(8,128)(2,1)}, u32[]{:S(2)}) copy-start(bf16[1,1,160,512]{3,2,1,0:T(8,128)(2,1)} %param.5) | copy-start | bytes 491524
  3.3 23.9 %all-to-all-start = ((bf16[8,30,8,128]{3,2,1,0:T(8,128)(2,1)}), bf16[8,30,8,128]{3,2,1,0:T(8,128)(2,1)S(1)}, u32[]{:S(2)}, u32[]{:S(2)}) async-start(bf16[8,30,8,128]{3,2,1,0:T(8,128)(2,1)} %shard_map.76), calls=%async_computation | async-start | bytes 983040 | tf_op jit(solution)/shard_map/all_to_all | solution.py:322
  11.8 1.1 %copy-start.2 = (bf16[1,2,320,512]{3,2,1,0:T(8,128)(2,1)S(1)}, bf16[1,2,320,512]{3,2,1,0:T(8,128)(2,1)}, u32[]{:S(2)}) copy-start(bf16[1,2,320,512]{3,2,1,0:T(8,128)(2,1)} %cot.1) | copy-start | bytes 1966084
  13.1 7.4 %collective-permute-start = (bf16[2,320,128]{2,1,0:T(8,128)(2,1)S(1)}, bf16[2,320,128]{2,1,0:T(8,128)(2,1)S(1)}, u32[]{:S(2)}, u32[]{:S(2)}) collective-permute-start(bf16[2,320,128]{2,1,0:T(8,128)(2,1)S(1)} %get-tuple-element.29), channel_id=1, source_target_pairs={{0,64},{64,128},{128,192},{192,0},{1,65},{65,129},{129,193},{193,1... | collective-permute-start | bytes 491528 | tf_op jit(solution)/shard_map/ppermute | solution.py:25
  14.7 9.6 %collective-permute-start.1 = (bf16[2,320,128]{2,1,0:T(8,128)(2,1)S(1)}, bf16[2,320,128]{2,1,0:T(8,128)(2,1)S(1)}, u32[]{:S(2)}, u32[]{:S(2)}) collective-permute-start(bf16[2,320,128]{2,1,0:T(8,128)(2,1)S(1)} %get-tuple-element.30), channel_id=1, source_target_pairs={{0,128},{64,192},{128,0},{192,64},{1,129},{65,193},{129,1},{193,65... | collective-permute-start | bytes 491528 | tf_op jit(solution)/shard_map/ppermute | solution.py:25
  17.4 6.9 %collective-permute-start.2 = (bf16[2,320,128]{2,1,0:T(8,128)(2,1)S(1)}, bf16[2,320,128]{2,1,0:T(8,128)(2,1)S(1)}, u32[]{:S(2)}, u32[]{:S(2)}) collective-permute-start(bf16[2,320,128]{2,1,0:T(8,128)(2,1)S(1)} %get-tuple-element.31), channel_id=1, source_target_pairs={{0,192},{64,0},{128,64},{192,128},{1,193},{65,1},{129,65},{193,129... | collective-permute-start | bytes 491528 | tf_op jit(solution)/shard_map/ppermute | solution.py:25
  27.2 20.8 %collective-permute-start.10 = (bf16[8,30,8,128]{3,2,1,0:T(8,128)(2,1)S(1)}, bf16[8,30,8,128]{3,2,1,0:T(8,128)(2,1)S(1)}, u32[]{:S(2)}, u32[]{:S(2)}) collective-permute-start(bf16[8,30,8,128]{3,2,1,0:T(8,128)(2,1)S(1)} %all-to-all-done.refs_0_), channel_id=1, source_target_pairs={{0,48},{16,0},{32,16},{48,32},{1,49},{17,1},{33,17},{49,33},{2,50}... | collective-permute-start | bytes 1474568 | tf_op jit(solution)/shard_map/ppermute | solution.py:25
  30.2 20.8 %collective-permute-start.3 = (bf16[8,30,8,128]{3,2,1,0:T(8,128)(2,1)S(1)}, bf16[8,30,8,128]{3,2,1,0:T(8,128)(2,1)S(1)}, u32[]{:S(2)}, u32[]{:S(2)}) collective-permute-start(bf16[8,30,8,128]{3,2,1,0:T(8,128)(2,1)S(1)} %all-to-all-done.refs_0_), channel_id=1, source_target_pairs={{0,32},{16,48},{32,0},{48,16},{1,33},{17,49},{33,1},{49,17},{2,34}... | collective-permute-start | bytes 1474568 | tf_op jit(solution)/shard_map/ppermute | solution.py:25
  30.9 7.0 %collective-permute-start.8 = (bf16[4,320,128]{2,1,0:T(8,128)(2,1)S(1)}, bf16[4,320,128]{2,1,0:T(8,128)(2,1)S(1)}, u32[]{:S(2)}, u32[]{:S(2)}) collective-permute-start(bf16[4,320,128]{2,1,0:T(8,128)(2,1)S(1)} %get-tuple-element.38), channel_id=1, source_target_pairs={{1,0},{2,1},{3,2},{4,3},{5,4},{6,5},{7,6},{8,7},{9,8},{10,9},{11,1... | collective-permute-start | bytes 983048 | tf_op jit(solution)/shard_map/ppermute | solution.py:333
  33.3 18.4 %collective-permute-start.5 = (bf16[8,30,8,128]{3,2,1,0:T(8,128)(2,1)S(1)}, bf16[8,30,8,128]{3,2,1,0:T(8,128)(2,1)S(1)}, u32[]{:S(2)}, u32[]{:S(2)}) collective-permute-start(bf16[8,30,8,128]{3,2,1,0:T(8,128)(2,1)S(1)} %all-to-all-done.refs_0_), channel_id=1, source_target_pairs={{0,16},{16,32},{32,48},{48,0},{1,17},{17,33},{33,49},{49,1},{2,18}... | collective-permute-start | bytes 1474568 | tf_op jit(solution)/shard_map/ppermute | solution.py:25
  34.3 13.6 %collective-permute-start.7 = (bf16[4,320,128]{2,1,0:T(8,128)(2,1)S(1)}, bf16[4,320,128]{2,1,0:T(8,128)(2,1)S(1)}, u32[]{:S(2)}, u32[]{:S(2)}) collective-permute-start(bf16[4,320,128]{2,1,0:T(8,128)(2,1)S(1)} %get-tuple-element.37), channel_id=1, source_target_pairs={{0,1},{1,2},{2,3},{3,4},{4,5},{5,6},{6,7},{7,8},{8,9},{9,10},{10,1... | collective-permute-start | bytes 983048 | tf_op jit(solution)/shard_map/ppermute | solution.py:332
  37.9 13.9 %collective-permute-start.9 = (bf16[8,30,8,128]{3,2,1,0:T(8,128)(2,1)S(1)}, bf16[8,30,8,128]{3,2,1,0:T(8,128)(2,1)S(1)}, u32[]{:S(2)}, u32[]{:S(2)}) collective-permute-start(bf16[8,30,8,128]{3,2,1,0:T(8,128)(2,1)S(1)} %all-to-all-done.refs_0_), channel_id=1, source_target_pairs={{0,1},{1,0},{2,3},{3,2},{4,5},{5,4},{6,7},{7,6},{8,9},{9,8},{10,11... | collective-permute-start | bytes 1474568 | tf_op jit(solution)/shard_map/ppermute | solution.py:25
  47.9 6.9 %collective-permute-start.11 = (bf16[8,30,8,128]{3,2,1,0:T(8,128)(2,1)S(1)}, bf16[8,30,8,128]{3,2,1,0:T(8,128)(2,1)S(1)}, u32[]{:S(2)}, u32[]{:S(2)}) collective-permute-start(bf16[8,30,8,128]{3,2,1,0:T(8,128)(2,1)S(1)} %collective-permute-done.10.refs_2_), channel_id=1, source_target_pairs={{0,1},{1,0},{2,3},{3,2},{4,5},{5,4},{6,7},{7,6},{8,9},{9,8},{10,11... | collective-permute-start | bytes 1474568 | tf_op jit(solution)/shard_map/ppermute | solution.py:25
  48.0 18.6 %collective-permute-start.12 = (bf16[160,512]{1,0:T(8,128)(2,1)S(1)}, bf16[160,512]{1,0:T(8,128)(2,1)S(1)}, u32[]{:S(2)}, u32[]{:S(2)}) collective-permute-start(bf16[160,512]{1,0:T(8,128)(2,1)S(1)} %bitcast.20), channel_id=1, source_target_pairs={{0,64},{64,128},{128,192},{192,0},{1,65},{65,129},{129,193},{193,1... | collective-permute-start | bytes 491528 | tf_op jit(solution)/shard_map/ppermute | solution.py:25
  51.0 3.9 %collective-permute-start.4 = (bf16[8,30,8,128]{3,2,1,0:T(8,128)(2,1)S(1)}, bf16[8,30,8,128]{3,2,1,0:T(8,128)(2,1)S(1)}, u32[]{:S(2)}, u32[]{:S(2)}) collective-permute-start(bf16[8,30,8,128]{3,2,1,0:T(8,128)(2,1)S(1)} %collective-permute-done.3.refs_0_), channel_id=1, source_target_pairs={{0,1},{1,0},{2,3},{3,2},{4,5},{5,4},{6,7},{7,6},{8,9},{9,8},{10,11... | collective-permute-start | bytes 1474568 | tf_op jit(solution)/shard_map/ppermute | solution.py:25
  51.6 3.3 %collective-permute-start.6 = (bf16[8,30,8,128]{3,2,1,0:T(8,128)(2,1)S(1)}, bf16[8,30,8,128]{3,2,1,0:T(8,128)(2,1)S(1)}, u32[]{:S(2)}, u32[]{:S(2)}) collective-permute-start(bf16[8,30,8,128]{3,2,1,0:T(8,128)(2,1)S(1)} %collective-permute-done.5.refs_2_), channel_id=1, source_target_pairs={{0,1},{1,0},{2,3},{3,2},{4,5},{5,4},{6,7},{7,6},{8,9},{9,8},{10,11... | collective-permute-start | bytes 1474568 | tf_op jit(solution)/shard_map/ppermute | solution.py:25
  51.8 14.8 %collective-permute-start.13 = (bf16[160,512]{1,0:T(8,128)(2,1)S(1)}, bf16[160,512]{1,0:T(8,128)(2,1)S(1)}, u32[]{:S(2)}, u32[]{:S(2)}) collective-permute-start(bf16[160,512]{1,0:T(8,128)(2,1)S(1)} %bitcast.21), channel_id=1, source_target_pairs={{0,128},{64,192},{128,0},{192,64},{1,129},{65,193},{129,1},{193,65... | collective-permute-start | bytes 491528 | tf_op jit(solution)/shard_map/ppermute | solution.py:25
  55.0 10.5 %collective-permute-start.15 = (f32[8,128]{1,0:T(8,128)S(1)}, f32[8,128]{1,0:T(8,128)S(1)}, u32[]{:S(2)}, u32[]{:S(2)}) collective-permute-start(f32[8,128]{1,0:T(8,128)S(1)} %add_add_fusion.1), channel_id=1, source_target_pairs={{0,64},{64,128},{128,192},{192,0},{1,65},{65,129},{129,193},{193,1... | collective-permute-start | bytes 12296 | tf_op jit(solution)/shard_map/ppermute | solution.py:25
  55.6 10.4 %collective-permute-start.16 = (f32[8,128]{1,0:T(8,128)S(1)}, f32[8,128]{1,0:T(8,128)S(1)}, u32[]{:S(2)}, u32[]{:S(2)}) collective-permute-start(f32[8,128]{1,0:T(8,128)S(1)} %add_add_fusion.1), channel_id=1, source_target_pairs={{0,128},{64,192},{128,0},{192,64},{1,129},{65,193},{129,1},{193,65... | collective-permute-start | bytes 12296 | tf_op jit(solution)/shard_map/ppermute | solution.py:25
  57.9 8.2 %collective-permute-start.17 = (f32[8,128]{1,0:T(8,128)S(1)}, f32[8,128]{1,0:T(8,128)S(1)}, u32[]{:S(2)}, u32[]{:S(2)}) collective-permute-start(f32[8,128]{1,0:T(8,128)S(1)} %add_add_fusion.1), channel_id=1, source_target_pairs={{0,192},{64,0},{128,64},{192,128},{1,193},{65,1},{129,65},{193,129... | collective-permute-start | bytes 12296 | tf_op jit(solution)/shard_map/ppermute | solution.py:25
  62.4 4.2 %copy-start.4 = (f32[512]{0:T(512)S(1)}, f32[512]{0:T(512)}, u32[]{:S(2)}) copy-start(f32[512]{0:T(512)} %param.7) | copy-start | bytes 6148
  62.4 4.2 %copy-start.5 = (f32[512]{0:T(512)S(1)}, f32[512]{0:T(512)}, u32[]{:S(2)}) copy-start(f32[512]{0:T(512)} %param.6) | copy-start | bytes 6148
  65.5 5.5 %collective-permute-start.14 = (bf16[160,512]{1,0:T(8,128)(2,1)S(1)}, bf16[160,512]{1,0:T(8,128)(2,1)S(1)}, u32[]{:S(2)}, u32[]{:S(2)}) collective-permute-start(bf16[160,512]{1,0:T(8,128)(2,1)S(1)} %bitcast.22), channel_id=1, source_target_pairs={{0,192},{64,0},{128,64},{192,128},{1,193},{65,1},{129,65},{193,129... | collective-permute-start | bytes 491528 | tf_op jit(solution)/shard_map/ppermute | solution.py:25
  72.5 22.6 %all-to-all-start.1 = ((f32[64,8,128]{2,1,0:T(8,128)}), f32[64,8,128]{2,1,0:T(8,128)S(1)}, u32[]{:S(2)}, u32[]{:S(2)}) async-start(f32[64,8,128]{2,1,0:T(8,128)} %broadcast_in_dim.14), calls=%async_computation.1 | async-start | bytes 524288 | tf_op jit(solution)/shard_map/all_to_all | solution.py:357
  83.4 15.1 %collective-permute-start.21 = (f32[4,160,128]{2,1,0:T(8,128)S(1)}, f32[4,160,128]{2,1,0:T(8,128)S(1)}, u32[]{:S(2)}, u32[]{:S(2)}) collective-permute-start(f32[4,160,128]{2,1,0:T(8,128)S(1)} %get-tuple-element.49.part3), channel_id=1, source_target_pairs={{0,64},{64,128},{128,192},{192,0},{1,65},{65,129},{129,193},{193,1... | collective-permute-start | bytes 983048 | tf_op jit(solution)/shard_map/ppermute | solution.py:25
  84.1 17.5 %collective-permute-start.22 = (f32[4,160,128]{2,1,0:T(8,128)S(1)}, f32[4,160,128]{2,1,0:T(8,128)S(1)}, u32[]{:S(2)}, u32[]{:S(2)}) collective-permute-start(f32[4,160,128]{2,1,0:T(8,128)S(1)} %get-tuple-element.48.part2), channel_id=1, source_target_pairs={{0,128},{64,192},{128,0},{192,64},{1,129},{65,193},{129,1},{193,65... | collective-permute-start | bytes 983048 | tf_op jit(solution)/shard_map/ppermute | solution.py:25
  86.7 15.5 %collective-permute-start.23 = (f32[4,160,128]{2,1,0:T(8,128)S(1)}, f32[4,160,128]{2,1,0:T(8,128)S(1)}, u32[]{:S(2)}, u32[]{:S(2)}) collective-permute-start(f32[4,160,128]{2,1,0:T(8,128)S(1)} %get-tuple-element.47.part1), channel_id=1, source_target_pairs={{0,192},{64,0},{128,64},{192,128},{1,193},{65,1},{129,65},{193,129... | collective-permute-start | bytes 983048 | tf_op jit(solution)/shard_map/ppermute | solution.py:25
  95.2 7.0 %collective-permute-start.18 = (f32[8,128]{1,0:T(8,128)S(1)}, f32[8,128]{1,0:T(8,128)S(1)}, u32[]{:S(2)}, u32[]{:S(2)}) collective-permute-start(f32[8,128]{1,0:T(8,128)S(1)} %reduce_sum.99.sum0), channel_id=1, source_target_pairs={{0,64},{64,128},{128,192},{192,0},{1,65},{65,129},{129,193},{193,1... | collective-permute-start | bytes 12296 | tf_op jit(solution)/shard_map/ppermute | solution.py:25
  95.9 6.3 %collective-permute-start.19 = (f32[8,128]{1,0:T(8,128)S(1)}, f32[8,128]{1,0:T(8,128)S(1)}, u32[]{:S(2)}, u32[]{:S(2)}) collective-permute-start(f32[8,128]{1,0:T(8,128)S(1)} %reduce_sum.99.sum0), channel_id=1, source_target_pairs={{0,128},{64,192},{128,0},{192,64},{1,129},{65,193},{129,1},{193,65... | collective-permute-start | bytes 12296 | tf_op jit(solution)/shard_map/ppermute | solution.py:25
  98.5 3.8 %collective-permute-start.20 = (f32[8,128]{1,0:T(8,128)S(1)}, f32[8,128]{1,0:T(8,128)S(1)}, u32[]{:S(2)}, u32[]{:S(2)}) collective-permute-start(f32[8,128]{1,0:T(8,128)S(1)} %reduce_sum.99.sum0), channel_id=1, source_target_pairs={{0,192},{64,0},{128,64},{192,128},{1,193},{65,1},{129,65},{193,129... | collective-permute-start | bytes 12296 | tf_op jit(solution)/shard_map/ppermute | solution.py:25

commit v4 on v3

--- a/solution.py
+++ b/solution.py
@@ -18,6 +18,7 @@
 PLANES = 3 * TAPS
 UNITS = ((0, 1, 2, 3), (0, 1, 2), (0, 1))
 VMEM = pl.BlockSpec(memory_space=pltpu.VMEM)
+HBM = pl.BlockSpec(memory_space=pltpu.HBM)
 
 
 def send(value, axis, step):
@@ -35,8 +36,8 @@
         sums[band, 8 + fine : 16 + fine] = zero
     for k, msg in enumerate((msg0, msg1, msg2, msg3)):
         frame = lax.rem(place + FRAMES - k, FRAMES)
-        upper = msg[0].astype(jnp.float32)
-        lower = msg[1].astype(jnp.float32)
+        upper = msg[0:fine].astype(jnp.float32)
+        lower = msg[fine : 2 * fine].astype(jnp.float32)
         sums[0, 8 : 8 + fine] = lower + high[k].astype(jnp.float32)
         sums[1, 8 : 8 + fine] = upper + lower
         sums[2, 8 : 8 + fine] = low[k].astype(jnp.float32) + upper
@@ -86,37 +87,54 @@
             pltpu.VMEM((FRAMES, TAPS, cells, 128), jnp.float32),
         ],
         compiler_params=pltpu.CompilerParams(vmem_limit_bytes=12 << 20),
-        cost_estimate=pl.CostEstimate(flops=20_000_000, bytes_accessed=9_000_000, transcendentals=0),
+        cost_estimate=pl.CostEstimate(flops=1_000, bytes_accessed=1_000, transcendentals=0),
     )(*msgs, low, high)
 
 
-def split_kernel(cot, out0, out1, out2, out3, sems):
+def split_kernel(cot, lat, out0, out1, out2, out3, sems):
     place = lax.axis_index("x")
+    fine, cells = cot.shape[2], lat.shape[2]
     copies = []
     for k, out in enumerate((out0, out1, out2, out3)):
         first = pl.multiple_of(lax.rem(place + k, FRAMES) * 128, 128)
-        copies.append(pltpu.make_async_copy(cot.at[0, :, :, pl.ds(first, 128)], out, sems.at[k]))
+        moves = [
+            (cot.at[0, row, :, pl.ds(first, 128)], out.at[row * fine : (row + 1) * fine])
+            for row in range(2)
+        ]
+        for q in range(lat.shape[3] // 128):
+            start = 2 * fine + q * cells
+            moves.append((lat.at[0, 0, :, q * 128 : q * 128 + 128], out.at[start : start + cells]))
+        for source, target in moves:
+            copies.append(pltpu.make_async_copy(source, target, sems.at[len(copies)]))
     for copy in copies:
         copy.start()
     for copy in copies:
         copy.wait()
 
 
-def split(cotangent):
-    shape = jax.ShapeDtypeStruct(cotangent.shape[1:3] + (128,), cotangent.dtype)
+def split(cotangent, latent):
+    rows = 2 * cotangent.shape[2] + 4 * latent.shape[2]
     return pl.pallas_call(
         split_kernel,
-        out_shape=[shape] * FRAMES,
-        in_specs=[pl.BlockSpec(memory_space=pl.ANY)],
+        out_shape=[jax.ShapeDtypeStruct((rows, 128), cotangent.dtype)] * FRAMES,
+        in_specs=[HBM] * 2,
         out_specs=[VMEM] * FRAMES,
-        scratch_shapes=[pltpu.SemaphoreType.DMA((FRAMES,))],
+        scratch_shapes=[pltpu.SemaphoreType.DMA((6 * FRAMES,))],
         compiler_params=pltpu.CompilerParams(vmem_limit_bytes=2 << 20),
-        cost_estimate=pl.CostEstimate(flops=0, bytes_accessed=1_300_000, transcendentals=0),
-    )(cotangent)
-
-
-def message_kernel(latent, weight, out, stats):
+        cost_estimate=pl.CostEstimate(flops=0, bytes_accessed=2_600_000, transcendentals=0),
+    )(cotangent, latent)
+
+
+def message_kernel(lat, weight, out, stats, latent, held, sems):
     channels = latent.shape[1]
+    copies = [
+        pltpu.make_async_copy(lat.at[0, 0], latent, sems.at[0]),
+        pltpu.make_async_copy(weight, held, sems.at[1]),
+    ]
+    for copy in copies:
+        copy.start()
+    for copy in copies:
+        copy.wait()
     for q in range(channels // 128):
         values = latent[:, q * 128 : q * 128 + 128].astype(jnp.float32)
         stats[q : q + 1] = jnp.sum(values, axis=0, keepdims=True)
@@ -127,7 +145,7 @@
     middle = rest.astype(jnp.bfloat16)
     last = (rest - middle.astype(jnp.float32)).astype(jnp.bfloat16)
     for z in range(ZS):
-        out[z, 0:PLANES] = weight[...]
+        out[z, 0:PLANES] = held[...]
         out[z, PLANES] = head
         out[z, PLANES + 1] = middle
         out[z, PLANES + 2] = last
@@ -137,9 +155,14 @@
     return pl.pallas_call(
         message_kernel,
         out_shape=jax.ShapeDtypeStruct((ZS, PLANES + 3, 8, 128), jnp.bfloat16),
-        in_specs=[VMEM] * 2,
+        in_specs=[HBM] * 2,
         out_specs=VMEM,
-        scratch_shapes=[pltpu.VMEM((8, 128), jnp.float32)],
+        scratch_shapes=[
+            pltpu.VMEM((8, 128), jnp.float32),
+            pltpu.VMEM(latent.shape[2:], latent.dtype),
+            pltpu.VMEM(weight.shape, weight.dtype),
+            pltpu.SemaphoreType.DMA((2,)),
+        ],
         compiler_params=pltpu.CompilerParams(vmem_limit_bytes=3 << 20),
         cost_estimate=pl.CostEstimate(flops=250_000, bytes_accessed=720_000, transcendentals=0),
     )(latent, weight)
@@ -147,19 +170,20 @@
 
 def rims_kernel(msg0, msg1, msg2, msg3, first, last):
     for k, msg in enumerate((msg0, msg1, msg2, msg3)):
-        first[k] = msg[0]
-        last[k] = msg[1]
-
-
-def rims(msgs):
-    shape = jax.ShapeDtypeStruct((FRAMES,) + msgs[0].shape[1:], jnp.bfloat16)
+        fine = first.shape[1]
+        first[k] = msg[0:fine]
+        last[k] = msg[fine : 2 * fine]
+
+
+def rims(msgs, fine):
+    shape = jax.ShapeDtypeStruct((FRAMES, fine, 128), jnp.bfloat16)
     return pl.pallas_call(
         rims_kernel,
         out_shape=[shape] * 2,
         in_specs=[VMEM] * FRAMES,
         out_specs=[VMEM] * 2,
         compiler_params=pltpu.CompilerParams(vmem_limit_bytes=3 << 20),
-        cost_estimate=pl.CostEstimate(flops=0, bytes_accessed=1_300_000, transcendentals=0),
+        cost_estimate=pl.CostEstimate(flops=0, bytes_accessed=1_000, transcendentals=0),
     )(*msgs)
 
 
@@ -242,39 +266,47 @@
     return normed, sigmoid_pre * (1.0 + pre * (1.0 - sigmoid_pre))
 
 
-def sums_kernel(part0, part1, part2, part3, lat0, lat1, lat2, lat3, chan, out):
-    cells, channels = lat0.shape
-    for q in range(channels // 128):
+def sums_kernel(part0, part1, part2, part3, msg0, msg1, msg2, msg3, chan, out, kept):
+    cells = part0.shape[1]
+    offset = msg0.shape[0] - 4 * cells
+    for q in range(4):
         lanes = slice(q * 128, q * 128 + 128)
         first = jnp.zeros((8, 128), jnp.float32)
         second = jnp.zeros((8, 128), jnp.float32)
-        for part, lat in ((part0, lat0), (part1, lat1), (part2, lat2), (part3, lat3)):
-            normed, gate = slope(lat[:, lanes], chan, lanes)
+        for part, msg in ((part0, msg0), (part1, msg1), (part2, msg2), (part3, msg3)):
+            start = offset + q * cells
+            normed, gate = slope(msg[start : start + cells], chan, lanes)
             act = part[q] * gate
             first = first + act.reshape(cells // 8, 8, 128).sum(axis=0)
             second = second + (act * normed).reshape(cells // 8, 8, 128).sum(axis=0)
-        out[q : q + 1] = jnp.sum(first, axis=0, keepdims=True)
-        out[4 + q : 5 + q] = jnp.sum(second, axis=0, keepdims=True)
-
-
-def partial_sums(parts, lats, chan):
+        kept[q : q + 1] = jnp.sum(first, axis=0, keepdims=True)
+        kept[4 + q : 5 + q] = jnp.sum(second, axis=0, keepdims=True)
+    total = kept[...]
+    for i in range(out.shape[0]):
+        out[i] = total
+
+
+def partial_sums(parts, msgs, chan):
     return pl.pallas_call(
         sums_kernel,
-        out_shape=jax.ShapeDtypeStruct((8, 128), jnp.float32),
+        out_shape=jax.ShapeDtypeStruct((ROWS, 8, 128), jnp.float32),
         in_specs=[VMEM] * 9,
         out_specs=VMEM,
+        scratch_shapes=[pltpu.VMEM((8, 128), jnp.float32)],
         compiler_params=pltpu.CompilerParams(vmem_limit_bytes=4 << 20),
         cost_estimate=pl.CostEstimate(
-            flops=6_000_000, bytes_accessed=2_600_000, transcendentals=330_000
+            flops=6_000_000, bytes_accessed=2_900_000, transcendentals=330_000
         ),
-    )(*parts, *lats, chan)
-
-
-def final_kernel(count, sum0, sum1, sum2, sum3, part0, part1, part2, part3, lat, chan, grad, sums):
+    )(*parts, *msgs, chan)
+
+
+def final_kernel(count, sum0, sum1, sum2, sum3, part0, part1, part2, part3, lat, chan, grad, gain_grad, bias_grad):
     cells, channels = lat.shape
     per_group = channels // GROUPS
     total = (sum0[...] + sum1[...] + (sum2[...] + sum3[...])) / count
-    sums[...] = total
+    for q in range(4):
+        bias_grad[q * 128 : q * 128 + 128] = total[q]
+        gain_grad[q * 128 : q * 128 + 128] = total[4 + q]
     row = lax.broadcasted_iota(jnp.int32, (128, 128), 0) // per_group
     col = lax.broadcasted_iota(jnp.int32, (128, 128), 1) // per_group
     same = jnp.where(row == col, 1.0, 0.0)
@@ -302,10 +334,11 @@
         functools.partial(final_kernel, count),
         out_shape=[
             jax.ShapeDtypeStruct(lat.shape, jnp.float32),
-            jax.ShapeDtypeStruct((8, 128), jnp.float32),
+            jax.ShapeDtypeStruct((lat.shape[1],), jnp.float32),
+            jax.ShapeDtypeStruct((lat.shape[1],), jnp.float32),
         ],
         in_specs=[VMEM] * 10,
-        out_specs=[VMEM] * 2,
+        out_specs=[VMEM] * 3,
         compiler_params=pltpu.CompilerParams(vmem_limit_bytes=4 << 20),
         cost_estimate=pl.CostEstimate(
             flops=2_000_000, bytes_accessed=1_900_000, transcendentals=82_000
@@ -320,19 +353,17 @@
     own = latent[0, 0]
 
     block = lax.all_to_all(
-        message(own, conv_weight.reshape(PLANES, 8, 128)), "z", 0, 0, tiled=True
+        message(latent, conv_weight.reshape(PLANES, 8, 128)), "z", 0, 0, tiled=True
     )
+    pieces = [block] + [send(block, "y", step) for step in range(1, YS)]
 
     msgs = [
-        msg if step == 0 else send(msg, "x", step) for step, msg in enumerate(split(cotangent))
+        msg if step == 0 else send(msg, "x", step)
+        for step, msg in enumerate(split(cotangent, latent))
     ]
-    block, msgs = lax.optimization_barrier((block, msgs))
-    pieces = [block] + [send(block, "y", step) for step in range(1, YS)]
-    first, last = rims(msgs)
+    first, last = rims(msgs, cotangent.shape[2])
     low = lax.ppermute(last, ROW_AXES, [(i, i + 1) for i in range(ROWS - 1)])
     high = lax.ppermute(first, ROW_AXES, [(i + 1, i) for i in range(ROWS - 1)])
-    late, _ = lax.optimization_barrier((own, first))
-    lats = [own] + [send(late, "x", step) for step in range(1, FRAMES)]
     lefts = pool(msgs, low, high)
     others = [send(piece, "c", 1) for piece in pieces]
     partial = None
@@ -352,14 +383,11 @@
         [jnp.repeat(group_mean, per_group), jnp.repeat(inv_std, per_group), norm_gain, norm_bias]
     )
 
-    sums = partial_sums(partial, lats, chan)
+    sums = partial_sums(partial, msgs, chan)
     parts = [partial[0]] + [send(partial[FRAMES - step], "x", step) for step in range(1, FRAMES)]
-    sums = lax.all_to_all(
-        jnp.broadcast_to(sums[None], (ROWS, 8, 128)), ROW_AXES, 0, 0, tiled=True
-    ).sum(axis=0)
+    sums = lax.all_to_all(sums, ROW_AXES, 0, 0, tiled=True).sum(axis=0)
     sums = [sums] + [send(sums, "x", step) for step in range(1, FRAMES)]
-    latent_grad, chan_grad = final(cell_count, sums, parts, own, chan)
-    bias_grad, gain_grad = chan_grad.reshape(2, channels)
+    latent_grad, gain_grad, bias_grad = final(cell_count, sums, parts, own, chan)
     return (latent_grad.reshape(1, 1, cells, channels), gain_grad, bias_grad)
 
 

time: 105 us -> 102 us (0.971)
  waiting for transfers between devices: 34.1 us -> 31 us
  Pallas kernels: 10.6 us -> 11.9 us
    ppermute x22 -> x19, waiting for transfers between devices: 22.5 us -> 14.7 us  [send(): lax.ppermute(value, axis, [(i, (i + step) % size) for i in range(size)])]
    all_to_all x2, waiting for transfers between devices: 9.94 us -> 15 us  [the longest x1 7.91 us: on_device(): sums = lax.all_to_all(sums, ROW_AXES, 0, 0, tiled=True).sum(axis=0)]
    ppermute x22 -> x19, starting transfers between devices: 29.7 us -> 28.2 us  [send(): lax.ppermute(value, axis, [(i, (i + step) % size) for i in range(size)])]
    ppermute x1, starting transfers between devices: 2.43 us -> 3.64 us  [on_device(): high = lax.ppermute(first, ROW_AXES, [(i + 1, i) for i in range(ROWS - 1)])]
    unnamed x12 -> x14, local copies, waits for them, and re-layouts: 2.83 us -> 3.75 us
  transfers between devices with their start and end apart: 26 -> 23, of which waited for: 11 -> 10; matrix products, arithmetic and copies ran while one was open for 1% -> 0% of each run, Pallas kernels for 8% -> 8%
where the time goes in v4:
time: 102 us; the launch traced here: 101 us
  starting transfers between devices  52.7 us (52%)
  waiting for transfers between devices  31 us (30%)
  Pallas kernels  11.9 us (12%)
  local copies, waits for them, and re-layouts  4.13 us (4%)
    ppermute x19, starting transfers between devices, send(): lax.ppermute(value, axis, [(i, (i + step) % size) for i in range(size)])  28.2 us
    ppermute x19, waiting for transfers between devices, send(): lax.ppermute(value, axis, [(i, (i + step) % size) for i in range(size)])  14.7 us
    all_to_all x1, starting transfers between devices, on_device(): sums = lax.all_to_all(sums, ROW_AXES, 0, 0, tiled=True).sum(axis=0)  10.4 us
    all_to_all x1, starting transfers between devices, on_device(): lax.all_to_all(message(latent, conv_weight.reshape(PLANES, 8, 128)), 'z',...  8.58 us
    all_to_all x1, waiting for transfers between devices, on_device(): sums = lax.all_to_all(sums, ROW_AXES, 0, 0, tiled=True).sum(axis=0)  7.91 us
    all_to_all x1, waiting for transfers between devices, on_device(): lax.all_to_all(message(latent, conv_weight.reshape(PLANES, 8, 128)), 'z',...  7.1 us
    pallas_call x2, Pallas kernels, product(): pl.pallas_call(functools.partial(product_kernel, steps, aliased), out_sha...  6.15 us
    unnamed x14, local copies, waits for them, and re-layouts  3.75 us
  transfers between devices with their start and end apart: 23, of which 10 were waited for; matrix products, arithmetic and copies ran while one was open for 0% of the time, Pallas kernels for 8%

profile of v4, /device:TPU:32, one launch (start us, length us, event | category | flops | bytes accessed | tf_op | source)
XLA Modules:
  0.0 101.0 jit_solution(17356773332878958338)
XLA Ops:
  2.4 1.2 %shard_map.76 = bf16[8,30,8,128]{3,2,1,0:T(8,128)(2,1)} custom-call(bf16[1,1,160,512]{3,2,1,0:T(8,128)(2,1)S(1)} %copy-done, bf16[27,8,128]{2,1,0:T(8,128)(2,1)S(1)} %bitcast.16), custom_call_target="tpu_custom_call" | custom-call | flops 250000 | bytes 720000 | tf_op jit(solution)/shard_map/pallas_call | solution.py:155
  3.5 8.6 %all-to-all-start = ((bf16[8,30,8,128]{3,2,1,0:T(8,128)(2,1)}), bf16[8,30,8,128]{3,2,1,0:T(8,128)(2,1)S(1)}, u32[]{:S(2)}, u32[]{:S(2)}) async-start(bf16[8,30,8,128]{3,2,1,0:T(8,128)(2,1)} %shard_map.76), calls=%async_computation | async-start | bytes 983040 | tf_op jit(solution)/shard_map/all_to_all | solution.py:355
  13.0 1.1 %copy-done.3 = bf16[1,2,320,512]{3,2,1,0:T(8,128)(2,1)S(1)} copy-done((bf16[1,2,320,512]{3,2,1,0:T(8,128)(2,1)S(1)}, bf16[1,2,320,512]{3,2,1,0:T(8,128)(2,1)}, u32[]{:S(2)}) %copy-start.3) | copy-done | bytes 655384
  14.6 1.6 %collective-permute-start.4 = (bf16[1280,128]{1,0:T(8,128)(2,1)S(1)}, bf16[1280,128]{1,0:T(8,128)(2,1)S(1)}, u32[]{:S(2)}, u32[]{:S(2)}) collective-permute-start(bf16[1280,128]{1,0:T(8,128)(2,1)S(1)} %get-tuple-element.24), channel_id=1, source_target_pairs={{0,64},{64,128},{128,192},{192,0},{1,65},{65,129},{129,193},{193,1... | collective-permute-start | bytes 983048 | tf_op jit(solution)/shard_map/ppermute | solution.py:26
  16.2 2.7 %collective-permute-start.5 = (bf16[1280,128]{1,0:T(8,128)(2,1)S(1)}, bf16[1280,128]{1,0:T(8,128)(2,1)S(1)}, u32[]{:S(2)}, u32[]{:S(2)}) collective-permute-start(bf16[1280,128]{1,0:T(8,128)(2,1)S(1)} %get-tuple-element.25), channel_id=1, source_target_pairs={{0,128},{64,192},{128,0},{192,64},{1,129},{65,193},{129,1},{193,65... | collective-permute-start | bytes 983048 | tf_op jit(solution)/shard_map/ppermute | solution.py:26
  18.9 1.4 %collective-permute-start.6 = (bf16[1280,128]{1,0:T(8,128)(2,1)S(1)}, bf16[1280,128]{1,0:T(8,128)(2,1)S(1)}, u32[]{:S(2)}, u32[]{:S(2)}) collective-permute-start(bf16[1280,128]{1,0:T(8,128)(2,1)S(1)} %get-tuple-element.26), channel_id=1, source_target_pairs={{0,192},{64,0},{128,64},{192,128},{1,193},{65,1},{129,65},{193,129... | collective-permute-start | bytes 983048 | tf_op jit(solution)/shard_map/ppermute | solution.py:26
  20.3 7.1 %all-to-all-done.refs_0_ = bf16[8,30,8,128]{3,2,1,0:T(8,128)(2,1)S(1)} async-done(((bf16[8,30,8,128]{3,2,1,0:T(8,128)(2,1)}), bf16[8,30,8,128]{3,2,1,0:T(8,128)(2,1)S(1)}, u32[]{:S(2)}, u32[]{:S(2)}) %all-to-all-start) | async-done | bytes 491552 | tf_op jit(solution)/shard_map/all_to_all | solution.py:355
  27.4 3.0 %collective-permute-start.10 = (bf16[8,30,8,128]{3,2,1,0:T(8,128)(2,1)S(1)}, bf16[8,30,8,128]{3,2,1,0:T(8,128)(2,1)S(1)}, u32[]{:S(2)}, u32[]{:S(2)}) collective-permute-start(bf16[8,30,8,128]{3,2,1,0:T(8,128)(2,1)S(1)} %all-to-all-done.refs_0_), channel_id=1, source_target_pairs={{0,48},{16,0},{32,16},{48,32},{1,49},{17,1},{33,17},{49,33},{2,50}... | collective-permute-start | bytes 1474568 | tf_op jit(solution)/shard_map/ppermute | solution.py:26
  30.5 2.3 %collective-permute-done.5.msg2 = bf16[1280,128]{1,0:T(8,128)(2,1)S(1)} collective-permute-done((bf16[1280,128]{1,0:T(8,128)(2,1)S(1)}, bf16[1280,128]{1,0:T(8,128)(2,1)S(1)}, u32[]{:S(2)}, u32[]{:S(2)}) %collective-permute-start.5) | collective-permute-done | bytes 327712 | tf_op jit(solution)/shard_map/ppermute | solution.py:26
  32.9 1.9 %collective-permute-start.7 = (bf16[4,320,128]{2,1,0:T(8,128)(2,1)S(1)}, bf16[4,320,128]{2,1,0:T(8,128)(2,1)S(1)}, u32[]{:S(2)}, u32[]{:S(2)}) collective-permute-start(bf16[4,320,128]{2,1,0:T(8,128)(2,1)S(1)} %get-tuple-element.27), channel_id=1, source_target_pairs={{0,1},{1,2},{2,3},{3,4},{4,5},{5,6},{6,7},{7,8},{8,9},{9,10},{10,1... | collective-permute-start | bytes 983048 | tf_op jit(solution)/shard_map/ppermute | solution.py:365
  34.8 3.6 %collective-permute-start.8 = (bf16[4,320,128]{2,1,0:T(8,128)(2,1)S(1)}, bf16[4,320,128]{2,1,0:T(8,128)(2,1)S(1)}, u32[]{:S(2)}, u32[]{:S(2)}) collective-permute-start(bf16[4,320,128]{2,1,0:T(8,128)(2,1)S(1)} %get-tuple-element.28), channel_id=1, source_target_pairs={{1,0},{2,1},{3,2},{4,3},{5,4},{6,5},{7,6},{8,7},{9,8},{10,9},{11,1... | collective-permute-start | bytes 983048 | tf_op jit(solution)/shard_map/ppermute | solution.py:366
  38.4 3.3 %collective-permute-start = (bf16[8,30,8,128]{3,2,1,0:T(8,128)(2,1)S(1)}, bf16[8,30,8,128]{3,2,1,0:T(8,128)(2,1)S(1)}, u32[]{:S(2)}, u32[]{:S(2)}) collective-permute-start(bf16[8,30,8,128]{3,2,1,0:T(8,128)(2,1)S(1)} %all-to-all-done.refs_0_), channel_id=1, source_target_pairs={{0,32},{16,48},{32,0},{48,16},{1,33},{17,49},{33,1},{49,17},{2,34}... | collective-permute-start | bytes 1474568 | tf_op jit(solution)/shard_map/ppermute | solution.py:26
  41.7 1.3 %collective-permute-done.8.high = bf16[4,320,128]{2,1,0:T(8,128)(2,1)S(1)} collective-permute-done((bf16[4,320,128]{2,1,0:T(8,128)(2,1)S(1)}, bf16[4,320,128]{2,1,0:T(8,128)(2,1)S(1)}, u32[]{:S(2)}, u32[]{:S(2)}) %collective-permute-start.8) | collective-permute-done | bytes 327712 | tf_op jit(solution)/shard_map/ppermute | solution.py:366
  43.0 1.5 %shard_map.79 = (bf16[2,640,1152]{2,1,0:T(8,128)(2,1)S(1)}, bf16[2,480,1152]{2,1,0:T(8,128)(2,1)S(1)}, bf16[2,320,1152]{2,1,0:T(8,128)(2,1)S(1)}) custom-call(bf16[1280,128]{1,0:T(8,128)(2,1)S(1)} %get-tuple-element.23.msg0, bf16[1280,128]{1,0:T(8,128)(2,1)S(1)} %collective-permute-done.4.msg1, bf16[1280,128]{1,0:T(8,128)(2,1)S(1)} %collective-permute-done.5.msg2, ...), custom_call_target="tpu_custom_call" | custom-call | flops 1000 | bytes 1000 | tf_op jit(solution)/shard_map/pallas_call | solution.py:80
  44.5 2.1 %collective-permute-start.11 = (bf16[8,30,8,128]{3,2,1,0:T(8,128)(2,1)S(1)}, bf16[8,30,8,128]{3,2,1,0:T(8,128)(2,1)S(1)}, u32[]{:S(2)}, u32[]{:S(2)}) collective-permute-start(bf16[8,30,8,128]{3,2,1,0:T(8,128)(2,1)S(1)} %collective-permute-done.10.refs_2_), channel_id=1, source_target_pairs={{0,1},{1,0},{2,3},{3,2},{4,5},{5,4},{6,7},{7,6},{8,9},{9,8},{10,11... | collective-permute-start | bytes 1474568 | tf_op jit(solution)/shard_map/ppermute | solution.py:26
  46.8 6.2 %collective-permute-done.refs_0_ = bf16[8,30,8,128]{3,2,1,0:T(8,128)(2,1)S(1)} collective-permute-done((bf16[8,30,8,128]{3,2,1,0:T(8,128)(2,1)S(1)}, bf16[8,30,8,128]{3,2,1,0:T(8,128)(2,1)S(1)}, u32[]{:S(2)}, u32[]{:S(2)}) %collective-permute-start) | collective-permute-done | bytes 491552 | tf_op jit(solution)/shard_map/ppermute | solution.py:26
  53.2 1.7 %collective-permute-done.1.refs_1_ = bf16[8,30,8,128]{3,2,1,0:T(8,128)(2,1)S(1)} collective-permute-done((bf16[8,30,8,128]{3,2,1,0:T(8,128)(2,1)S(1)}, bf16[8,30,8,128]{3,2,1,0:T(8,128)(2,1)S(1)}, u32[]{:S(2)}, u32[]{:S(2)}) %collective-permute-start.1) | collective-permute-done | bytes 491552 | tf_op jit(solution)/shard_map/ppermute | solution.py:26
  54.9 2.3 %collective-permute-start.14 = (f32[8,128]{1,0:T(8,128)S(1)}, f32[8,128]{1,0:T(8,128)S(1)}, u32[]{:S(2)}, u32[]{:S(2)}) collective-permute-start(f32[8,128]{1,0:T(8,128)S(1)} %add_add_fusion.1), channel_id=1, source_target_pairs={{0,192},{64,0},{128,64},{192,128},{1,193},{65,1},{129,65},{193,129... | collective-permute-start | bytes 12296 | tf_op jit(solution)/shard_map/ppermute | solution.py:26
  57.2 1.1 %collective-permute-start.13 = (f32[8,128]{1,0:T(8,128)S(1)}, f32[8,128]{1,0:T(8,128)S(1)}, u32[]{:S(2)}, u32[]{:S(2)}) collective-permute-start(f32[8,128]{1,0:T(8,128)S(1)} %add_add_fusion.1), channel_id=1, source_target_pairs={{0,128},{64,192},{128,0},{192,64},{1,129},{65,193},{129,1},{193,65... | collective-permute-start | bytes 12296 | tf_op jit(solution)/shard_map/ppermute | solution.py:26
  59.1 3.1 %shard_map.80 = (f32[4,160,128]{2,1,0:T(8,128)S(1)}, f32[4,160,128]{2,1,0:T(8,128)S(1)}, f32[4,160,128]{2,1,0:T(8,128)S(1)}, f32[4,160,128]{2,1,0:T(8,128)S(1)}) custom-call(bf16[8,30,8,128]{3,2,1,0:T(8,128)(2,1)S(1)} %all-to-all-done.refs_0_, bf16[8,30,8,128]{3,2,1,0:T(8,128)(2,1)S(1)} %collective-permute-done.9.refs_1_, ...), custom_call_target="tpu_custom_call" | custom-call | flops 1700000000 | bytes 9000000 | tf_op jit(solution)/shard_map/pallas_call | solution.py:242
  62.2 3.1 %shard_map.81 = (f32[4,160,128]{2,1,0:T(8,128)S(1)}, f32[4,160,128]{2,1,0:T(8,128)S(1)}, f32[4,160,128]{2,1,0:T(8,128)S(1)}, f32[4,160,128]{2,1,0:T(8,128)S(1)}) custom-call(bf16[8,30,8,128]{3,2,1,0:T(8,128)(2,1)S(1)} %collective-permute-done.refs_0_, ...), custom_call_target="tpu_custom_call", output_to_operand_aliasing={{0}: (7, {}), {1}: (8, {}), {2}: (9, {}), {3}: (10, {})} | custom-call | flops 1700000000 | bytes 9000000 | tf_op jit(solution)/shard_map/pallas_call | solution.py:242
  65.8 1.5 %shard_map.82 = f32[64,8,128]{2,1,0:T(8,128)} custom-call(f32[4,160,128]{2,1,0:T(8,128)S(1)} %get-tuple-element.36.part0, f32[4,160,128]{2,1,0:T(8,128)S(1)} %get-tuple-element.37.part1, f32[4,160,128]{2,1,0:T(8,128)S(1)} %get-tuple-element.38.part2, f32[4,160,128]{2,1,0:T(8,128)S(1)} %get-tuple-element.39.part3, ...), custom_call_target="tpu_custom_call" | custom-call | flops 6000000 | bytes 2900000 | tf_op jit(solution)/shard_map/pallas_call | solution.py:290
  67.4 10.4 %all-to-all-start.1 = ((f32[64,8,128]{2,1,0:T(8,128)}), f32[64,8,128]{2,1,0:T(8,128)S(1)}, u32[]{:S(2)}, u32[]{:S(2)}) async-start(f32[64,8,128]{2,1,0:T(8,128)} %shard_map.82), calls=%async_computation.1 | async-start | bytes 524288 | tf_op jit(solution)/shard_map/all_to_all | solution.py:388
  77.8 2.4 %collective-permute-start.20 = (f32[4,160,128]{2,1,0:T(8,128)S(1)}, f32[4,160,128]{2,1,0:T(8,128)S(1)}, u32[]{:S(2)}, u32[]{:S(2)}) collective-permute-start(f32[4,160,128]{2,1,0:T(8,128)S(1)} %get-tuple-element.37.part1), channel_id=1, source_target_pairs={{0,192},{64,0},{128,64},{192,128},{1,193},{65,1},{129,65},{193,129... | collective-permute-start | bytes 983048 | tf_op jit(solution)/shard_map/ppermute | solution.py:26
  80.2 1.5 %collective-permute-start.19 = (f32[4,160,128]{2,1,0:T(8,128)S(1)}, f32[4,160,128]{2,1,0:T(8,128)S(1)}, u32[]{:S(2)}, u32[]{:S(2)}) collective-permute-start(f32[4,160,128]{2,1,0:T(8,128)S(1)} %get-tuple-element.38.part2), channel_id=1, source_target_pairs={{0,128},{64,192},{128,0},{192,64},{1,129},{65,193},{129,1},{193,65... | collective-permute-start | bytes 983048 | tf_op jit(solution)/shard_map/ppermute | solution.py:26
  81.8 7.9 %all-to-all-done.1 = f32[64,8,128]{2,1,0:T(8,128)S(1)} async-done(((f32[64,8,128]{2,1,0:T(8,128)}), f32[64,8,128]{2,1,0:T(8,128)S(1)}, u32[]{:S(2)}, u32[]{:S(2)}) %all-to-all-start.1) | async-done | bytes 262176 | tf_op jit(solution)/shard_map/all_to_all | solution.py:388
  89.7 2.4 %collective-permute-start.17 = (f32[8,128]{1,0:T(8,128)S(1)}, f32[8,128]{1,0:T(8,128)S(1)}, u32[]{:S(2)}, u32[]{:S(2)}) collective-permute-start(f32[8,128]{1,0:T(8,128)S(1)} %reduce_sum.99.sum0), channel_id=1, source_target_pairs={{0,192},{64,0},{128,64},{192,128},{1,193},{65,1},{129,65},{193,129... | collective-permute-start | bytes 12296 | tf_op jit(solution)/shard_map/ppermute | solution.py:26
  92.2 1.5 %collective-permute-start.16 = (f32[8,128]{1,0:T(8,128)S(1)}, f32[8,128]{1,0:T(8,128)S(1)}, u32[]{:S(2)}, u32[]{:S(2)}) collective-permute-start(f32[8,128]{1,0:T(8,128)S(1)} %reduce_sum.99.sum0), channel_id=1, source_target_pairs={{0,128},{64,192},{128,0},{192,64},{1,129},{65,193},{129,1},{193,65... | collective-permute-start | bytes 12296 | tf_op jit(solution)/shard_map/ppermute | solution.py:26
  94.7 1.9 %collective-permute-start.15 = (f32[8,128]{1,0:T(8,128)S(1)}, f32[8,128]{1,0:T(8,128)S(1)}, u32[]{:S(2)}, u32[]{:S(2)}) collective-permute-start(f32[8,128]{1,0:T(8,128)S(1)} %reduce_sum.99.sum0), channel_id=1, source_target_pairs={{0,64},{64,128},{128,192},{192,0},{1,65},{65,129},{129,193},{193,1... | collective-permute-start | bytes 12296 | tf_op jit(solution)/shard_map/ppermute | solution.py:26
  96.6 1.8 %collective-permute-done.18.part1 = f32[4,160,128]{2,1,0:T(8,128)S(1)} collective-permute-done((f32[4,160,128]{2,1,0:T(8,128)S(1)}, f32[4,160,128]{2,1,0:T(8,128)S(1)}, u32[]{:S(2)}, u32[]{:S(2)}) %collective-permute-start.18) | collective-permute-done | bytes 327712 | tf_op jit(solution)/shard_map/ppermute | solution.py:26
  98.4 1.5 %collective-permute-done.15.sum1 = f32[8,128]{1,0:T(8,128)S(1)} collective-permute-done((f32[8,128]{1,0:T(8,128)S(1)}, f32[8,128]{1,0:T(8,128)S(1)}, u32[]{:S(2)}, u32[]{:S(2)}) %collective-permute-start.15) | collective-permute-done | bytes 4128 | tf_op jit(solution)/shard_map/ppermute | solution.py:26
  100.0 1.1 %shard_map.83 = (f32[160,512]{1,0:T(8,128)}, f32[512]{0:T(512)}, f32[512]{0:T(512)}) custom-call(f32[8,128]{1,0:T(8,128)S(1)} %reduce_sum.99.sum0, f32[8,128]{1,0:T(8,128)S(1)} %collective-permute-done.15.sum1, f32[8,128]{1,0:T(8,128)S(1)} %collective-permute-done.16.sum2, f32[8,128]{1,0:T(8,128)S(1)} %collective-permute-done.17.sum3, ...), custom_call_target="tpu_custom_call" | custom-call | flops 2000000 | bytes 1900000 | tf_op jit(solution)/shard_map/pallas_call | solution.py:333
  (57 shorter events, 5.9 us)
Async XLA Ops:
  0.6 0.9 copy-start
  1.5 0.8 copy-start.4
  3.5 23.9 %all-to-all-start = ((bf16[8,30,8,128]{3,2,1,0:T(8,128)(2,1)}), bf16[8,30,8,128]{3,2,1,0:T(8,128)(2,1)S(1)}, u32[]{:S(2)}, u32[]{:S(2)}) async-start(bf16[8,30,8,128]{3,2,1,0:T(8,128)(2,1)} %shard_map.76), calls=%async_computation | async-start | bytes 983040 | tf_op jit(solution)/shard_map/all_to_all | solution.py:355
  12.1 0.9 copy-start.1
  13.0 1.1 %copy-start.3 = (bf16[1,2,320,512]{3,2,1,0:T(8,128)(2,1)S(1)}, bf16[1,2,320,512]{3,2,1,0:T(8,128)(2,1)}, u32[]{:S(2)}) copy-start(bf16[1,2,320,512]{3,2,1,0:T(8,128)(2,1)} %cot.1) | copy-start | bytes 1966084
  14.6 15.9 %collective-permute-start.4 = (bf16[1280,128]{1,0:T(8,128)(2,1)S(1)}, bf16[1280,128]{1,0:T(8,128)(2,1)S(1)}, u32[]{:S(2)}, u32[]{:S(2)}) collective-permute-start(bf16[1280,128]{1,0:T(8,128)(2,1)S(1)} %get-tuple-element.24), channel_id=1, source_target_pairs={{0,64},{64,128},{128,192},{192,0},{1,65},{65,129},{129,193},{193,1... | collective-permute-start | bytes 983048 | tf_op jit(solution)/shard_map/ppermute | solution.py:26
  16.2 16.6 %collective-permute-start.5 = (bf16[1280,128]{1,0:T(8,128)(2,1)S(1)}, bf16[1280,128]{1,0:T(8,128)(2,1)S(1)}, u32[]{:S(2)}, u32[]{:S(2)}) collective-permute-start(bf16[1280,128]{1,0:T(8,128)(2,1)S(1)} %get-tuple-element.25), channel_id=1, source_target_pairs={{0,128},{64,192},{128,0},{192,64},{1,129},{65,193},{129,1},{193,65... | collective-permute-start | bytes 983048 | tf_op jit(solution)/shard_map/ppermute | solution.py:26
  18.9 13.9 %collective-permute-start.6 = (bf16[1280,128]{1,0:T(8,128)(2,1)S(1)}, bf16[1280,128]{1,0:T(8,128)(2,1)S(1)}, u32[]{:S(2)}, u32[]{:S(2)}) collective-permute-start(bf16[1280,128]{1,0:T(8,128)(2,1)S(1)} %get-tuple-element.26), channel_id=1, source_target_pairs={{0,192},{64,0},{128,64},{192,128},{1,193},{65,1},{129,65},{193,129... | collective-permute-start | bytes 983048 | tf_op jit(solution)/shard_map/ppermute | solution.py:26
  27.4 17.0 %collective-permute-start.10 = (bf16[8,30,8,128]{3,2,1,0:T(8,128)(2,1)S(1)}, bf16[8,30,8,128]{3,2,1,0:T(8,128)(2,1)S(1)}, u32[]{:S(2)}, u32[]{:S(2)}) collective-permute-start(bf16[8,30,8,128]{3,2,1,0:T(8,128)(2,1)S(1)} %all-to-all-done.refs_0_), channel_id=1, source_target_pairs={{0,48},{16,0},{32,16},{48,32},{1,49},{17,1},{33,17},{49,33},{2,50}... | collective-permute-start | bytes 1474568 | tf_op jit(solution)/shard_map/ppermute | solution.py:26
  30.5 16.2 %collective-permute-start.2 = (bf16[8,30,8,128]{3,2,1,0:T(8,128)(2,1)S(1)}, bf16[8,30,8,128]{3,2,1,0:T(8,128)(2,1)S(1)}, u32[]{:S(2)}, u32[]{:S(2)}) collective-permute-start(bf16[8,30,8,128]{3,2,1,0:T(8,128)(2,1)S(1)} %all-to-all-done.refs_0_), channel_id=1, source_target_pairs={{0,16},{16,32},{32,48},{48,0},{1,17},{17,33},{33,49},{49,1},{2,18}... | collective-permute-start | bytes 1474568 | tf_op jit(solution)/shard_map/ppermute | solution.py:26
  32.9 8.9 %collective-permute-start.7 = (bf16[4,320,128]{2,1,0:T(8,128)(2,1)S(1)}, bf16[4,320,128]{2,1,0:T(8,128)(2,1)S(1)}, u32[]{:S(2)}, u32[]{:S(2)}) collective-permute-start(bf16[4,320,128]{2,1,0:T(8,128)(2,1)S(1)} %get-tuple-element.27), channel_id=1, source_target_pairs={{0,1},{1,2},{2,3},{3,4},{4,5},{5,6},{6,7},{7,8},{8,9},{9,10},{10,1... | collective-permute-start | bytes 983048 | tf_op jit(solution)/shard_map/ppermute | solution.py:365
  34.8 8.2 %collective-permute-start.8 = (bf16[4,320,128]{2,1,0:T(8,128)(2,1)S(1)}, bf16[4,320,128]{2,1,0:T(8,128)(2,1)S(1)}, u32[]{:S(2)}, u32[]{:S(2)}) collective-permute-start(bf16[4,320,128]{2,1,0:T(8,128)(2,1)S(1)} %get-tuple-element.28), channel_id=1, source_target_pairs={{1,0},{2,1},{3,2},{4,3},{5,4},{6,5},{7,6},{8,7},{9,8},{10,9},{11,1... | collective-permute-start | bytes 983048 | tf_op jit(solution)/shard_map/ppermute | solution.py:366
  38.4 14.6 %collective-permute-start = (bf16[8,30,8,128]{3,2,1,0:T(8,128)(2,1)S(1)}, bf16[8,30,8,128]{3,2,1,0:T(8,128)(2,1)S(1)}, u32[]{:S(2)}, u32[]{:S(2)}) collective-permute-start(bf16[8,30,8,128]{3,2,1,0:T(8,128)(2,1)S(1)} %all-to-all-done.refs_0_), channel_id=1, source_target_pairs={{0,32},{16,48},{32,0},{48,16},{1,33},{17,49},{33,1},{49,17},{2,34}... | collective-permute-start | bytes 1474568 | tf_op jit(solution)/shard_map/ppermute | solution.py:26
  41.7 11.3 %collective-permute-start.9 = (bf16[8,30,8,128]{3,2,1,0:T(8,128)(2,1)S(1)}, bf16[8,30,8,128]{3,2,1,0:T(8,128)(2,1)S(1)}, u32[]{:S(2)}, u32[]{:S(2)}) collective-permute-start(bf16[8,30,8,128]{3,2,1,0:T(8,128)(2,1)S(1)} %all-to-all-done.refs_0_), channel_id=1, source_target_pairs={{0,1},{1,0},{2,3},{3,2},{4,5},{5,4},{6,7},{7,6},{8,9},{9,8},{10,11... | collective-permute-start | bytes 1474568 | tf_op jit(solution)/shard_map/ppermute | solution.py:26
  44.5 8.6 %collective-permute-start.11 = (bf16[8,30,8,128]{3,2,1,0:T(8,128)(2,1)S(1)}, bf16[8,30,8,128]{3,2,1,0:T(8,128)(2,1)S(1)}, u32[]{:S(2)}, u32[]{:S(2)}) collective-permute-start(bf16[8,30,8,128]{3,2,1,0:T(8,128)(2,1)S(1)} %collective-permute-done.10.refs_2_), channel_id=1, source_target_pairs={{0,1},{1,0},{2,3},{3,2},{4,5},{5,4},{6,7},{7,6},{8,9},{9,8},{10,11... | collective-permute-start | bytes 1474568 | tf_op jit(solution)/shard_map/ppermute | solution.py:26
  46.6 6.5 %collective-permute-start.3 = (bf16[8,30,8,128]{3,2,1,0:T(8,128)(2,1)S(1)}, bf16[8,30,8,128]{3,2,1,0:T(8,128)(2,1)S(1)}, u32[]{:S(2)}, u32[]{:S(2)}) collective-permute-start(bf16[8,30,8,128]{3,2,1,0:T(8,128)(2,1)S(1)} %collective-permute-done.2.refs_2_), channel_id=1, source_target_pairs={{0,1},{1,0},{2,3},{3,2},{4,5},{5,4},{6,7},{7,6},{8,9},{9,8},{10,11... | collective-permute-start | bytes 1474568 | tf_op jit(solution)/shard_map/ppermute | solution.py:26
  53.0 1.9 %collective-permute-start.1 = (bf16[8,30,8,128]{3,2,1,0:T(8,128)(2,1)S(1)}, bf16[8,30,8,128]{3,2,1,0:T(8,128)(2,1)S(1)}, u32[]{:S(2)}, u32[]{:S(2)}) collective-permute-start(bf16[8,30,8,128]{3,2,1,0:T(8,128)(2,1)S(1)} %collective-permute-done.refs_0_), channel_id=1, source_target_pairs={{0,1},{1,0},{2,3},{3,2},{4,5},{5,4},{6,7},{7,6},{8,9},{9,8},{10,11... | collective-permute-start | bytes 1474568 | tf_op jit(solution)/shard_map/ppermute | solution.py:26
  54.9 10.4 %collective-permute-start.14 = (f32[8,128]{1,0:T(8,128)S(1)}, f32[8,128]{1,0:T(8,128)S(1)}, u32[]{:S(2)}, u32[]{:S(2)}) collective-permute-start(f32[8,128]{1,0:T(8,128)S(1)} %add_add_fusion.1), channel_id=1, source_target_pairs={{0,192},{64,0},{128,64},{192,128},{1,193},{65,1},{129,65},{193,129... | collective-permute-start | bytes 12296 | tf_op jit(solution)/shard_map/ppermute | solution.py:26
  57.2 8.0 %collective-permute-start.13 = (f32[8,128]{1,0:T(8,128)S(1)}, f32[8,128]{1,0:T(8,128)S(1)}, u32[]{:S(2)}, u32[]{:S(2)}) collective-permute-start(f32[8,128]{1,0:T(8,128)S(1)} %add_add_fusion.1), channel_id=1, source_target_pairs={{0,128},{64,192},{128,0},{192,64},{1,129},{65,193},{129,1},{193,65... | collective-permute-start | bytes 12296 | tf_op jit(solution)/shard_map/ppermute | solution.py:26
  58.4 6.9 %collective-permute-start.12 = (f32[8,128]{1,0:T(8,128)S(1)}, f32[8,128]{1,0:T(8,128)S(1)}, u32[]{:S(2)}, u32[]{:S(2)}) collective-permute-start(f32[8,128]{1,0:T(8,128)S(1)} %add_add_fusion.1), channel_id=1, source_target_pairs={{0,64},{64,128},{128,192},{192,0},{1,65},{65,129},{129,193},{193,1... | collective-permute-start | bytes 12296 | tf_op jit(solution)/shard_map/ppermute | solution.py:26
  62.1 3.7 %copy-start.5 = (f32[512]{0:T(512)S(1)}, f32[512]{0:T(512)}, u32[]{:S(2)}) copy-start(f32[512]{0:T(512)} %param.7) | copy-start | bytes 6148
  62.1 3.7 %copy-start.6 = (f32[512]{0:T(512)S(1)}, f32[512]{0:T(512)}, u32[]{:S(2)}) copy-start(f32[512]{0:T(512)} %param.6) | copy-start | bytes 6148
  65.2 34.7 %copy-start.2 = (bf16[1,1,160,512]{3,2,1,0:T(8,128)(2,1)S(1)}, bf16[1,1,160,512]{3,2,1,0:T(8,128)(2,1)}, u32[]{:S(2)}) copy-start(bf16[1,1,160,512]{3,2,1,0:T(8,128)(2,1)} %lat.3) | copy-start | bytes 491524
  67.4 22.3 %all-to-all-start.1 = ((f32[64,8,128]{2,1,0:T(8,128)}), f32[64,8,128]{2,1,0:T(8,128)S(1)}, u32[]{:S(2)}, u32[]{:S(2)}) async-start(f32[64,8,128]{2,1,0:T(8,128)} %shard_map.82), calls=%async_computation.1 | async-start | bytes 524288 | tf_op jit(solution)/shard_map/all_to_all | solution.py:388
  77.8 16.9 %collective-permute-start.20 = (f32[4,160,128]{2,1,0:T(8,128)S(1)}, f32[4,160,128]{2,1,0:T(8,128)S(1)}, u32[]{:S(2)}, u32[]{:S(2)}) collective-permute-start(f32[4,160,128]{2,1,0:T(8,128)S(1)} %get-tuple-element.37.part1), channel_id=1, source_target_pairs={{0,192},{64,0},{128,64},{192,128},{1,193},{65,1},{129,65},{193,129... | collective-permute-start | bytes 983048 | tf_op jit(solution)/shard_map/ppermute | solution.py:26
  80.2 16.3 %collective-permute-start.19 = (f32[4,160,128]{2,1,0:T(8,128)S(1)}, f32[4,160,128]{2,1,0:T(8,128)S(1)}, u32[]{:S(2)}, u32[]{:S(2)}) collective-permute-start(f32[4,160,128]{2,1,0:T(8,128)S(1)} %get-tuple-element.38.part2), channel_id=1, source_target_pairs={{0,128},{64,192},{128,0},{192,64},{1,129},{65,193},{129,1},{193,65... | collective-permute-start | bytes 983048 | tf_op jit(solution)/shard_map/ppermute | solution.py:26
  81.8 16.6 %collective-permute-start.18 = (f32[4,160,128]{2,1,0:T(8,128)S(1)}, f32[4,160,128]{2,1,0:T(8,128)S(1)}, u32[]{:S(2)}, u32[]{:S(2)}) collective-permute-start(f32[4,160,128]{2,1,0:T(8,128)S(1)} %get-tuple-element.39.part3), channel_id=1, source_target_pairs={{0,64},{64,128},{128,192},{192,0},{1,65},{65,129},{129,193},{193,1... | collective-permute-start | bytes 983048 | tf_op jit(solution)/shard_map/ppermute | solution.py:26
  89.7 8.6 %collective-permute-start.17 = (f32[8,128]{1,0:T(8,128)S(1)}, f32[8,128]{1,0:T(8,128)S(1)}, u32[]{:S(2)}, u32[]{:S(2)}) collective-permute-start(f32[8,128]{1,0:T(8,128)S(1)} %reduce_sum.99.sum0), channel_id=1, source_target_pairs={{0,192},{64,0},{128,64},{192,128},{1,193},{65,1},{129,65},{193,129... | collective-permute-start | bytes 12296 | tf_op jit(solution)/shard_map/ppermute | solution.py:26
  92.2 6.3 %collective-permute-start.16 = (f32[8,128]{1,0:T(8,128)S(1)}, f32[8,128]{1,0:T(8,128)S(1)}, u32[]{:S(2)}, u32[]{:S(2)}) collective-permute-start(f32[8,128]{1,0:T(8,128)S(1)} %reduce_sum.99.sum0), channel_id=1, source_target_pairs={{0,128},{64,192},{128,0},{192,64},{1,129},{65,193},{129,1},{193,65... | collective-permute-start | bytes 12296 | tf_op jit(solution)/shard_map/ppermute | solution.py:26
  94.7 5.2 %collective-permute-start.15 = (f32[8,128]{1,0:T(8,128)S(1)}, f32[8,128]{1,0:T(8,128)S(1)}, u32[]{:S(2)}, u32[]{:S(2)}) collective-permute-start(f32[8,128]{1,0:T(8,128)S(1)} %reduce_sum.99.sum0), channel_id=1, source_target_pairs={{0,64},{64,128},{128,192},{192,0},{1,65},{65,129},{129,193},{193,1... | collective-permute-start | bytes 12296 | tf_op jit(solution)/shard_map/ppermute | solution.py:26

commit v5 on v4

--- a/solution.py
+++ b/solution.py
@@ -91,9 +91,9 @@
     )(*msgs, low, high)
 
 
-def split_kernel(cot, lat, out0, out1, out2, out3, sems):
+def split_kernel(cot, out0, out1, out2, out3, sems):
     place = lax.axis_index("x")
-    fine, cells = cot.shape[2], lat.shape[2]
+    fine = cot.shape[2]
     copies = []
     for k, out in enumerate((out0, out1, out2, out3)):
         first = pl.multiple_of(lax.rem(place + k, FRAMES) * 128, 128)
@@ -101,9 +101,6 @@
             (cot.at[0, row, :, pl.ds(first, 128)], out.at[row * fine : (row + 1) * fine])
             for row in range(2)
         ]
-        for q in range(lat.shape[3] // 128):
-            start = 2 * fine + q * cells
-            moves.append((lat.at[0, 0, :, q * 128 : q * 128 + 128], out.at[start : start + cells]))
         for source, target in moves:
             copies.append(pltpu.make_async_copy(source, target, sems.at[len(copies)]))
     for copy in copies:
@@ -112,17 +109,17 @@
         copy.wait()
 
 
-def split(cotangent, latent):
-    rows = 2 * cotangent.shape[2] + 4 * latent.shape[2]
+def split(cotangent):
+    rows = 2 * cotangent.shape[2]
     return pl.pallas_call(
         split_kernel,
         out_shape=[jax.ShapeDtypeStruct((rows, 128), cotangent.dtype)] * FRAMES,
-        in_specs=[HBM] * 2,
+        in_specs=[HBM],
         out_specs=[VMEM] * FRAMES,
-        scratch_shapes=[pltpu.SemaphoreType.DMA((6 * FRAMES,))],
+        scratch_shapes=[pltpu.SemaphoreType.DMA((2 * FRAMES,))],
         compiler_params=pltpu.CompilerParams(vmem_limit_bytes=2 << 20),
-        cost_estimate=pl.CostEstimate(flops=0, bytes_accessed=2_600_000, transcendentals=0),
-    )(cotangent, latent)
+        cost_estimate=pl.CostEstimate(flops=0, bytes_accessed=1_300_000, transcendentals=0),
+    )(cotangent)
 
 
 def message_kernel(lat, weight, out, stats, latent, held, sems):
@@ -168,6 +165,28 @@
     )(latent, weight)
 
 
+def share_kernel(total, lat, out):
+    cells = lat.shape[0]
+    for q in range(4):
+        out[q * cells : (q + 1) * cells] = lat[:, q * 128 : q * 128 + 128]
+    rest = jnp.concatenate([total[...], jnp.zeros((8, 128), jnp.float32)], axis=0)
+    for p in range(3):
+        part = rest.astype(jnp.bfloat16)
+        out[4 * cells + 16 * p : 4 * cells + 16 * p + 16] = part
+        rest = rest - part.astype(jnp.float32)
+
+
+def share(total, lat):
+    return pl.pallas_call(
+        share_kernel,
+        out_shape=jax.ShapeDtypeStruct((4 * lat.shape[0] + 48, 128), jnp.bfloat16),
+        in_specs=[VMEM] * 2,
+        out_specs=VMEM,
+        compiler_params=pltpu.CompilerParams(vmem_limit_bytes=2 << 20),
+        cost_estimate=pl.CostEstimate(flops=10_000, bytes_accessed=340_000, transcendentals=0),
+    )(total, lat)
+
+
 def rims_kernel(msg0, msg1, msg2, msg3, first, last):
     for k, msg in enumerate((msg0, msg1, msg2, msg3)):
         fine = first.shape[1]
@@ -202,7 +221,8 @@
             core = c if side == 0 else 1 - c
             piece = pieces[index * CS + side]
             for z in range(ZS):
-                row = pl.multiple_of(index * 128 + z * (CS * 8) + core * 8, 8)
+                source_z = z + core * (ZS - 1 - 2 * z)
+                row = pl.multiple_of(index * 128 + source_z * (CS * 8) + core * 8, 8)
                 copies.append(
                     pltpu.make_async_copy(
                         piece.at[z, 0:PLANES],
@@ -268,13 +288,12 @@
 
 def sums_kernel(part0, part1, part2, part3, msg0, msg1, msg2, msg3, chan, out, kept):
     cells = part0.shape[1]
-    offset = msg0.shape[0] - 4 * cells
     for q in range(4):
         lanes = slice(q * 128, q * 128 + 128)
         first = jnp.zeros((8, 128), jnp.float32)
         second = jnp.zeros((8, 128), jnp.float32)
         for part, msg in ((part0, msg0), (part1, msg1), (part2, msg2), (part3, msg3)):
-            start = offset + q * cells
+            start = q * cells
             normed, gate = slope(msg[start : start + cells], chan, lanes)
             act = part[q] * gate
             first = first + act.reshape(cells // 8, 8, 128).sum(axis=0)
@@ -353,17 +372,26 @@
     own = latent[0, 0]
 
     block = lax.all_to_all(
-        message(latent, conv_weight.reshape(PLANES, 8, 128)), "z", 0, 0, tiled=True
+        message(latent, conv_weight.reshape(PLANES, 8, 128)),
+        ("z", "c"),
+        0,
+        0,
+        axis_index_groups=[
+            [z * CS for z in range(ZS)],
+            [z * CS + 1 for z in reversed(range(ZS))],
+        ],
+        tiled=True,
     )
-    pieces = [block] + [send(block, "y", step) for step in range(1, YS)]
 
     msgs = [
         msg if step == 0 else send(msg, "x", step)
-        for step, msg in enumerate(split(cotangent, latent))
+        for step, msg in enumerate(split(cotangent))
     ]
-    first, last = rims(msgs, cotangent.shape[2])
-    low = lax.ppermute(last, ROW_AXES, [(i, i + 1) for i in range(ROWS - 1)])
-    high = lax.ppermute(first, ROW_AXES, [(i + 1, i) for i in range(ROWS - 1)])
+    block, msgs = lax.optimization_barrier((block, msgs))
+    pieces = [block] + [send(block, "y", step) for step in range(1, YS)]
+    first_rows, last_rows = rims(msgs, cotangent.shape[2])
+    low = lax.ppermute(last_rows, ROW_AXES, [(i, i + 1) for i in range(ROWS - 1)])
+    high = lax.ppermute(first_rows, ROW_AXES, [(i + 1, i) for i in range(ROWS - 1)])
     lefts = pool(msgs, low, high)
     others = [send(piece, "c", 1) for piece in pieces]
     partial = None
@@ -374,7 +402,13 @@
     gathered = sum(
         jnp.sum(piece[:, PLANES:].astype(jnp.float32), axis=(0, 1)) for piece in pieces + others
     )
-    total = gathered + sum(send(gathered, "x", step) for step in range(1, FRAMES))
+    shared = share(gathered, own)
+    lats = [shared] + [send(shared, "x", step) for step in range(1, FRAMES)]
+    total = sum(
+        lat[first : first + 8].astype(jnp.float32)
+        for lat in lats
+        for first in range(4 * cells, 4 * cells + 48, 16)
+    )
     group = total.reshape(2, GROUPS, per_group).sum(axis=2) / (cell_count * per_group)
     group_mean = group[0]
     group_var = group[1] - group_mean * group_mean
@@ -383,7 +417,7 @@
         [jnp.repeat(group_mean, per_group), jnp.repeat(inv_std, per_group), norm_gain, norm_bias]
     )
 
-    sums = partial_sums(partial, msgs, chan)
+    sums = partial_sums(partial, lats, chan)
     parts = [partial[0]] + [send(partial[FRAMES - step], "x", step) for step in range(1, FRAMES)]
     sums = lax.all_to_all(sums, ROW_AXES, 0, 0, tiled=True).sum(axis=0)
     sums = [sums] + [send(sums, "x", step) for step in range(1, FRAMES)]

time: 102 us -> 101 us (level)
  starting transfers between devices: 52.7 us -> 43.4 us
  waiting for transfers between devices: 31 us -> 39.9 us
    ppermute x19, waiting for transfers between devices: 14.7 us -> 28.9 us  [send(): lax.ppermute(value, axis, [(i, (i + step) % size) for i in range(size)])]
    ppermute x19, starting transfers between devices: 28.2 us -> 20.7 us  [send(): lax.ppermute(value, axis, [(i, (i + step) % size) for i in range(size)])]
    all_to_all x1, waiting for transfers between devices: 7.1 us -> 0.74 us  [on_device(): lax.all_to_all(message(latent, conv_weight.reshape(PLANES, 8, 128)), ('z'...]
    all_to_all x1, starting transfers between devices: 10.4 us -> 8.71 us  [on_device(): sums = lax.all_to_all(sums, ROW_AXES, 0, 0, tiled=True).sum(axis=0)]
    all_to_all x1, waiting for transfers between devices: 7.91 us -> 9.45 us  [on_device(): sums = lax.all_to_all(sums, ROW_AXES, 0, 0, tiled=True).sum(axis=0)]
    unnamed x14 -> x12, local copies, waits for them, and re-layouts: 3.75 us -> 2.83 us
  transfers between devices with their start and end apart: 23 -> 23, of which waited for: 10 -> 13; matrix products, arithmetic and copies ran while one was open for 0% -> 0% of each run, Pallas kernels for 8% -> 8%
where the time goes in v5:
time: 101 us; the launch traced here: 99.4 us
  starting transfers between devices  43.4 us (43%)
  waiting for transfers between devices  39.9 us (40%)
  Pallas kernels  11.7 us (12%)
  local copies, waits for them, and re-layouts  3.22 us (3%)
    ppermute x19, waiting for transfers between devices, send(): lax.ppermute(value, axis, [(i, (i + step) % size) for i in range(size)])  28.9 us
    ppermute x19, starting transfers between devices, send(): lax.ppermute(value, axis, [(i, (i + step) % size) for i in range(size)])  20.7 us
    all_to_all x1, waiting for transfers between devices, on_device(): sums = lax.all_to_all(sums, ROW_AXES, 0, 0, tiled=True).sum(axis=0)  9.45 us
    all_to_all x1, starting transfers between devices, on_device(): lax.all_to_all(message(latent, conv_weight.reshape(PLANES, 8, 128)), ('z'...  8.71 us
    all_to_all x1, starting transfers between devices, on_device(): sums = lax.all_to_all(sums, ROW_AXES, 0, 0, tiled=True).sum(axis=0)  8.71 us
    pallas_call x2, Pallas kernels, product(): pl.pallas_call(functools.partial(product_kernel, steps, aliased), out_sha...  6.19 us
    ppermute x1, starting transfers between devices, on_device(): lax.ppermute(first_rows, ROW_AXES, [(i + 1, i) for i in range(ROWS - 1)])  3.35 us
    unnamed x12, local copies, waits for them, and re-layouts  2.83 us
  transfers between devices with their start and end apart: 23, of which 13 were waited for; matrix products, arithmetic and copies ran while one was open for 0% of the time, Pallas kernels for 8%

profile of v5, /device:TPU:32, one launch (start us, length us, event | category | flops | bytes accessed | tf_op | source)
XLA Modules:
  0.0 99.4 jit_solution(16370195849453535768)
XLA Ops:
  0.6 0.9 copy-done
  1.6 0.8 copy-done.3
  2.4 1.2 %shard_map.76 = bf16[8,30,8,128]{3,2,1,0:T(8,128)(2,1)} custom-call(bf16[1,1,160,512]{3,2,1,0:T(8,128)(2,1)S(1)} %copy-done, bf16[27,8,128]{2,1,0:T(8,128)(2,1)S(1)} %bitcast.17), custom_call_target="tpu_custom_call" | custom-call | flops 250000 | bytes 720000 | tf_op jit(solution)/shard_map/pallas_call | solution.py:152
  3.5 8.7 %all-to-all-start = ((bf16[8,30,8,128]{3,2,1,0:T(8,128)(2,1)}), bf16[8,30,8,128]{3,2,1,0:T(8,128)(2,1)S(1)}, u32[]{:S(2)}, u32[]{:S(2)}) async-start(bf16[8,30,8,128]{3,2,1,0:T(8,128)(2,1)} %shard_map.76), calls=%async_computation | async-start | bytes 983040 | tf_op jit(solution)/shard_map/all_to_all | solution.py:374
  12.3 1.1 %copy-done.2 = bf16[1,2,320,512]{3,2,1,0:T(8,128)(2,1)S(1)} copy-done((bf16[1,2,320,512]{3,2,1,0:T(8,128)(2,1)S(1)}, bf16[1,2,320,512]{3,2,1,0:T(8,128)(2,1)}, u32[]{:S(2)}) %copy-start.2) | copy-done | bytes 655384
  13.6 1.6 %collective-permute-start = (bf16[640,128]{1,0:T(8,128)(2,1)S(1)}, bf16[640,128]{1,0:T(8,128)(2,1)S(1)}, u32[]{:S(2)}, u32[]{:S(2)}) collective-permute-start(bf16[640,128]{1,0:T(8,128)(2,1)S(1)} %get-tuple-element.29), channel_id=1, source_target_pairs={{0,64},{64,128},{128,192},{192,0},{1,65},{65,129},{129,193},{193,1... | collective-permute-start | bytes 491528 | tf_op jit(solution)/shard_map/ppermute | solution.py:26
  15.1 2.7 %collective-permute-start.1 = (bf16[640,128]{1,0:T(8,128)(2,1)S(1)}, bf16[640,128]{1,0:T(8,128)(2,1)S(1)}, u32[]{:S(2)}, u32[]{:S(2)}) collective-permute-start(bf16[640,128]{1,0:T(8,128)(2,1)S(1)} %get-tuple-element.30), channel_id=1, source_target_pairs={{0,128},{64,192},{128,0},{192,64},{1,129},{65,193},{129,1},{193,65... | collective-permute-start | bytes 491528 | tf_op jit(solution)/shard_map/ppermute | solution.py:26
  17.9 1.4 %collective-permute-start.2 = (bf16[640,128]{1,0:T(8,128)(2,1)S(1)}, bf16[640,128]{1,0:T(8,128)(2,1)S(1)}, u32[]{:S(2)}, u32[]{:S(2)}) collective-permute-start(bf16[640,128]{1,0:T(8,128)(2,1)S(1)} %get-tuple-element.31), channel_id=1, source_target_pairs={{0,192},{64,0},{128,64},{192,128},{1,193},{65,1},{129,65},{193,129... | collective-permute-start | bytes 491528 | tf_op jit(solution)/shard_map/ppermute | solution.py:26
  19.3 1.7 %collective-permute-done.msg1 = bf16[640,128]{1,0:T(8,128)(2,1)S(1)} collective-permute-done((bf16[640,128]{1,0:T(8,128)(2,1)S(1)}, bf16[640,128]{1,0:T(8,128)(2,1)S(1)}, u32[]{:S(2)}, u32[]{:S(2)}) %collective-permute-start) | collective-permute-done | bytes 163872 | tf_op jit(solution)/shard_map/ppermute | solution.py:26
  20.9 4.3 %collective-permute-done.1.msg2 = bf16[640,128]{1,0:T(8,128)(2,1)S(1)} collective-permute-done((bf16[640,128]{1,0:T(8,128)(2,1)S(1)}, bf16[640,128]{1,0:T(8,128)(2,1)S(1)}, u32[]{:S(2)}, u32[]{:S(2)}) %collective-permute-start.1) | collective-permute-done | bytes 163872 | tf_op jit(solution)/shard_map/ppermute | solution.py:26
  26.0 3.0 %collective-permute-start.10 = (bf16[8,30,8,128]{3,2,1,0:T(8,128)(2,1)S(1)}, bf16[8,30,8,128]{3,2,1,0:T(8,128)(2,1)S(1)}, u32[]{:S(2)}, u32[]{:S(2)}) collective-permute-start(bf16[8,30,8,128]{3,2,1,0:T(8,128)(2,1)S(1)} %all-to-all-done.refs_0_), channel_id=1, source_target_pairs={{0,48},{16,0},{32,16},{48,32},{1,49},{17,1},{33,17},{49,33},{2,50}... | collective-permute-start | bytes 1474568 | tf_op jit(solution)/shard_map/ppermute | solution.py:26
  29.1 1.9 %collective-permute-start.7 = (bf16[4,320,128]{2,1,0:T(8,128)(2,1)S(1)}, bf16[4,320,128]{2,1,0:T(8,128)(2,1)S(1)}, u32[]{:S(2)}, u32[]{:S(2)}) collective-permute-start(bf16[4,320,128]{2,1,0:T(8,128)(2,1)S(1)} %get-tuple-element.37), channel_id=1, source_target_pairs={{0,1},{1,2},{2,3},{3,4},{4,5},{5,6},{6,7},{7,8},{8,9},{9,10},{10,1... | collective-permute-start | bytes 983048 | tf_op jit(solution)/shard_map/ppermute | solution.py:393
  31.0 2.3 %collective-permute-start.3 = (bf16[8,30,8,128]{3,2,1,0:T(8,128)(2,1)S(1)}, bf16[8,30,8,128]{3,2,1,0:T(8,128)(2,1)S(1)}, u32[]{:S(2)}, u32[]{:S(2)}) collective-permute-start(bf16[8,30,8,128]{3,2,1,0:T(8,128)(2,1)S(1)} %all-to-all-done.refs_0_), channel_id=1, source_target_pairs={{0,32},{16,48},{32,0},{48,16},{1,33},{17,49},{33,1},{49,17},{2,34}... | collective-permute-start | bytes 1474568 | tf_op jit(solution)/shard_map/ppermute | solution.py:26
  33.3 3.4 %collective-permute-start.8 = (bf16[4,320,128]{2,1,0:T(8,128)(2,1)S(1)}, bf16[4,320,128]{2,1,0:T(8,128)(2,1)S(1)}, u32[]{:S(2)}, u32[]{:S(2)}) collective-permute-start(bf16[4,320,128]{2,1,0:T(8,128)(2,1)S(1)} %get-tuple-element.38), channel_id=1, source_target_pairs={{1,0},{2,1},{3,2},{4,3},{5,4},{6,5},{7,6},{8,7},{9,8},{10,9},{11,1... | collective-permute-start | bytes 983048 | tf_op jit(solution)/shard_map/ppermute | solution.py:394
  36.6 0.8 collective-permute-done.7.low
  37.4 10.9 %collective-permute-done.10.refs_2_ = bf16[8,30,8,128]{3,2,1,0:T(8,128)(2,1)S(1)} collective-permute-done((bf16[8,30,8,128]{3,2,1,0:T(8,128)(2,1)S(1)}, bf16[8,30,8,128]{3,2,1,0:T(8,128)(2,1)S(1)}, u32[]{:S(2)}, u32[]{:S(2)}) %collective-permute-start.10) | collective-permute-done | bytes 491552 | tf_op jit(solution)/shard_map/ppermute | solution.py:26
  48.4 1.5 %shard_map.79 = (bf16[2,640,1152]{2,1,0:T(8,128)(2,1)S(1)}, bf16[2,480,1152]{2,1,0:T(8,128)(2,1)S(1)}, bf16[2,320,1152]{2,1,0:T(8,128)(2,1)S(1)}) custom-call(bf16[640,128]{1,0:T(8,128)(2,1)S(1)} %get-tuple-element.33.msg0, bf16[640,128]{1,0:T(8,128)(2,1)S(1)} %collective-permute-done.msg1, bf16[640,128]{1,0:T(8,128)(2,1)S(1)} %collective-permute-done.1.msg2, ...), custom_call_target="tpu_custom_call" | custom-call | flops 1000 | bytes 1000 | tf_op jit(solution)/shard_map/pallas_call | solution.py:80
  49.9 1.9 %collective-permute-done.5.refs_2_ = bf16[8,30,8,128]{3,2,1,0:T(8,128)(2,1)S(1)} collective-permute-done((bf16[8,30,8,128]{3,2,1,0:T(8,128)(2,1)S(1)}, bf16[8,30,8,128]{3,2,1,0:T(8,128)(2,1)S(1)}, u32[]{:S(2)}, u32[]{:S(2)}) %collective-permute-start.5) | collective-permute-done | bytes 491552 | tf_op jit(solution)/shard_map/ppermute | solution.py:26
  52.5 1.1 %collective-permute-done.6.refs_3_ = bf16[8,30,8,128]{3,2,1,0:T(8,128)(2,1)S(1)} collective-permute-done((bf16[8,30,8,128]{3,2,1,0:T(8,128)(2,1)S(1)}, bf16[8,30,8,128]{3,2,1,0:T(8,128)(2,1)S(1)}, u32[]{:S(2)}, u32[]{:S(2)}) %collective-permute-start.6) | collective-permute-done | bytes 491552 | tf_op jit(solution)/shard_map/ppermute | solution.py:26
  54.4 2.7 %collective-permute-start.14 = (bf16[688,128]{1,0:T(8,128)(2,1)S(1)}, bf16[688,128]{1,0:T(8,128)(2,1)S(1)}, u32[]{:S(2)}, u32[]{:S(2)}) collective-permute-start(bf16[688,128]{1,0:T(8,128)(2,1)S(1)} %shard_map.82.msg0), channel_id=1, source_target_pairs={{0,192},{64,0},{128,64},{192,128},{1,193},{65,1},{129,65},{193,129... | collective-permute-start | bytes 528392 | tf_op jit(solution)/shard_map/ppermute | solution.py:26
  57.2 1.1 %collective-permute-start.13 = (bf16[688,128]{1,0:T(8,128)(2,1)S(1)}, bf16[688,128]{1,0:T(8,128)(2,1)S(1)}, u32[]{:S(2)}, u32[]{:S(2)}) collective-permute-start(bf16[688,128]{1,0:T(8,128)(2,1)S(1)} %shard_map.82.msg0), channel_id=1, source_target_pairs={{0,128},{64,192},{128,0},{192,64},{1,129},{65,193},{129,1},{193,65... | collective-permute-start | bytes 528392 | tf_op jit(solution)/shard_map/ppermute | solution.py:26
  58.9 3.1 %shard_map.80 = (f32[4,160,128]{2,1,0:T(8,128)S(1)}, f32[4,160,128]{2,1,0:T(8,128)S(1)}, f32[4,160,128]{2,1,0:T(8,128)S(1)}, f32[4,160,128]{2,1,0:T(8,128)S(1)}) custom-call(bf16[8,30,8,128]{3,2,1,0:T(8,128)(2,1)S(1)} %all-to-all-done.refs_0_, bf16[8,30,8,128]{3,2,1,0:T(8,128)(2,1)S(1)} %collective-permute-done.9.refs_1_, ...), custom_call_target="tpu_custom_call" | custom-call | flops 1700000000 | bytes 9000000 | tf_op jit(solution)/shard_map/pallas_call | solution.py:262
  62.0 3.1 %shard_map.81 = (f32[4,160,128]{2,1,0:T(8,128)S(1)}, f32[4,160,128]{2,1,0:T(8,128)S(1)}, f32[4,160,128]{2,1,0:T(8,128)S(1)}, f32[4,160,128]{2,1,0:T(8,128)S(1)}) custom-call(bf16[8,30,8,128]{3,2,1,0:T(8,128)(2,1)S(1)} %collective-permute-done.3.refs_0_, ...), custom_call_target="tpu_custom_call", output_to_operand_aliasing={{0}: (7, {}), {1}: (8, {}), {2}: (9, {}), {3}: (10, {})} | custom-call | flops 1700000000 | bytes 9000000 | tf_op jit(solution)/shard_map/pallas_call | solution.py:262
  65.1 1.0 collective-permute-done.13.msg2
  66.1 2.6 %collective-permute-done.12.msg1 = bf16[688,128]{1,0:T(8,128)(2,1)S(1)} collective-permute-done((bf16[688,128]{1,0:T(8,128)(2,1)S(1)}, bf16[688,128]{1,0:T(8,128)(2,1)S(1)}, u32[]{:S(2)}, u32[]{:S(2)}) %collective-permute-start.12) | collective-permute-done | bytes 176160 | tf_op jit(solution)/shard_map/ppermute | solution.py:26
  69.3 1.5 %shard_map.83 = f32[64,8,128]{2,1,0:T(8,128)} custom-call(f32[4,160,128]{2,1,0:T(8,128)S(1)} %get-tuple-element.46.part0, f32[4,160,128]{2,1,0:T(8,128)S(1)} %get-tuple-element.47.part1, f32[4,160,128]{2,1,0:T(8,128)S(1)} %get-tuple-element.48.part2, f32[4,160,128]{2,1,0:T(8,128)S(1)} %get-tuple-element.49.part3, bf16[688,128]{1,0:T(8,128)(2,1)S(1)} %shard_map.82.msg0, ...), custom_call_target="tpu_custom_call" | custom-call | flops 6000000 | bytes 2900000 | tf_op jit(solution)/shard_map/pallas_call | solution.py:309
  70.8 8.7 %all-to-all-start.1 = ((f32[64,8,128]{2,1,0:T(8,128)}), f32[64,8,128]{2,1,0:T(8,128)S(1)}, u32[]{:S(2)}, u32[]{:S(2)}) async-start(f32[64,8,128]{2,1,0:T(8,128)} %shard_map.83), calls=%async_computation.1 | async-start | bytes 524288 | tf_op jit(solution)/shard_map/all_to_all | solution.py:422
  81.0 0.8 collective-permute-start.18
  81.8 9.5 %all-to-all-done.1 = f32[64,8,128]{2,1,0:T(8,128)S(1)} async-done(((f32[64,8,128]{2,1,0:T(8,128)}), f32[64,8,128]{2,1,0:T(8,128)S(1)}, u32[]{:S(2)}, u32[]{:S(2)}) %all-to-all-start.1) | async-done | bytes 262176 | tf_op jit(solution)/shard_map/all_to_all | solution.py:422
  92.8 0.8 collective-permute-start.15
  93.6 4.7 %collective-permute-done.18.part1 = f32[4,160,128]{2,1,0:T(8,128)S(1)} collective-permute-done((f32[4,160,128]{2,1,0:T(8,128)S(1)}, f32[4,160,128]{2,1,0:T(8,128)S(1)}, u32[]{:S(2)}, u32[]{:S(2)}) %collective-permute-start.18) | collective-permute-done | bytes 327712 | tf_op jit(solution)/shard_map/ppermute | solution.py:26
  98.4 1.1 %shard_map.84 = (f32[160,512]{1,0:T(8,128)}, f32[512]{0:T(512)}, f32[512]{0:T(512)}) custom-call(f32[8,128]{1,0:T(8,128)S(1)} %reduce_sum.99.sum0, f32[8,128]{1,0:T(8,128)S(1)} %collective-permute-done.15.sum1, f32[8,128]{1,0:T(8,128)S(1)} %collective-permute-done.16.sum2, f32[8,128]{1,0:T(8,128)S(1)} %collective-permute-done.17.sum3, ...), custom_call_target="tpu_custom_call" | custom-call | flops 2000000 | bytes 1900000 | tf_op jit(solution)/shard_map/pallas_call | solution.py:352
  (56 shorter events, 6.8 us)
Async XLA Ops:
  0.6 0.9 copy-start
  1.5 0.8 copy-start.3
  3.5 50.9 %copy-start.1 = (bf16[1,1,160,512]{3,2,1,0:T(8,128)(2,1)S(1)}, bf16[1,1,160,512]{3,2,1,0:T(8,128)(2,1)}, u32[]{:S(2)}) copy-start(bf16[1,1,160,512]{3,2,1,0:T(8,128)(2,1)} %lat.1) | copy-start | bytes 491524
  3.5 22.4 %all-to-all-start = ((bf16[8,30,8,128]{3,2,1,0:T(8,128)(2,1)}), bf16[8,30,8,128]{3,2,1,0:T(8,128)(2,1)S(1)}, u32[]{:S(2)}, u32[]{:S(2)}) async-start(bf16[8,30,8,128]{3,2,1,0:T(8,128)(2,1)} %shard_map.76), calls=%async_computation | async-start | bytes 983040 | tf_op jit(solution)/shard_map/all_to_all | solution.py:374
  12.3 1.1 %copy-start.2 = (bf16[1,2,320,512]{3,2,1,0:T(8,128)(2,1)S(1)}, bf16[1,2,320,512]{3,2,1,0:T(8,128)(2,1)}, u32[]{:S(2)}) copy-start(bf16[1,2,320,512]{3,2,1,0:T(8,128)(2,1)} %cot.1) | copy-start | bytes 1966084
  13.6 7.4 %collective-permute-start = (bf16[640,128]{1,0:T(8,128)(2,1)S(1)}, bf16[640,128]{1,0:T(8,128)(2,1)S(1)}, u32[]{:S(2)}, u32[]{:S(2)}) collective-permute-start(bf16[640,128]{1,0:T(8,128)(2,1)S(1)} %get-tuple-element.29), channel_id=1, source_target_pairs={{0,64},{64,128},{128,192},{192,0},{1,65},{65,129},{129,193},{193,1... | collective-permute-start | bytes 491528 | tf_op jit(solution)/shard_map/ppermute | solution.py:26
  15.1 10.1 %collective-permute-start.1 = (bf16[640,128]{1,0:T(8,128)(2,1)S(1)}, bf16[640,128]{1,0:T(8,128)(2,1)S(1)}, u32[]{:S(2)}, u32[]{:S(2)}) collective-permute-start(bf16[640,128]{1,0:T(8,128)(2,1)S(1)} %get-tuple-element.30), channel_id=1, source_target_pairs={{0,128},{64,192},{128,0},{192,64},{1,129},{65,193},{129,1},{193,65... | collective-permute-start | bytes 491528 | tf_op jit(solution)/shard_map/ppermute | solution.py:26
  17.9 7.4 %collective-permute-start.2 = (bf16[640,128]{1,0:T(8,128)(2,1)S(1)}, bf16[640,128]{1,0:T(8,128)(2,1)S(1)}, u32[]{:S(2)}, u32[]{:S(2)}) collective-permute-start(bf16[640,128]{1,0:T(8,128)(2,1)S(1)} %get-tuple-element.31), channel_id=1, source_target_pairs={{0,192},{64,0},{128,64},{192,128},{1,193},{65,1},{129,65},{193,129... | collective-permute-start | bytes 491528 | tf_op jit(solution)/shard_map/ppermute | solution.py:26
  26.0 22.4 %collective-permute-start.10 = (bf16[8,30,8,128]{3,2,1,0:T(8,128)(2,1)S(1)}, bf16[8,30,8,128]{3,2,1,0:T(8,128)(2,1)S(1)}, u32[]{:S(2)}, u32[]{:S(2)}) collective-permute-start(bf16[8,30,8,128]{3,2,1,0:T(8,128)(2,1)S(1)} %all-to-all-done.refs_0_), channel_id=1, source_target_pairs={{0,48},{16,0},{32,16},{48,32},{1,49},{17,1},{33,17},{49,33},{2,50}... | collective-permute-start | bytes 1474568 | tf_op jit(solution)/shard_map/ppermute | solution.py:26
  29.0 22.8 %collective-permute-start.5 = (bf16[8,30,8,128]{3,2,1,0:T(8,128)(2,1)S(1)}, bf16[8,30,8,128]{3,2,1,0:T(8,128)(2,1)S(1)}, u32[]{:S(2)}, u32[]{:S(2)}) collective-permute-start(bf16[8,30,8,128]{3,2,1,0:T(8,128)(2,1)S(1)} %all-to-all-done.refs_0_), channel_id=1, source_target_pairs={{0,16},{16,32},{32,48},{48,0},{1,17},{17,33},{33,49},{49,1},{2,18}... | collective-permute-start | bytes 1474568 | tf_op jit(solution)/shard_map/ppermute | solution.py:26
  29.1 8.4 %collective-permute-start.7 = (bf16[4,320,128]{2,1,0:T(8,128)(2,1)S(1)}, bf16[4,320,128]{2,1,0:T(8,128)(2,1)S(1)}, u32[]{:S(2)}, u32[]{:S(2)}) collective-permute-start(bf16[4,320,128]{2,1,0:T(8,128)(2,1)S(1)} %get-tuple-element.37), channel_id=1, source_target_pairs={{0,1},{1,2},{2,3},{3,4},{4,5},{5,6},{6,7},{7,8},{8,9},{9,10},{10,1... | collective-permute-start | bytes 983048 | tf_op jit(solution)/shard_map/ppermute | solution.py:393
  31.0 20.8 %collective-permute-start.3 = (bf16[8,30,8,128]{3,2,1,0:T(8,128)(2,1)S(1)}, bf16[8,30,8,128]{3,2,1,0:T(8,128)(2,1)S(1)}, u32[]{:S(2)}, u32[]{:S(2)}) collective-permute-start(bf16[8,30,8,128]{3,2,1,0:T(8,128)(2,1)S(1)} %all-to-all-done.refs_0_), channel_id=1, source_target_pairs={{0,32},{16,48},{32,0},{48,16},{1,33},{17,49},{33,1},{49,17},{2,34}... | collective-permute-start | bytes 1474568 | tf_op jit(solution)/shard_map/ppermute | solution.py:26
  33.3 15.1 %collective-permute-start.8 = (bf16[4,320,128]{2,1,0:T(8,128)(2,1)S(1)}, bf16[4,320,128]{2,1,0:T(8,128)(2,1)S(1)}, u32[]{:S(2)}, u32[]{:S(2)}) collective-permute-start(bf16[4,320,128]{2,1,0:T(8,128)(2,1)S(1)} %get-tuple-element.38), channel_id=1, source_target_pairs={{1,0},{2,1},{3,2},{4,3},{5,4},{6,5},{7,6},{8,7},{9,8},{10,9},{11,1... | collective-permute-start | bytes 983048 | tf_op jit(solution)/shard_map/ppermute | solution.py:394
  37.4 15.0 %collective-permute-start.9 = (bf16[8,30,8,128]{3,2,1,0:T(8,128)(2,1)S(1)}, bf16[8,30,8,128]{3,2,1,0:T(8,128)(2,1)S(1)}, u32[]{:S(2)}, u32[]{:S(2)}) collective-permute-start(bf16[8,30,8,128]{3,2,1,0:T(8,128)(2,1)S(1)} %all-to-all-done.refs_0_), channel_id=1, source_target_pairs={{0,1},{1,0},{2,3},{3,2},{4,5},{5,4},{6,7},{7,6},{8,9},{9,8},{10,11... | collective-permute-start | bytes 1474568 | tf_op jit(solution)/shard_map/ppermute | solution.py:26
  48.4 4.1 %collective-permute-start.11 = (bf16[8,30,8,128]{3,2,1,0:T(8,128)(2,1)S(1)}, bf16[8,30,8,128]{3,2,1,0:T(8,128)(2,1)S(1)}, u32[]{:S(2)}, u32[]{:S(2)}) collective-permute-start(bf16[8,30,8,128]{3,2,1,0:T(8,128)(2,1)S(1)} %collective-permute-done.10.refs_2_), channel_id=1, source_target_pairs={{0,1},{1,0},{2,3},{3,2},{4,5},{5,4},{6,7},{7,6},{8,9},{9,8},{10,11... | collective-permute-start | bytes 1474568 | tf_op jit(solution)/shard_map/ppermute | solution.py:26
  51.8 1.9 %collective-permute-start.6 = (bf16[8,30,8,128]{3,2,1,0:T(8,128)(2,1)S(1)}, bf16[8,30,8,128]{3,2,1,0:T(8,128)(2,1)S(1)}, u32[]{:S(2)}, u32[]{:S(2)}) collective-permute-start(bf16[8,30,8,128]{3,2,1,0:T(8,128)(2,1)S(1)} %collective-permute-done.5.refs_2_), channel_id=1, source_target_pairs={{0,1},{1,0},{2,3},{3,2},{4,5},{5,4},{6,7},{7,6},{8,9},{9,8},{10,11... | collective-permute-start | bytes 1474568 | tf_op jit(solution)/shard_map/ppermute | solution.py:26
  51.8 2.5 %collective-permute-start.4 = (bf16[8,30,8,128]{3,2,1,0:T(8,128)(2,1)S(1)}, bf16[8,30,8,128]{3,2,1,0:T(8,128)(2,1)S(1)}, u32[]{:S(2)}, u32[]{:S(2)}) collective-permute-start(bf16[8,30,8,128]{3,2,1,0:T(8,128)(2,1)S(1)} %collective-permute-done.3.refs_0_), channel_id=1, source_target_pairs={{0,1},{1,0},{2,3},{3,2},{4,5},{5,4},{6,7},{7,6},{8,9},{9,8},{10,11... | collective-permute-start | bytes 1474568 | tf_op jit(solution)/shard_map/ppermute | solution.py:26
  54.4 10.7 %collective-permute-start.14 = (bf16[688,128]{1,0:T(8,128)(2,1)S(1)}, bf16[688,128]{1,0:T(8,128)(2,1)S(1)}, u32[]{:S(2)}, u32[]{:S(2)}) collective-permute-start(bf16[688,128]{1,0:T(8,128)(2,1)S(1)} %shard_map.82.msg0), channel_id=1, source_target_pairs={{0,192},{64,0},{128,64},{192,128},{1,193},{65,1},{129,65},{193,129... | collective-permute-start | bytes 528392 | tf_op jit(solution)/shard_map/ppermute | solution.py:26
  57.2 8.9 %collective-permute-start.13 = (bf16[688,128]{1,0:T(8,128)(2,1)S(1)}, bf16[688,128]{1,0:T(8,128)(2,1)S(1)}, u32[]{:S(2)}, u32[]{:S(2)}) collective-permute-start(bf16[688,128]{1,0:T(8,128)(2,1)S(1)} %shard_map.82.msg0), channel_id=1, source_target_pairs={{0,128},{64,192},{128,0},{192,64},{1,129},{65,193},{129,1},{193,65... | collective-permute-start | bytes 528392 | tf_op jit(solution)/shard_map/ppermute | solution.py:26
  58.3 10.4 %collective-permute-start.12 = (bf16[688,128]{1,0:T(8,128)(2,1)S(1)}, bf16[688,128]{1,0:T(8,128)(2,1)S(1)}, u32[]{:S(2)}, u32[]{:S(2)}) collective-permute-start(bf16[688,128]{1,0:T(8,128)(2,1)S(1)} %shard_map.82.msg0), channel_id=1, source_target_pairs={{0,64},{64,128},{128,192},{192,0},{1,65},{65,129},{129,193},{193,1... | collective-permute-start | bytes 528392 | tf_op jit(solution)/shard_map/ppermute | solution.py:26
  62.0 7.3 %copy-start.4 = (f32[512]{0:T(512)S(1)}, f32[512]{0:T(512)}, u32[]{:S(2)}) copy-start(f32[512]{0:T(512)} %param.7) | copy-start | bytes 6148
  62.0 7.3 %copy-start.5 = (f32[512]{0:T(512)S(1)}, f32[512]{0:T(512)}, u32[]{:S(2)}) copy-start(f32[512]{0:T(512)} %param.6) | copy-start | bytes 6148
  70.8 20.5 %all-to-all-start.1 = ((f32[64,8,128]{2,1,0:T(8,128)}), f32[64,8,128]{2,1,0:T(8,128)S(1)}, u32[]{:S(2)}, u32[]{:S(2)}) async-start(f32[64,8,128]{2,1,0:T(8,128)} %shard_map.83), calls=%async_computation.1 | async-start | bytes 524288 | tf_op jit(solution)/shard_map/all_to_all | solution.py:422
  79.5 13.3 %collective-permute-start.20 = (f32[4,160,128]{2,1,0:T(8,128)S(1)}, f32[4,160,128]{2,1,0:T(8,128)S(1)}, u32[]{:S(2)}, u32[]{:S(2)}) collective-permute-start(f32[4,160,128]{2,1,0:T(8,128)S(1)} %get-tuple-element.47.part1), channel_id=1, source_target_pairs={{0,192},{64,0},{128,64},{192,128},{1,193},{65,1},{129,65},{193,129... | collective-permute-start | bytes 983048 | tf_op jit(solution)/shard_map/ppermute | solution.py:26
  80.2 13.4 %collective-permute-start.19 = (f32[4,160,128]{2,1,0:T(8,128)S(1)}, f32[4,160,128]{2,1,0:T(8,128)S(1)}, u32[]{:S(2)}, u32[]{:S(2)}) collective-permute-start(f32[4,160,128]{2,1,0:T(8,128)S(1)} %get-tuple-element.48.part2), channel_id=1, source_target_pairs={{0,128},{64,192},{128,0},{192,64},{1,129},{65,193},{129,1},{193,65... | collective-permute-start | bytes 983048 | tf_op jit(solution)/shard_map/ppermute | solution.py:26
  81.0 17.3 %collective-permute-start.18 = (f32[4,160,128]{2,1,0:T(8,128)S(1)}, f32[4,160,128]{2,1,0:T(8,128)S(1)}, u32[]{:S(2)}, u32[]{:S(2)}) collective-permute-start(f32[4,160,128]{2,1,0:T(8,128)S(1)} %get-tuple-element.49.part3), channel_id=1, source_target_pairs={{0,64},{64,128},{128,192},{192,0},{1,65},{65,129},{129,193},{193,1... | collective-permute-start | bytes 983048 | tf_op jit(solution)/shard_map/ppermute | solution.py:26
  91.3 7.0 %collective-permute-start.17 = (f32[8,128]{1,0:T(8,128)S(1)}, f32[8,128]{1,0:T(8,128)S(1)}, u32[]{:S(2)}, u32[]{:S(2)}) collective-permute-start(f32[8,128]{1,0:T(8,128)S(1)} %reduce_sum.99.sum0), channel_id=1, source_target_pairs={{0,192},{64,0},{128,64},{192,128},{1,193},{65,1},{129,65},{193,129... | collective-permute-start | bytes 12296 | tf_op jit(solution)/shard_map/ppermute | solution.py:26
  92.0 6.4 %collective-permute-start.16 = (f32[8,128]{1,0:T(8,128)S(1)}, f32[8,128]{1,0:T(8,128)S(1)}, u32[]{:S(2)}, u32[]{:S(2)}) collective-permute-start(f32[8,128]{1,0:T(8,128)S(1)} %reduce_sum.99.sum0), channel_id=1, source_target_pairs={{0,128},{64,192},{128,0},{192,64},{1,129},{65,193},{129,1},{193,65... | collective-permute-start | bytes 12296 | tf_op jit(solution)/shard_map/ppermute | solution.py:26
  92.8 5.6 %collective-permute-start.15 = (f32[8,128]{1,0:T(8,128)S(1)}, f32[8,128]{1,0:T(8,128)S(1)}, u32[]{:S(2)}, u32[]{:S(2)}) collective-permute-start(f32[8,128]{1,0:T(8,128)S(1)} %reduce_sum.99.sum0), channel_id=1, source_target_pairs={{0,64},{64,128},{128,192},{192,0},{1,65},{65,129},{129,193},{193,1... | collective-permute-start | bytes 12296 | tf_op jit(solution)/shard_map/ppermute | solution.py:26

commit v6 on v5

--- a/solution.py
+++ b/solution.py
@@ -26,10 +26,12 @@
     return lax.ppermute(value, axis, [(i, (i + step) % size) for i in range(size)])
 
 
-def pool_kernel(msg0, msg1, msg2, msg3, low, high, out2, out1, out0, sums, pooled):
+def pool_kernel(msg0, msg1, msg2, msg3, cross, inner, out2, out1, out0, sums, pooled):
     cells = out2.shape[1] // FRAMES
     fine = 2 * cells
-    place = lax.axis_index("x")
+    place, c = lax.axis_index("x"), lax.axis_index("c")
+    mine = pl.ds(pl.multiple_of(c * fine, fine), fine)
+    other = pl.ds(pl.multiple_of((1 - c) * fine, fine), fine)
     zero = jnp.zeros((8, 128), jnp.float32)
     for band in range(3):
         sums[band, 0:8] = zero
@@ -38,9 +40,11 @@
         frame = lax.rem(place + FRAMES - k, FRAMES)
         upper = msg[0:fine].astype(jnp.float32)
         lower = msg[fine : 2 * fine].astype(jnp.float32)
-        sums[0, 8 : 8 + fine] = lower + high[k].astype(jnp.float32)
         sums[1, 8 : 8 + fine] = upper + lower
-        sums[2, 8 : 8 + fine] = low[k].astype(jnp.float32) + upper
+        sums[2 - 2 * c, 8 : 8 + fine] = (
+            msg[mine].astype(jnp.float32) + cross[k].astype(jnp.float32)
+        )
+        sums[2 * c, 8 : 8 + fine] = msg[other].astype(jnp.float32) + inner[k].astype(jnp.float32)
         for band in range(3):
             at = sums.at[band]
             before = at[pl.ds(7, cells, stride=2), :]
@@ -72,8 +76,8 @@
         put(out0, 1, p3)
 
 
-def pool(msgs, low, high):
-    cells = low.shape[1] // 2
+def pool(msgs, cross, inner):
+    cells = cross.shape[1] // 2
     shapes = [
         jax.ShapeDtypeStruct((2, len(units) * cells, TAPS * 128), jnp.bfloat16) for units in UNITS
     ]
@@ -88,7 +92,7 @@
         ],
         compiler_params=pltpu.CompilerParams(vmem_limit_bytes=12 << 20),
         cost_estimate=pl.CostEstimate(flops=1_000, bytes_accessed=1_000, transcendentals=0),
-    )(*msgs, low, high)
+    )(*msgs, cross, inner)
 
 
 def split_kernel(cot, out0, out1, out2, out3, sems):
@@ -187,11 +191,12 @@
     )(total, lat)
 
 
-def rims_kernel(msg0, msg1, msg2, msg3, first, last):
+def rims_kernel(msg0, msg1, msg2, msg3, cross, inner):
+    fine = cross.shape[1]
+    c = lax.axis_index("c")
     for k, msg in enumerate((msg0, msg1, msg2, msg3)):
-        fine = first.shape[1]
-        first[k] = msg[0:fine]
-        last[k] = msg[fine : 2 * fine]
+        cross[k] = msg[pl.ds(pl.multiple_of(c * fine, fine), fine)]
+        inner[k] = msg[pl.ds(pl.multiple_of((1 - c) * fine, fine), fine)]
 
 
 def rims(msgs, fine):
@@ -286,7 +291,7 @@
     return normed, sigmoid_pre * (1.0 + pre * (1.0 - sigmoid_pre))
 
 
-def sums_kernel(part0, part1, part2, part3, msg0, msg1, msg2, msg3, chan, out, kept):
+def sums_kernel(part0, part1, part2, part3, msg0, msg1, msg2, msg3, chan, kept):
     cells = part0.shape[1]
     for q in range(4):
         lanes = slice(q * 128, q * 128 + 128)
@@ -300,18 +305,14 @@
             second = second + (act * normed).reshape(cells // 8, 8, 128).sum(axis=0)
         kept[q : q + 1] = jnp.sum(first, axis=0, keepdims=True)
         kept[4 + q : 5 + q] = jnp.sum(second, axis=0, keepdims=True)
-    total = kept[...]
-    for i in range(out.shape[0]):
-        out[i] = total
 
 
 def partial_sums(parts, msgs, chan):
     return pl.pallas_call(
         sums_kernel,
-        out_shape=jax.ShapeDtypeStruct((ROWS, 8, 128), jnp.float32),
+        out_shape=jax.ShapeDtypeStruct((8, 128), jnp.float32),
         in_specs=[VMEM] * 9,
         out_specs=VMEM,
-        scratch_shapes=[pltpu.VMEM((8, 128), jnp.float32)],
         compiler_params=pltpu.CompilerParams(vmem_limit_bytes=4 << 20),
         cost_estimate=pl.CostEstimate(
             flops=6_000_000, bytes_accessed=2_900_000, transcendentals=330_000
@@ -390,9 +391,10 @@
     block, msgs = lax.optimization_barrier((block, msgs))
     pieces = [block] + [send(block, "y", step) for step in range(1, YS)]
     first_rows, last_rows = rims(msgs, cotangent.shape[2])
-    low = lax.ppermute(last_rows, ROW_AXES, [(i, i + 1) for i in range(ROWS - 1)])
-    high = lax.ppermute(first_rows, ROW_AXES, [(i + 1, i) for i in range(ROWS - 1)])
-    lefts = pool(msgs, low, high)
+    pairs = [(i, i + 1) for i in range(1, ROWS - 1, CS)]
+    cross = lax.ppermute(first_rows, ROW_AXES, pairs + [(j, i) for i, j in pairs])
+    inner = send(last_rows, "c", 1)
+    lefts = pool(msgs, cross, inner)
     others = [send(piece, "c", 1) for piece in pieces]
     partial = None
     for steps in ((0, 3), (2, 1)):
@@ -419,7 +421,16 @@
 
     sums = partial_sums(partial, lats, chan)
     parts = [partial[0]] + [send(partial[FRAMES - step], "x", step) for step in range(1, FRAMES)]
-    sums = lax.all_to_all(sums, ROW_AXES, 0, 0, tiled=True).sum(axis=0)
+    sums = sums + send(sums, "c", 1)
+    sums = jnp.broadcast_to(sums[None], (YS * ZS, 8, 128))
+    sums = lax.all_to_all(
+        sums,
+        ROW_AXES,
+        0,
+        0,
+        axis_index_groups=[list(range(0, ROWS, CS)), list(range(ROWS - 1, 0, -CS))],
+        tiled=True,
+    ).sum(axis=0)
     sums = [sums] + [send(sums, "x", step) for step in range(1, FRAMES)]
     latent_grad, gain_grad, bias_grad = final(cell_count, sums, parts, own, chan)
     return (latent_grad.reshape(1, 1, cells, channels), gain_grad, bias_grad)

time: 101 us -> 99.9 us (0.989); the launches traced: 99.4 us -> 99.5 us
  blocking collectives: 0 us -> 17.6 us
  waiting for transfers between devices: 39.9 us -> 30.9 us
  starting transfers between devices: 43.4 us -> 35.5 us
    all_to_all x0 -> x1, blocking collectives: none -> 17.6 us  [on_device(): lax.all_to_all(sums, ROW_AXES, 0, 0, axis_index_groups=[list(range(0, ROW...]
    all_to_all x1 -> x0, waiting for transfers between devices: 9.45 us -> none  [on_device(): sums = lax.all_to_all(sums, ROW_AXES, 0, 0, tiled=True).sum(axis=0)]
    all_to_all x1 -> x0, starting transfers between devices: 8.71 us -> none  [on_device(): sums = lax.all_to_all(sums, ROW_AXES, 0, 0, tiled=True).sum(axis=0)]
    ppermute x19 -> x21, starting transfers between devices: 20.7 us -> 24.9 us  [send(): lax.ppermute(value, axis, [(i, (i + step) % size) for i in range(size)])]
    ppermute x2 -> x1, starting transfers between devices: 5.27 us -> 1.92 us  [on_device(): lax.ppermute(first_rows, ROW_AXES, pairs + [(j, i) for i, j in pairs])]
    ppermute x2 -> x1, waiting for transfers between devices: 0.82 us -> 3.63 us  [on_device(): lax.ppermute(first_rows, ROW_AXES, pairs + [(j, i) for i, j in pairs])]
    ppermute x19 -> x21, waiting for transfers between devices: 28.9 us -> 26.5 us  [send(): lax.ppermute(value, axis, [(i, (i + step) % size) for i in range(size)])]
  transfers between devices with their start and end apart: 23 -> 23, of which waited for: 13 -> 12; matrix products, arithmetic and copies ran while one was open for 0% -> 1% of each run, Pallas kernels for 8% -> 9%
where the time goes in v6:
time: 99.9 us; the launch traced here: 99.5 us
  starting transfers between devices  35.5 us (36%)
  waiting for transfers between devices  30.9 us (31%)
  blocking collectives  17.6 us (18%)
  Pallas kernels  11 us (11%)
  local copies, waits for them, and re-layouts  3.23 us (3%)
    ppermute x21, waiting for transfers between devices, send(): lax.ppermute(value, axis, [(i, (i + step) % size) for i in range(size)])  26.5 us
    ppermute x21, starting transfers between devices, send(): lax.ppermute(value, axis, [(i, (i + step) % size) for i in range(size)])  24.9 us
    all_to_all x1, blocking collectives, on_device(): lax.all_to_all(sums, ROW_AXES, 0, 0, axis_index_groups=[list(range(0, ROW...  17.6 us
    all_to_all x1, starting transfers between devices, on_device(): lax.all_to_all(message(latent, conv_weight.reshape(PLANES, 8, 128)), ('z'...  8.71 us
    pallas_call x2, Pallas kernels, product(): pl.pallas_call(functools.partial(product_kernel, steps, aliased), out_sha...  6.19 us
    ppermute x1, waiting for transfers between devices, on_device(): lax.ppermute(first_rows, ROW_AXES, pairs + [(j, i) for i, j in pairs])  3.63 us
    unnamed x12, local copies, waits for them, and re-layouts  2.83 us
  transfers between devices with their start and end apart: 23, of which 12 were waited for; matrix products, arithmetic and copies ran while one was open for 1% of the time, Pallas kernels for 9%

profile of v6, /device:TPU:32, one launch (start us, length us, event | category | flops | bytes accessed | tf_op | source)
XLA Modules:
  0.0 99.5 jit_solution(13084870257183398944)
XLA Ops:
  0.6 0.9 copy-done
  1.6 0.8 copy-done.3
  2.4 1.2 %shard_map.76 = bf16[8,30,8,128]{3,2,1,0:T(8,128)(2,1)} custom-call(bf16[1,1,160,512]{3,2,1,0:T(8,128)(2,1)S(1)} %copy-done, bf16[27,8,128]{2,1,0:T(8,128)(2,1)S(1)} %bitcast.17), custom_call_target="tpu_custom_call" | custom-call | flops 250000 | bytes 720000 | tf_op jit(solution)/shard_map/pallas_call | solution.py:156
  3.5 8.7 %all-to-all-start = ((bf16[8,30,8,128]{3,2,1,0:T(8,128)(2,1)}), bf16[8,30,8,128]{3,2,1,0:T(8,128)(2,1)S(1)}, u32[]{:S(2)}, u32[]{:S(2)}) async-start(bf16[8,30,8,128]{3,2,1,0:T(8,128)(2,1)} %shard_map.76), calls=%async_computation | async-start | bytes 983040 | tf_op jit(solution)/shard_map/all_to_all | solution.py:375
  12.3 1.1 %copy-done.2 = bf16[1,2,320,512]{3,2,1,0:T(8,128)(2,1)S(1)} copy-done((bf16[1,2,320,512]{3,2,1,0:T(8,128)(2,1)S(1)}, bf16[1,2,320,512]{3,2,1,0:T(8,128)(2,1)}, u32[]{:S(2)}) %copy-start.2) | copy-done | bytes 655384
  13.6 1.6 %collective-permute-start = (bf16[640,128]{1,0:T(8,128)(2,1)S(1)}, bf16[640,128]{1,0:T(8,128)(2,1)S(1)}, u32[]{:S(2)}, u32[]{:S(2)}) collective-permute-start(bf16[640,128]{1,0:T(8,128)(2,1)S(1)} %get-tuple-element.29), channel_id=1, source_target_pairs={{0,64},{64,128},{128,192},{192,0},{1,65},{65,129},{129,193},{193,1... | collective-permute-start | bytes 491528 | tf_op jit(solution)/shard_map/ppermute | solution.py:26
  15.1 2.7 %collective-permute-start.1 = (bf16[640,128]{1,0:T(8,128)(2,1)S(1)}, bf16[640,128]{1,0:T(8,128)(2,1)S(1)}, u32[]{:S(2)}, u32[]{:S(2)}) collective-permute-start(bf16[640,128]{1,0:T(8,128)(2,1)S(1)} %get-tuple-element.30), channel_id=1, source_target_pairs={{0,128},{64,192},{128,0},{192,64},{1,129},{65,193},{129,1},{193,65... | collective-permute-start | bytes 491528 | tf_op jit(solution)/shard_map/ppermute | solution.py:26
  17.9 1.4 %collective-permute-start.2 = (bf16[640,128]{1,0:T(8,128)(2,1)S(1)}, bf16[640,128]{1,0:T(8,128)(2,1)S(1)}, u32[]{:S(2)}, u32[]{:S(2)}) collective-permute-start(bf16[640,128]{1,0:T(8,128)(2,1)S(1)} %get-tuple-element.31), channel_id=1, source_target_pairs={{0,192},{64,0},{128,64},{192,128},{1,193},{65,1},{129,65},{193,129... | collective-permute-start | bytes 491528 | tf_op jit(solution)/shard_map/ppermute | solution.py:26
  19.3 1.7 %collective-permute-done.msg1 = bf16[640,128]{1,0:T(8,128)(2,1)S(1)} collective-permute-done((bf16[640,128]{1,0:T(8,128)(2,1)S(1)}, bf16[640,128]{1,0:T(8,128)(2,1)S(1)}, u32[]{:S(2)}, u32[]{:S(2)}) %collective-permute-start) | collective-permute-done | bytes 163872 | tf_op jit(solution)/shard_map/ppermute | solution.py:26
  21.0 4.3 %collective-permute-done.1.msg2 = bf16[640,128]{1,0:T(8,128)(2,1)S(1)} collective-permute-done((bf16[640,128]{1,0:T(8,128)(2,1)S(1)}, bf16[640,128]{1,0:T(8,128)(2,1)S(1)}, u32[]{:S(2)}, u32[]{:S(2)}) %collective-permute-start.1) | collective-permute-done | bytes 163872 | tf_op jit(solution)/shard_map/ppermute | solution.py:26
  25.3 0.7 all-to-all-done.refs_0_
  26.0 3.0 %collective-permute-start.10 = (bf16[8,30,8,128]{3,2,1,0:T(8,128)(2,1)S(1)}, bf16[8,30,8,128]{3,2,1,0:T(8,128)(2,1)S(1)}, u32[]{:S(2)}, u32[]{:S(2)}) collective-permute-start(bf16[8,30,8,128]{3,2,1,0:T(8,128)(2,1)S(1)} %all-to-all-done.refs_0_), channel_id=1, source_target_pairs={{0,48},{16,0},{32,16},{48,32},{1,49},{17,1},{33,17},{49,33},{2,50}... | collective-permute-start | bytes 1474568 | tf_op jit(solution)/shard_map/ppermute | solution.py:26
  29.1 1.9 %collective-permute-start.7 = (bf16[4,320,128]{2,1,0:T(8,128)(2,1)S(1)}, bf16[4,320,128]{2,1,0:T(8,128)(2,1)S(1)}, u32[]{:S(2)}, u32[]{:S(2)}) collective-permute-start(bf16[4,320,128]{2,1,0:T(8,128)(2,1)S(1)} %get-tuple-element.37), channel_id=1, source_target_pairs={{1,2},{3,4},{5,6},{7,8},{9,10},{11,12},{13,14},{15,16},{17,18},{19... | collective-permute-start | bytes 983048 | tf_op jit(solution)/shard_map/ppermute | solution.py:395
  31.0 2.3 %collective-permute-start.3 = (bf16[8,30,8,128]{3,2,1,0:T(8,128)(2,1)S(1)}, bf16[8,30,8,128]{3,2,1,0:T(8,128)(2,1)S(1)}, u32[]{:S(2)}, u32[]{:S(2)}) collective-permute-start(bf16[8,30,8,128]{3,2,1,0:T(8,128)(2,1)S(1)} %all-to-all-done.refs_0_), channel_id=1, source_target_pairs={{0,32},{16,48},{32,0},{48,16},{1,33},{17,49},{33,1},{49,17},{2,34}... | collective-permute-start | bytes 1474568 | tf_op jit(solution)/shard_map/ppermute | solution.py:26
  33.8 3.6 %collective-permute-done.7.cross = bf16[4,320,128]{2,1,0:T(8,128)(2,1)S(1)} collective-permute-done((bf16[4,320,128]{2,1,0:T(8,128)(2,1)S(1)}, bf16[4,320,128]{2,1,0:T(8,128)(2,1)S(1)}, u32[]{:S(2)}, u32[]{:S(2)}) %collective-permute-start.7) | collective-permute-done | bytes 327712 | tf_op jit(solution)/shard_map/ppermute | solution.py:395
  37.5 10.9 %collective-permute-done.10.refs_2_ = bf16[8,30,8,128]{3,2,1,0:T(8,128)(2,1)S(1)} collective-permute-done((bf16[8,30,8,128]{3,2,1,0:T(8,128)(2,1)S(1)}, bf16[8,30,8,128]{3,2,1,0:T(8,128)(2,1)S(1)}, u32[]{:S(2)}, u32[]{:S(2)}) %collective-permute-start.10) | collective-permute-done | bytes 491552 | tf_op jit(solution)/shard_map/ppermute | solution.py:26
  48.4 1.5 %shard_map.79 = (bf16[2,640,1152]{2,1,0:T(8,128)(2,1)S(1)}, bf16[2,480,1152]{2,1,0:T(8,128)(2,1)S(1)}, bf16[2,320,1152]{2,1,0:T(8,128)(2,1)S(1)}) custom-call(bf16[640,128]{1,0:T(8,128)(2,1)S(1)} %get-tuple-element.33.msg0, bf16[640,128]{1,0:T(8,128)(2,1)S(1)} %collective-permute-done.msg1, bf16[640,128]{1,0:T(8,128)(2,1)S(1)} %collective-permute-done.1.msg2, ...), custom_call_target="tpu_custom_call" | custom-call | flops 1000 | bytes 1000 | tf_op jit(solution)/shard_map/pallas_call | solution.py:84
  49.9 1.9 %collective-permute-done.5.refs_2_ = bf16[8,30,8,128]{3,2,1,0:T(8,128)(2,1)S(1)} collective-permute-done((bf16[8,30,8,128]{3,2,1,0:T(8,128)(2,1)S(1)}, bf16[8,30,8,128]{3,2,1,0:T(8,128)(2,1)S(1)}, u32[]{:S(2)}, u32[]{:S(2)}) %collective-permute-start.5) | collective-permute-done | bytes 491552 | tf_op jit(solution)/shard_map/ppermute | solution.py:26
  52.5 1.1 %collective-permute-done.6.refs_3_ = bf16[8,30,8,128]{3,2,1,0:T(8,128)(2,1)S(1)} collective-permute-done((bf16[8,30,8,128]{3,2,1,0:T(8,128)(2,1)S(1)}, bf16[8,30,8,128]{3,2,1,0:T(8,128)(2,1)S(1)}, u32[]{:S(2)}, u32[]{:S(2)}) %collective-permute-start.6) | collective-permute-done | bytes 491552 | tf_op jit(solution)/shard_map/ppermute | solution.py:26
  54.5 2.7 %collective-permute-start.14 = (bf16[688,128]{1,0:T(8,128)(2,1)S(1)}, bf16[688,128]{1,0:T(8,128)(2,1)S(1)}, u32[]{:S(2)}, u32[]{:S(2)}) collective-permute-start(bf16[688,128]{1,0:T(8,128)(2,1)S(1)} %shard_map.82.msg0), channel_id=1, source_target_pairs={{0,192},{64,0},{128,64},{192,128},{1,193},{65,1},{129,65},{193,129... | collective-permute-start | bytes 528392 | tf_op jit(solution)/shard_map/ppermute | solution.py:26
  57.2 1.1 %collective-permute-start.13 = (bf16[688,128]{1,0:T(8,128)(2,1)S(1)}, bf16[688,128]{1,0:T(8,128)(2,1)S(1)}, u32[]{:S(2)}, u32[]{:S(2)}) collective-permute-start(bf16[688,128]{1,0:T(8,128)(2,1)S(1)} %shard_map.82.msg0), channel_id=1, source_target_pairs={{0,128},{64,192},{128,0},{192,64},{1,129},{65,193},{129,1},{193,65... | collective-permute-start | bytes 528392 | tf_op jit(solution)/shard_map/ppermute | solution.py:26
  58.9 3.1 %shard_map.80 = (f32[4,160,128]{2,1,0:T(8,128)S(1)}, f32[4,160,128]{2,1,0:T(8,128)S(1)}, f32[4,160,128]{2,1,0:T(8,128)S(1)}, f32[4,160,128]{2,1,0:T(8,128)S(1)}) custom-call(bf16[8,30,8,128]{3,2,1,0:T(8,128)(2,1)S(1)} %all-to-all-done.refs_0_, bf16[8,30,8,128]{3,2,1,0:T(8,128)(2,1)S(1)} %collective-permute-done.9.refs_1_, ...), custom_call_target="tpu_custom_call" | custom-call | flops 1700000000 | bytes 9000000 | tf_op jit(solution)/shard_map/pallas_call | solution.py:267
  62.0 3.1 %shard_map.81 = (f32[4,160,128]{2,1,0:T(8,128)S(1)}, f32[4,160,128]{2,1,0:T(8,128)S(1)}, f32[4,160,128]{2,1,0:T(8,128)S(1)}, f32[4,160,128]{2,1,0:T(8,128)S(1)}) custom-call(bf16[8,30,8,128]{3,2,1,0:T(8,128)(2,1)S(1)} %collective-permute-done.3.refs_0_, ...), custom_call_target="tpu_custom_call", output_to_operand_aliasing={{0}: (7, {}), {1}: (8, {}), {2}: (9, {}), {3}: (10, {})} | custom-call | flops 1700000000 | bytes 9000000 | tf_op jit(solution)/shard_map/pallas_call | solution.py:267
  65.1 2.7 %collective-permute-start.21 = (f32[4,160,128]{2,1,0:T(8,128)S(1)}, f32[4,160,128]{2,1,0:T(8,128)S(1)}, u32[]{:S(2)}, u32[]{:S(2)}) collective-permute-start(f32[4,160,128]{2,1,0:T(8,128)S(1)} %get-tuple-element.47.part1), channel_id=1, source_target_pairs={{0,192},{64,0},{128,64},{192,128},{1,193},{65,1},{129,65},{193,129... | collective-permute-start | bytes 983048 | tf_op jit(solution)/shard_map/ppermute | solution.py:26
  67.8 1.2 %collective-permute-start.20 = (f32[4,160,128]{2,1,0:T(8,128)S(1)}, f32[4,160,128]{2,1,0:T(8,128)S(1)}, u32[]{:S(2)}, u32[]{:S(2)}) collective-permute-start(f32[4,160,128]{2,1,0:T(8,128)S(1)} %get-tuple-element.48.part2), channel_id=1, source_target_pairs={{0,128},{64,192},{128,0},{192,64},{1,129},{65,193},{129,1},{193,65... | collective-permute-start | bytes 983048 | tf_op jit(solution)/shard_map/ppermute | solution.py:26
  69.6 0.8 shard_map.83
  70.5 1.2 %collective-permute-done.15 = f32[8,128]{1,0:T(8,128)S(1)} collective-permute-done((f32[8,128]{1,0:T(8,128)S(1)}, f32[8,128]{1,0:T(8,128)S(1)}, u32[]{:S(2)}, u32[]{:S(2)}) %collective-permute-start.15) | collective-permute-done | bytes 4128 | tf_op jit(solution)/shard_map/ppermute | solution.py:26
  71.7 17.6 %all_to_all.10 = f32[32,8,128]{2,1,0:T(8,128)S(1)} all-to-all(f32[32,8,128]{2,1,0:T(8,128)S(1)} %broadcast_in_dim.14), channel_id=1, replica_groups={{0,2,4,6,8,10,12,14,16,18,20,22,24,26,28,30,32,34,36,38,40,42,44,46,48,..., dimensions={0} | all-to-all | bytes 262144 | tf_op jit(solution)/shard_map/all_to_all | solution.py:426
  89.4 3.3 %collective-permute-start.18 = (f32[8,128]{1,0:T(8,128)S(1)}, f32[8,128]{1,0:T(8,128)S(1)}, u32[]{:S(2)}, u32[]{:S(2)}) collective-permute-start(f32[8,128]{1,0:T(8,128)S(1)} %reduce_sum.99.sum0), channel_id=1, source_target_pairs={{0,192},{64,0},{128,64},{192,128},{1,193},{65,1},{129,65},{193,129... | collective-permute-start | bytes 12296 | tf_op jit(solution)/shard_map/ppermute | solution.py:26
  92.7 0.9 collective-permute-start.17
  94.0 3.8 %collective-permute-done.17.sum2 = f32[8,128]{1,0:T(8,128)S(1)} collective-permute-done((f32[8,128]{1,0:T(8,128)S(1)}, f32[8,128]{1,0:T(8,128)S(1)}, u32[]{:S(2)}, u32[]{:S(2)}) %collective-permute-start.17) | collective-permute-done | bytes 4128 | tf_op jit(solution)/shard_map/ppermute | solution.py:26
  98.4 1.1 %shard_map.84 = (f32[160,512]{1,0:T(8,128)}, f32[512]{0:T(512)}, f32[512]{0:T(512)}) custom-call(f32[8,128]{1,0:T(8,128)S(1)} %reduce_sum.99.sum0, f32[8,128]{1,0:T(8,128)S(1)} %collective-permute-done.16.sum1, f32[8,128]{1,0:T(8,128)S(1)} %collective-permute-done.17.sum2, f32[8,128]{1,0:T(8,128)S(1)} %collective-permute-done.18.sum3, ...), custom_call_target="tpu_custom_call" | custom-call | flops 2000000 | bytes 1900000 | tf_op jit(solution)/shard_map/pallas_call | solution.py:353
  (59 shorter events, 4.7 us)
Async XLA Ops:
  0.6 0.9 copy-start
  1.5 0.8 copy-start.3
  3.5 50.9 %copy-start.1 = (bf16[1,1,160,512]{3,2,1,0:T(8,128)(2,1)S(1)}, bf16[1,1,160,512]{3,2,1,0:T(8,128)(2,1)}, u32[]{:S(2)}) copy-start(bf16[1,1,160,512]{3,2,1,0:T(8,128)(2,1)} %lat.1) | copy-start | bytes 491524
  3.5 22.4 %all-to-all-start = ((bf16[8,30,8,128]{3,2,1,0:T(8,128)(2,1)}), bf16[8,30,8,128]{3,2,1,0:T(8,128)(2,1)S(1)}, u32[]{:S(2)}, u32[]{:S(2)}) async-start(bf16[8,30,8,128]{3,2,1,0:T(8,128)(2,1)} %shard_map.76), calls=%async_computation | async-start | bytes 983040 | tf_op jit(solution)/shard_map/all_to_all | solution.py:375
  12.3 1.1 %copy-start.2 = (bf16[1,2,320,512]{3,2,1,0:T(8,128)(2,1)S(1)}, bf16[1,2,320,512]{3,2,1,0:T(8,128)(2,1)}, u32[]{:S(2)}) copy-start(bf16[1,2,320,512]{3,2,1,0:T(8,128)(2,1)} %cot.1) | copy-start | bytes 1966084
  13.6 7.4 %collective-permute-start = (bf16[640,128]{1,0:T(8,128)(2,1)S(1)}, bf16[640,128]{1,0:T(8,128)(2,1)S(1)}, u32[]{:S(2)}, u32[]{:S(2)}) collective-permute-start(bf16[640,128]{1,0:T(8,128)(2,1)S(1)} %get-tuple-element.29), channel_id=1, source_target_pairs={{0,64},{64,128},{128,192},{192,0},{1,65},{65,129},{129,193},{193,1... | collective-permute-start | bytes 491528 | tf_op jit(solution)/shard_map/ppermute | solution.py:26
  15.1 10.1 %collective-permute-start.1 = (bf16[640,128]{1,0:T(8,128)(2,1)S(1)}, bf16[640,128]{1,0:T(8,128)(2,1)S(1)}, u32[]{:S(2)}, u32[]{:S(2)}) collective-permute-start(bf16[640,128]{1,0:T(8,128)(2,1)S(1)} %get-tuple-element.30), channel_id=1, source_target_pairs={{0,128},{64,192},{128,0},{192,64},{1,129},{65,193},{129,1},{193,65... | collective-permute-start | bytes 491528 | tf_op jit(solution)/shard_map/ppermute | solution.py:26
  17.9 7.4 %collective-permute-start.2 = (bf16[640,128]{1,0:T(8,128)(2,1)S(1)}, bf16[640,128]{1,0:T(8,128)(2,1)S(1)}, u32[]{:S(2)}, u32[]{:S(2)}) collective-permute-start(bf16[640,128]{1,0:T(8,128)(2,1)S(1)} %get-tuple-element.31), channel_id=1, source_target_pairs={{0,192},{64,0},{128,64},{192,128},{1,193},{65,1},{129,65},{193,129... | collective-permute-start | bytes 491528 | tf_op jit(solution)/shard_map/ppermute | solution.py:26
  26.0 22.4 %collective-permute-start.10 = (bf16[8,30,8,128]{3,2,1,0:T(8,128)(2,1)S(1)}, bf16[8,30,8,128]{3,2,1,0:T(8,128)(2,1)S(1)}, u32[]{:S(2)}, u32[]{:S(2)}) collective-permute-start(bf16[8,30,8,128]{3,2,1,0:T(8,128)(2,1)S(1)} %all-to-all-done.refs_0_), channel_id=1, source_target_pairs={{0,48},{16,0},{32,16},{48,32},{1,49},{17,1},{33,17},{49,33},{2,50}... | collective-permute-start | bytes 1474568 | tf_op jit(solution)/shard_map/ppermute | solution.py:26
  29.0 22.8 %collective-permute-start.5 = (bf16[8,30,8,128]{3,2,1,0:T(8,128)(2,1)S(1)}, bf16[8,30,8,128]{3,2,1,0:T(8,128)(2,1)S(1)}, u32[]{:S(2)}, u32[]{:S(2)}) collective-permute-start(bf16[8,30,8,128]{3,2,1,0:T(8,128)(2,1)S(1)} %all-to-all-done.refs_0_), channel_id=1, source_target_pairs={{0,16},{16,32},{32,48},{48,0},{1,17},{17,33},{33,49},{49,1},{2,18}... | collective-permute-start | bytes 1474568 | tf_op jit(solution)/shard_map/ppermute | solution.py:26
  29.1 8.4 %collective-permute-start.7 = (bf16[4,320,128]{2,1,0:T(8,128)(2,1)S(1)}, bf16[4,320,128]{2,1,0:T(8,128)(2,1)S(1)}, u32[]{:S(2)}, u32[]{:S(2)}) collective-permute-start(bf16[4,320,128]{2,1,0:T(8,128)(2,1)S(1)} %get-tuple-element.37), channel_id=1, source_target_pairs={{1,2},{3,4},{5,6},{7,8},{9,10},{11,12},{13,14},{15,16},{17,18},{19... | collective-permute-start | bytes 983048 | tf_op jit(solution)/shard_map/ppermute | solution.py:395
  31.0 20.8 %collective-permute-start.3 = (bf16[8,30,8,128]{3,2,1,0:T(8,128)(2,1)S(1)}, bf16[8,30,8,128]{3,2,1,0:T(8,128)(2,1)S(1)}, u32[]{:S(2)}, u32[]{:S(2)}) collective-permute-start(bf16[8,30,8,128]{3,2,1,0:T(8,128)(2,1)S(1)} %all-to-all-done.refs_0_), channel_id=1, source_target_pairs={{0,32},{16,48},{32,0},{48,16},{1,33},{17,49},{33,1},{49,17},{2,34}... | collective-permute-start | bytes 1474568 | tf_op jit(solution)/shard_map/ppermute | solution.py:26
  33.3 15.1 %collective-permute-start.8 = (bf16[4,320,128]{2,1,0:T(8,128)(2,1)S(1)}, bf16[4,320,128]{2,1,0:T(8,128)(2,1)S(1)}, u32[]{:S(2)}, u32[]{:S(2)}) collective-permute-start(bf16[4,320,128]{2,1,0:T(8,128)(2,1)S(1)} %get-tuple-element.38), channel_id=1, source_target_pairs={{0,1},{1,0},{2,3},{3,2},{4,5},{5,4},{6,7},{7,6},{8,9},{9,8},{10,11... | collective-permute-start | bytes 983048 | tf_op jit(solution)/shard_map/ppermute | solution.py:26
  37.5 15.0 %collective-permute-start.9 = (bf16[8,30,8,128]{3,2,1,0:T(8,128)(2,1)S(1)}, bf16[8,30,8,128]{3,2,1,0:T(8,128)(2,1)S(1)}, u32[]{:S(2)}, u32[]{:S(2)}) collective-permute-start(bf16[8,30,8,128]{3,2,1,0:T(8,128)(2,1)S(1)} %all-to-all-done.refs_0_), channel_id=1, source_target_pairs={{0,1},{1,0},{2,3},{3,2},{4,5},{5,4},{6,7},{7,6},{8,9},{9,8},{10,11... | collective-permute-start | bytes 1474568 | tf_op jit(solution)/shard_map/ppermute | solution.py:26
  48.4 4.1 %collective-permute-start.11 = (bf16[8,30,8,128]{3,2,1,0:T(8,128)(2,1)S(1)}, bf16[8,30,8,128]{3,2,1,0:T(8,128)(2,1)S(1)}, u32[]{:S(2)}, u32[]{:S(2)}) collective-permute-start(bf16[8,30,8,128]{3,2,1,0:T(8,128)(2,1)S(1)} %collective-permute-done.10.refs_2_), channel_id=1, source_target_pairs={{0,1},{1,0},{2,3},{3,2},{4,5},{5,4},{6,7},{7,6},{8,9},{9,8},{10,11... | collective-permute-start | bytes 1474568 | tf_op jit(solution)/shard_map/ppermute | solution.py:26
  51.8 1.9 %collective-permute-start.6 = (bf16[8,30,8,128]{3,2,1,0:T(8,128)(2,1)S(1)}, bf16[8,30,8,128]{3,2,1,0:T(8,128)(2,1)S(1)}, u32[]{:S(2)}, u32[]{:S(2)}) collective-permute-start(bf16[8,30,8,128]{3,2,1,0:T(8,128)(2,1)S(1)} %collective-permute-done.5.refs_2_), channel_id=1, source_target_pairs={{0,1},{1,0},{2,3},{3,2},{4,5},{5,4},{6,7},{7,6},{8,9},{9,8},{10,11... | collective-permute-start | bytes 1474568 | tf_op jit(solution)/shard_map/ppermute | solution.py:26
  51.8 2.5 %collective-permute-start.4 = (bf16[8,30,8,128]{3,2,1,0:T(8,128)(2,1)S(1)}, bf16[8,30,8,128]{3,2,1,0:T(8,128)(2,1)S(1)}, u32[]{:S(2)}, u32[]{:S(2)}) collective-permute-start(bf16[8,30,8,128]{3,2,1,0:T(8,128)(2,1)S(1)} %collective-permute-done.3.refs_0_), channel_id=1, source_target_pairs={{0,1},{1,0},{2,3},{3,2},{4,5},{5,4},{6,7},{7,6},{8,9},{9,8},{10,11... | collective-permute-start | bytes 1474568 | tf_op jit(solution)/shard_map/ppermute | solution.py:26
  54.5 14.6 %collective-permute-start.14 = (bf16[688,128]{1,0:T(8,128)(2,1)S(1)}, bf16[688,128]{1,0:T(8,128)(2,1)S(1)}, u32[]{:S(2)}, u32[]{:S(2)}) collective-permute-start(bf16[688,128]{1,0:T(8,128)(2,1)S(1)} %shard_map.82.msg0), channel_id=1, source_target_pairs={{0,192},{64,0},{128,64},{192,128},{1,193},{65,1},{129,65},{193,129... | collective-permute-start | bytes 528392 | tf_op jit(solution)/shard_map/ppermute | solution.py:26
  57.2 11.9 %collective-permute-start.13 = (bf16[688,128]{1,0:T(8,128)(2,1)S(1)}, bf16[688,128]{1,0:T(8,128)(2,1)S(1)}, u32[]{:S(2)}, u32[]{:S(2)}) collective-permute-start(bf16[688,128]{1,0:T(8,128)(2,1)S(1)} %shard_map.82.msg0), channel_id=1, source_target_pairs={{0,128},{64,192},{128,0},{192,64},{1,129},{65,193},{129,1},{193,65... | collective-permute-start | bytes 528392 | tf_op jit(solution)/shard_map/ppermute | solution.py:26
  58.3 10.8 %collective-permute-start.12 = (bf16[688,128]{1,0:T(8,128)(2,1)S(1)}, bf16[688,128]{1,0:T(8,128)(2,1)S(1)}, u32[]{:S(2)}, u32[]{:S(2)}) collective-permute-start(bf16[688,128]{1,0:T(8,128)(2,1)S(1)} %shard_map.82.msg0), channel_id=1, source_target_pairs={{0,64},{64,128},{128,192},{192,0},{1,65},{65,129},{129,193},{193,1... | collective-permute-start | bytes 528392 | tf_op jit(solution)/shard_map/ppermute | solution.py:26
  62.0 7.6 %copy-start.4 = (f32[512]{0:T(512)S(1)}, f32[512]{0:T(512)}, u32[]{:S(2)}) copy-start(f32[512]{0:T(512)} %param.7) | copy-start | bytes 6148
  62.0 7.6 %copy-start.5 = (f32[512]{0:T(512)S(1)}, f32[512]{0:T(512)}, u32[]{:S(2)}) copy-start(f32[512]{0:T(512)} %param.6) | copy-start | bytes 6148
  65.1 28.5 %collective-permute-start.21 = (f32[4,160,128]{2,1,0:T(8,128)S(1)}, f32[4,160,128]{2,1,0:T(8,128)S(1)}, u32[]{:S(2)}, u32[]{:S(2)}) collective-permute-start(f32[4,160,128]{2,1,0:T(8,128)S(1)} %get-tuple-element.47.part1), channel_id=1, source_target_pairs={{0,192},{64,0},{128,64},{192,128},{1,193},{65,1},{129,65},{193,129... | collective-permute-start | bytes 983048 | tf_op jit(solution)/shard_map/ppermute | solution.py:26
  67.8 25.8 %collective-permute-start.20 = (f32[4,160,128]{2,1,0:T(8,128)S(1)}, f32[4,160,128]{2,1,0:T(8,128)S(1)}, u32[]{:S(2)}, u32[]{:S(2)}) collective-permute-start(f32[4,160,128]{2,1,0:T(8,128)S(1)} %get-tuple-element.48.part2), channel_id=1, source_target_pairs={{0,128},{64,192},{128,0},{192,64},{1,129},{65,193},{129,1},{193,65... | collective-permute-start | bytes 983048 | tf_op jit(solution)/shard_map/ppermute | solution.py:26
  69.1 24.6 %collective-permute-start.19 = (f32[4,160,128]{2,1,0:T(8,128)S(1)}, f32[4,160,128]{2,1,0:T(8,128)S(1)}, u32[]{:S(2)}, u32[]{:S(2)}) collective-permute-start(f32[4,160,128]{2,1,0:T(8,128)S(1)} %get-tuple-element.49.part3), channel_id=1, source_target_pairs={{0,64},{64,128},{128,192},{192,0},{1,65},{65,129},{129,193},{193,1... | collective-permute-start | bytes 983048 | tf_op jit(solution)/shard_map/ppermute | solution.py:26
  70.5 1.3 %collective-permute-start.15 = (f32[8,128]{1,0:T(8,128)S(1)}, f32[8,128]{1,0:T(8,128)S(1)}, u32[]{:S(2)}, u32[]{:S(2)}) collective-permute-start(f32[8,128]{1,0:T(8,128)S(1)} %shard_map.83), channel_id=1, source_target_pairs={{0,1},{1,0},{2,3},{3,2},{4,5},{5,4},{6,7},{7,6},{8,9},{9,8},{10,11... | collective-permute-start | bytes 12296 | tf_op jit(solution)/shard_map/ppermute | solution.py:26
  89.4 4.6 %collective-permute-start.18 = (f32[8,128]{1,0:T(8,128)S(1)}, f32[8,128]{1,0:T(8,128)S(1)}, u32[]{:S(2)}, u32[]{:S(2)}) collective-permute-start(f32[8,128]{1,0:T(8,128)S(1)} %reduce_sum.99.sum0), channel_id=1, source_target_pairs={{0,192},{64,0},{128,64},{192,128},{1,193},{65,1},{129,65},{193,129... | collective-permute-start | bytes 12296 | tf_op jit(solution)/shard_map/ppermute | solution.py:26
  92.7 5.1 %collective-permute-start.17 = (f32[8,128]{1,0:T(8,128)S(1)}, f32[8,128]{1,0:T(8,128)S(1)}, u32[]{:S(2)}, u32[]{:S(2)}) collective-permute-start(f32[8,128]{1,0:T(8,128)S(1)} %reduce_sum.99.sum0), channel_id=1, source_target_pairs={{0,128},{64,192},{128,0},{192,64},{1,129},{65,193},{129,1},{193,65... | collective-permute-start | bytes 12296 | tf_op jit(solution)/shard_map/ppermute | solution.py:26
  93.6 4.8 %collective-permute-start.16 = (f32[8,128]{1,0:T(8,128)S(1)}, f32[8,128]{1,0:T(8,128)S(1)}, u32[]{:S(2)}, u32[]{:S(2)}) collective-permute-start(f32[8,128]{1,0:T(8,128)S(1)} %reduce_sum.99.sum0), channel_id=1, source_target_pairs={{0,64},{64,128},{128,192},{192,0},{1,65},{65,129},{129,193},{193,1... | collective-permute-start | bytes 12296 | tf_op jit(solution)/shard_map/ppermute | solution.py:26

commit v7 on v6

--- a/solution.py
+++ b/solution.py
@@ -164,7 +164,7 @@
             pltpu.VMEM(weight.shape, weight.dtype),
             pltpu.SemaphoreType.DMA((2,)),
         ],
-        compiler_params=pltpu.CompilerParams(vmem_limit_bytes=3 << 20),
+        compiler_params=pltpu.CompilerParams(vmem_limit_bytes=59 << 20),
         cost_estimate=pl.CostEstimate(flops=250_000, bytes_accessed=720_000, transcendentals=0),
     )(latent, weight)
 

time: 99.9 us -> 98.8 us (0.989)
  local copies, waits for them, and re-layouts: 3.23 us -> 1.51 us
    unnamed x12 -> x8, local copies, waits for them, and re-layouts: 2.83 us -> 1.11 us
where the time goes in v7:
time: 98.8 us; the launch traced here: 98.5 us
  starting transfers between devices  35.5 us (36%)
  waiting for transfers between devices  30.8 us (31%)
  blocking collectives  17.7 us (18%)
  Pallas kernels  11.7 us (12%)
  local copies, waits for them, and re-layouts  1.51 us (2%)
    ppermute x21, waiting for transfers between devices, send(): lax.ppermute(value, axis, [(i, (i + step) % size) for i in range(size)])  26.5 us
    ppermute x21, starting transfers between devices, send(): lax.ppermute(value, axis, [(i, (i + step) % size) for i in range(size)])  24.9 us
    all_to_all x1, blocking collectives, on_device(): lax.all_to_all(sums, ROW_AXES, 0, 0, axis_index_groups=[list(range(0, ROW...  17.7 us
    all_to_all x1, starting transfers between devices, on_device(): lax.all_to_all(message(latent, conv_weight.reshape(PLANES, 8, 128)), ('z'...  8.71 us
    pallas_call x2, Pallas kernels, product(): pl.pallas_call(functools.partial(product_kernel, steps, aliased), out_sha...  6.19 us
    ppermute x1, waiting for transfers between devices, on_device(): lax.ppermute(first_rows, ROW_AXES, pairs + [(j, i) for i, j in pairs])  3.63 us
  transfers between devices with their start and end apart: 23, of which 12 were waited for; matrix products, arithmetic and copies ran while one was open for 1% of the time, Pallas kernels for 9%

profile of v7, /device:TPU:32, one launch (start us, length us, event | category | flops | bytes accessed | tf_op | source)
XLA Modules:
  0.0 98.5 jit_solution(5943756204199221415)
XLA Ops:
  0.6 1.8 %shard_map.76 = bf16[8,30,8,128]{3,2,1,0:T(8,128)(2,1)} custom-call(bf16[1,1,160,512]{3,2,1,0:T(8,128)(2,1)} %lat.1, bf16[27,8,128]{2,1,0:T(8,128)(2,1)} %bitcast.17), custom_call_target="tpu_custom_call" | custom-call | flops 250000 | bytes 720000 | tf_op jit(solution)/shard_map/pallas_call | solution.py:156
  2.5 8.7 %all-to-all-start = ((bf16[8,30,8,128]{3,2,1,0:T(8,128)(2,1)}), bf16[8,30,8,128]{3,2,1,0:T(8,128)(2,1)S(1)}, u32[]{:S(2)}, u32[]{:S(2)}) async-start(bf16[8,30,8,128]{3,2,1,0:T(8,128)(2,1)} %shard_map.76), calls=%async_computation | async-start | bytes 983040 | tf_op jit(solution)/shard_map/all_to_all | solution.py:375
  11.2 1.1 %copy-done.1 = bf16[1,2,320,512]{3,2,1,0:T(8,128)(2,1)S(1)} copy-done((bf16[1,2,320,512]{3,2,1,0:T(8,128)(2,1)S(1)}, bf16[1,2,320,512]{3,2,1,0:T(8,128)(2,1)}, u32[]{:S(2)}) %copy-start.1) | copy-done | bytes 655384
  12.5 1.6 %collective-permute-start = (bf16[640,128]{1,0:T(8,128)(2,1)S(1)}, bf16[640,128]{1,0:T(8,128)(2,1)S(1)}, u32[]{:S(2)}, u32[]{:S(2)}) collective-permute-start(bf16[640,128]{1,0:T(8,128)(2,1)S(1)} %get-tuple-element.29), channel_id=1, source_target_pairs={{0,64},{64,128},{128,192},{192,0},{1,65},{65,129},{129,193},{193,1... | collective-permute-start | bytes 491528 | tf_op jit(solution)/shard_map/ppermute | solution.py:26
  14.1 2.7 %collective-permute-start.1 = (bf16[640,128]{1,0:T(8,128)(2,1)S(1)}, bf16[640,128]{1,0:T(8,128)(2,1)S(1)}, u32[]{:S(2)}, u32[]{:S(2)}) collective-permute-start(bf16[640,128]{1,0:T(8,128)(2,1)S(1)} %get-tuple-element.30), channel_id=1, source_target_pairs={{0,128},{64,192},{128,0},{192,64},{1,129},{65,193},{129,1},{193,65... | collective-permute-start | bytes 491528 | tf_op jit(solution)/shard_map/ppermute | solution.py:26
  16.8 1.4 %collective-permute-start.2 = (bf16[640,128]{1,0:T(8,128)(2,1)S(1)}, bf16[640,128]{1,0:T(8,128)(2,1)S(1)}, u32[]{:S(2)}, u32[]{:S(2)}) collective-permute-start(bf16[640,128]{1,0:T(8,128)(2,1)S(1)} %get-tuple-element.31), channel_id=1, source_target_pairs={{0,192},{64,0},{128,64},{192,128},{1,193},{65,1},{129,65},{193,129... | collective-permute-start | bytes 491528 | tf_op jit(solution)/shard_map/ppermute | solution.py:26
  18.2 1.7 %collective-permute-done.msg1 = bf16[640,128]{1,0:T(8,128)(2,1)S(1)} collective-permute-done((bf16[640,128]{1,0:T(8,128)(2,1)S(1)}, bf16[640,128]{1,0:T(8,128)(2,1)S(1)}, u32[]{:S(2)}, u32[]{:S(2)}) %collective-permute-start) | collective-permute-done | bytes 163872 | tf_op jit(solution)/shard_map/ppermute | solution.py:26
  19.9 4.3 %collective-permute-done.1.msg2 = bf16[640,128]{1,0:T(8,128)(2,1)S(1)} collective-permute-done((bf16[640,128]{1,0:T(8,128)(2,1)S(1)}, bf16[640,128]{1,0:T(8,128)(2,1)S(1)}, u32[]{:S(2)}, u32[]{:S(2)}) %collective-permute-start.1) | collective-permute-done | bytes 163872 | tf_op jit(solution)/shard_map/ppermute | solution.py:26
  24.2 0.7 all-to-all-done.refs_0_
  24.9 3.0 %collective-permute-start.10 = (bf16[8,30,8,128]{3,2,1,0:T(8,128)(2,1)S(1)}, bf16[8,30,8,128]{3,2,1,0:T(8,128)(2,1)S(1)}, u32[]{:S(2)}, u32[]{:S(2)}) collective-permute-start(bf16[8,30,8,128]{3,2,1,0:T(8,128)(2,1)S(1)} %all-to-all-done.refs_0_), channel_id=1, source_target_pairs={{0,48},{16,0},{32,16},{48,32},{1,49},{17,1},{33,17},{49,33},{2,50}... | collective-permute-start | bytes 1474568 | tf_op jit(solution)/shard_map/ppermute | solution.py:26
  28.0 1.9 %collective-permute-start.7 = (bf16[4,320,128]{2,1,0:T(8,128)(2,1)S(1)}, bf16[4,320,128]{2,1,0:T(8,128)(2,1)S(1)}, u32[]{:S(2)}, u32[]{:S(2)}) collective-permute-start(bf16[4,320,128]{2,1,0:T(8,128)(2,1)S(1)} %get-tuple-element.37), channel_id=1, source_target_pairs={{1,2},{3,4},{5,6},{7,8},{9,10},{11,12},{13,14},{15,16},{17,18},{19... | collective-permute-start | bytes 983048 | tf_op jit(solution)/shard_map/ppermute | solution.py:395
  29.9 2.3 %collective-permute-start.3 = (bf16[8,30,8,128]{3,2,1,0:T(8,128)(2,1)S(1)}, bf16[8,30,8,128]{3,2,1,0:T(8,128)(2,1)S(1)}, u32[]{:S(2)}, u32[]{:S(2)}) collective-permute-start(bf16[8,30,8,128]{3,2,1,0:T(8,128)(2,1)S(1)} %all-to-all-done.refs_0_), channel_id=1, source_target_pairs={{0,32},{16,48},{32,0},{48,16},{1,33},{17,49},{33,1},{49,17},{2,34}... | collective-permute-start | bytes 1474568 | tf_op jit(solution)/shard_map/ppermute | solution.py:26
  32.8 3.6 %collective-permute-done.7.cross = bf16[4,320,128]{2,1,0:T(8,128)(2,1)S(1)} collective-permute-done((bf16[4,320,128]{2,1,0:T(8,128)(2,1)S(1)}, bf16[4,320,128]{2,1,0:T(8,128)(2,1)S(1)}, u32[]{:S(2)}, u32[]{:S(2)}) %collective-permute-start.7) | collective-permute-done | bytes 327712 | tf_op jit(solution)/shard_map/ppermute | solution.py:395
  36.4 10.9 %collective-permute-done.10.refs_2_ = bf16[8,30,8,128]{3,2,1,0:T(8,128)(2,1)S(1)} collective-permute-done((bf16[8,30,8,128]{3,2,1,0:T(8,128)(2,1)S(1)}, bf16[8,30,8,128]{3,2,1,0:T(8,128)(2,1)S(1)}, u32[]{:S(2)}, u32[]{:S(2)}) %collective-permute-start.10) | collective-permute-done | bytes 491552 | tf_op jit(solution)/shard_map/ppermute | solution.py:26
  47.4 1.5 %shard_map.79 = (bf16[2,640,1152]{2,1,0:T(8,128)(2,1)S(1)}, bf16[2,480,1152]{2,1,0:T(8,128)(2,1)S(1)}, bf16[2,320,1152]{2,1,0:T(8,128)(2,1)S(1)}) custom-call(bf16[640,128]{1,0:T(8,128)(2,1)S(1)} %get-tuple-element.33.msg0, bf16[640,128]{1,0:T(8,128)(2,1)S(1)} %collective-permute-done.msg1, bf16[640,128]{1,0:T(8,128)(2,1)S(1)} %collective-permute-done.1.msg2, ...), custom_call_target="tpu_custom_call" | custom-call | flops 1000 | bytes 1000 | tf_op jit(solution)/shard_map/pallas_call | solution.py:84
  48.9 1.9 %collective-permute-done.5.refs_2_ = bf16[8,30,8,128]{3,2,1,0:T(8,128)(2,1)S(1)} collective-permute-done((bf16[8,30,8,128]{3,2,1,0:T(8,128)(2,1)S(1)}, bf16[8,30,8,128]{3,2,1,0:T(8,128)(2,1)S(1)}, u32[]{:S(2)}, u32[]{:S(2)}) %collective-permute-start.5) | collective-permute-done | bytes 491552 | tf_op jit(solution)/shard_map/ppermute | solution.py:26
  51.5 1.1 %collective-permute-done.6.refs_3_ = bf16[8,30,8,128]{3,2,1,0:T(8,128)(2,1)S(1)} collective-permute-done((bf16[8,30,8,128]{3,2,1,0:T(8,128)(2,1)S(1)}, bf16[8,30,8,128]{3,2,1,0:T(8,128)(2,1)S(1)}, u32[]{:S(2)}, u32[]{:S(2)}) %collective-permute-start.6) | collective-permute-done | bytes 491552 | tf_op jit(solution)/shard_map/ppermute | solution.py:26
  52.6 0.7 collective-permute-done.4.refs_1_
  53.4 2.7 %collective-permute-start.14 = (bf16[688,128]{1,0:T(8,128)(2,1)S(1)}, bf16[688,128]{1,0:T(8,128)(2,1)S(1)}, u32[]{:S(2)}, u32[]{:S(2)}) collective-permute-start(bf16[688,128]{1,0:T(8,128)(2,1)S(1)} %shard_map.82.msg0), channel_id=1, source_target_pairs={{0,192},{64,0},{128,64},{192,128},{1,193},{65,1},{129,65},{193,129... | collective-permute-start | bytes 528392 | tf_op jit(solution)/shard_map/ppermute | solution.py:26
  56.1 1.1 %collective-permute-start.13 = (bf16[688,128]{1,0:T(8,128)(2,1)S(1)}, bf16[688,128]{1,0:T(8,128)(2,1)S(1)}, u32[]{:S(2)}, u32[]{:S(2)}) collective-permute-start(bf16[688,128]{1,0:T(8,128)(2,1)S(1)} %shard_map.82.msg0), channel_id=1, source_target_pairs={{0,128},{64,192},{128,0},{192,64},{1,129},{65,193},{129,1},{193,65... | collective-permute-start | bytes 528392 | tf_op jit(solution)/shard_map/ppermute | solution.py:26
  57.8 3.1 %shard_map.80 = (f32[4,160,128]{2,1,0:T(8,128)S(1)}, f32[4,160,128]{2,1,0:T(8,128)S(1)}, f32[4,160,128]{2,1,0:T(8,128)S(1)}, f32[4,160,128]{2,1,0:T(8,128)S(1)}) custom-call(bf16[8,30,8,128]{3,2,1,0:T(8,128)(2,1)S(1)} %all-to-all-done.refs_0_, bf16[8,30,8,128]{3,2,1,0:T(8,128)(2,1)S(1)} %collective-permute-done.9.refs_1_, ...), custom_call_target="tpu_custom_call" | custom-call | flops 1700000000 | bytes 9000000 | tf_op jit(solution)/shard_map/pallas_call | solution.py:267
  60.9 3.1 %shard_map.81 = (f32[4,160,128]{2,1,0:T(8,128)S(1)}, f32[4,160,128]{2,1,0:T(8,128)S(1)}, f32[4,160,128]{2,1,0:T(8,128)S(1)}, f32[4,160,128]{2,1,0:T(8,128)S(1)}) custom-call(bf16[8,30,8,128]{3,2,1,0:T(8,128)(2,1)S(1)} %collective-permute-done.3.refs_0_, ...), custom_call_target="tpu_custom_call", output_to_operand_aliasing={{0}: (7, {}), {1}: (8, {}), {2}: (9, {}), {3}: (10, {})} | custom-call | flops 1700000000 | bytes 9000000 | tf_op jit(solution)/shard_map/pallas_call | solution.py:267
  64.1 2.7 %collective-permute-start.21 = (f32[4,160,128]{2,1,0:T(8,128)S(1)}, f32[4,160,128]{2,1,0:T(8,128)S(1)}, u32[]{:S(2)}, u32[]{:S(2)}) collective-permute-start(f32[4,160,128]{2,1,0:T(8,128)S(1)} %get-tuple-element.47.part1), channel_id=1, source_target_pairs={{0,192},{64,0},{128,64},{192,128},{1,193},{65,1},{129,65},{193,129... | collective-permute-start | bytes 983048 | tf_op jit(solution)/shard_map/ppermute | solution.py:26
  66.8 1.2 %collective-permute-start.20 = (f32[4,160,128]{2,1,0:T(8,128)S(1)}, f32[4,160,128]{2,1,0:T(8,128)S(1)}, u32[]{:S(2)}, u32[]{:S(2)}) collective-permute-start(f32[4,160,128]{2,1,0:T(8,128)S(1)} %get-tuple-element.48.part2), channel_id=1, source_target_pairs={{0,128},{64,192},{128,0},{192,64},{1,129},{65,193},{129,1},{193,65... | collective-permute-start | bytes 983048 | tf_op jit(solution)/shard_map/ppermute | solution.py:26
  68.6 0.8 shard_map.83
  69.5 1.2 %collective-permute-done.15 = f32[8,128]{1,0:T(8,128)S(1)} collective-permute-done((f32[8,128]{1,0:T(8,128)S(1)}, f32[8,128]{1,0:T(8,128)S(1)}, u32[]{:S(2)}, u32[]{:S(2)}) %collective-permute-start.15) | collective-permute-done | bytes 4128 | tf_op jit(solution)/shard_map/ppermute | solution.py:26
  70.7 17.7 %all_to_all.10 = f32[32,8,128]{2,1,0:T(8,128)S(1)} all-to-all(f32[32,8,128]{2,1,0:T(8,128)S(1)} %broadcast_in_dim.14), channel_id=1, replica_groups={{0,2,4,6,8,10,12,14,16,18,20,22,24,26,28,30,32,34,36,38,40,42,44,46,48,..., dimensions={0} | all-to-all | bytes 262144 | tf_op jit(solution)/shard_map/all_to_all | solution.py:426
  88.4 3.3 %collective-permute-start.18 = (f32[8,128]{1,0:T(8,128)S(1)}, f32[8,128]{1,0:T(8,128)S(1)}, u32[]{:S(2)}, u32[]{:S(2)}) collective-permute-start(f32[8,128]{1,0:T(8,128)S(1)} %reduce_sum.99.sum0), channel_id=1, source_target_pairs={{0,192},{64,0},{128,64},{192,128},{1,193},{65,1},{129,65},{193,129... | collective-permute-start | bytes 12296 | tf_op jit(solution)/shard_map/ppermute | solution.py:26
  91.6 0.9 collective-permute-start.17
  93.0 3.8 %collective-permute-done.17.sum2 = f32[8,128]{1,0:T(8,128)S(1)} collective-permute-done((f32[8,128]{1,0:T(8,128)S(1)}, f32[8,128]{1,0:T(8,128)S(1)}, u32[]{:S(2)}, u32[]{:S(2)}) %collective-permute-start.17) | collective-permute-done | bytes 4128 | tf_op jit(solution)/shard_map/ppermute | solution.py:26
  96.8 0.6 collective-permute-done.16.sum1
  97.4 1.1 %shard_map.84 = (f32[160,512]{1,0:T(8,128)}, f32[512]{0:T(512)}, f32[512]{0:T(512)}) custom-call(f32[8,128]{1,0:T(8,128)S(1)} %reduce_sum.99.sum0, f32[8,128]{1,0:T(8,128)S(1)} %collective-permute-done.16.sum1, f32[8,128]{1,0:T(8,128)S(1)} %collective-permute-done.17.sum2, f32[8,128]{1,0:T(8,128)S(1)} %collective-permute-done.18.sum3, ...), custom_call_target="tpu_custom_call" | custom-call | flops 2000000 | bytes 1900000 | tf_op jit(solution)/shard_map/pallas_call | solution.py:353
  (55 shorter events, 3.4 us)
Async XLA Ops:
  2.5 50.9 %copy-start = (bf16[1,1,160,512]{3,2,1,0:T(8,128)(2,1)S(1)}, bf16[1,1,160,512]{3,2,1,0:T(8,128)(2,1)}, u32[]{:S(2)}) copy-start(bf16[1,1,160,512]{3,2,1,0:T(8,128)(2,1)} %lat.1) | copy-start | bytes 491524
  2.5 22.4 %all-to-all-start = ((bf16[8,30,8,128]{3,2,1,0:T(8,128)(2,1)}), bf16[8,30,8,128]{3,2,1,0:T(8,128)(2,1)S(1)}, u32[]{:S(2)}, u32[]{:S(2)}) async-start(bf16[8,30,8,128]{3,2,1,0:T(8,128)(2,1)} %shard_map.76), calls=%async_computation | async-start | bytes 983040 | tf_op jit(solution)/shard_map/all_to_all | solution.py:375
  11.2 1.1 %copy-start.1 = (bf16[1,2,320,512]{3,2,1,0:T(8,128)(2,1)S(1)}, bf16[1,2,320,512]{3,2,1,0:T(8,128)(2,1)}, u32[]{:S(2)}) copy-start(bf16[1,2,320,512]{3,2,1,0:T(8,128)(2,1)} %cot.1) | copy-start | bytes 1966084
  12.5 7.4 %collective-permute-start = (bf16[640,128]{1,0:T(8,128)(2,1)S(1)}, bf16[640,128]{1,0:T(8,128)(2,1)S(1)}, u32[]{:S(2)}, u32[]{:S(2)}) collective-permute-start(bf16[640,128]{1,0:T(8,128)(2,1)S(1)} %get-tuple-element.29), channel_id=1, source_target_pairs={{0,64},{64,128},{128,192},{192,0},{1,65},{65,129},{129,193},{193,1... | collective-permute-start | bytes 491528 | tf_op jit(solution)/shard_map/ppermute | solution.py:26
  14.1 10.1 %collective-permute-start.1 = (bf16[640,128]{1,0:T(8,128)(2,1)S(1)}, bf16[640,128]{1,0:T(8,128)(2,1)S(1)}, u32[]{:S(2)}, u32[]{:S(2)}) collective-permute-start(bf16[640,128]{1,0:T(8,128)(2,1)S(1)} %get-tuple-element.30), channel_id=1, source_target_pairs={{0,128},{64,192},{128,0},{192,64},{1,129},{65,193},{129,1},{193,65... | collective-permute-start | bytes 491528 | tf_op jit(solution)/shard_map/ppermute | solution.py:26
  16.8 7.4 %collective-permute-start.2 = (bf16[640,128]{1,0:T(8,128)(2,1)S(1)}, bf16[640,128]{1,0:T(8,128)(2,1)S(1)}, u32[]{:S(2)}, u32[]{:S(2)}) collective-permute-start(bf16[640,128]{1,0:T(8,128)(2,1)S(1)} %get-tuple-element.31), channel_id=1, source_target_pairs={{0,192},{64,0},{128,64},{192,128},{1,193},{65,1},{129,65},{193,129... | collective-permute-start | bytes 491528 | tf_op jit(solution)/shard_map/ppermute | solution.py:26
  24.9 22.4 %collective-permute-start.10 = (bf16[8,30,8,128]{3,2,1,0:T(8,128)(2,1)S(1)}, bf16[8,30,8,128]{3,2,1,0:T(8,128)(2,1)S(1)}, u32[]{:S(2)}, u32[]{:S(2)}) collective-permute-start(bf16[8,30,8,128]{3,2,1,0:T(8,128)(2,1)S(1)} %all-to-all-done.refs_0_), channel_id=1, source_target_pairs={{0,48},{16,0},{32,16},{48,32},{1,49},{17,1},{33,17},{49,33},{2,50}... | collective-permute-start | bytes 1474568 | tf_op jit(solution)/shard_map/ppermute | solution.py:26
  27.9 22.8 %collective-permute-start.5 = (bf16[8,30,8,128]{3,2,1,0:T(8,128)(2,1)S(1)}, bf16[8,30,8,128]{3,2,1,0:T(8,128)(2,1)S(1)}, u32[]{:S(2)}, u32[]{:S(2)}) collective-permute-start(bf16[8,30,8,128]{3,2,1,0:T(8,128)(2,1)S(1)} %all-to-all-done.refs_0_), channel_id=1, source_target_pairs={{0,16},{16,32},{32,48},{48,0},{1,17},{17,33},{33,49},{49,1},{2,18}... | collective-permute-start | bytes 1474568 | tf_op jit(solution)/shard_map/ppermute | solution.py:26
  28.0 8.4 %collective-permute-start.7 = (bf16[4,320,128]{2,1,0:T(8,128)(2,1)S(1)}, bf16[4,320,128]{2,1,0:T(8,128)(2,1)S(1)}, u32[]{:S(2)}, u32[]{:S(2)}) collective-permute-start(bf16[4,320,128]{2,1,0:T(8,128)(2,1)S(1)} %get-tuple-element.37), channel_id=1, source_target_pairs={{1,2},{3,4},{5,6},{7,8},{9,10},{11,12},{13,14},{15,16},{17,18},{19... | collective-permute-start | bytes 983048 | tf_op jit(solution)/shard_map/ppermute | solution.py:395
  29.9 20.8 %collective-permute-start.3 = (bf16[8,30,8,128]{3,2,1,0:T(8,128)(2,1)S(1)}, bf16[8,30,8,128]{3,2,1,0:T(8,128)(2,1)S(1)}, u32[]{:S(2)}, u32[]{:S(2)}) collective-permute-start(bf16[8,30,8,128]{3,2,1,0:T(8,128)(2,1)S(1)} %all-to-all-done.refs_0_), channel_id=1, source_target_pairs={{0,32},{16,48},{32,0},{48,16},{1,33},{17,49},{33,1},{49,17},{2,34}... | collective-permute-start | bytes 1474568 | tf_op jit(solution)/shard_map/ppermute | solution.py:26
  32.2 15.1 %collective-permute-start.8 = (bf16[4,320,128]{2,1,0:T(8,128)(2,1)S(1)}, bf16[4,320,128]{2,1,0:T(8,128)(2,1)S(1)}, u32[]{:S(2)}, u32[]{:S(2)}) collective-permute-start(bf16[4,320,128]{2,1,0:T(8,128)(2,1)S(1)} %get-tuple-element.38), channel_id=1, source_target_pairs={{0,1},{1,0},{2,3},{3,2},{4,5},{5,4},{6,7},{7,6},{8,9},{9,8},{10,11... | collective-permute-start | bytes 983048 | tf_op jit(solution)/shard_map/ppermute | solution.py:26
  36.4 15.0 %collective-permute-start.9 = (bf16[8,30,8,128]{3,2,1,0:T(8,128)(2,1)S(1)}, bf16[8,30,8,128]{3,2,1,0:T(8,128)(2,1)S(1)}, u32[]{:S(2)}, u32[]{:S(2)}) collective-permute-start(bf16[8,30,8,128]{3,2,1,0:T(8,128)(2,1)S(1)} %all-to-all-done.refs_0_), channel_id=1, source_target_pairs={{0,1},{1,0},{2,3},{3,2},{4,5},{5,4},{6,7},{7,6},{8,9},{9,8},{10,11... | collective-permute-start | bytes 1474568 | tf_op jit(solution)/shard_map/ppermute | solution.py:26
  47.3 4.1 %collective-permute-start.11 = (bf16[8,30,8,128]{3,2,1,0:T(8,128)(2,1)S(1)}, bf16[8,30,8,128]{3,2,1,0:T(8,128)(2,1)S(1)}, u32[]{:S(2)}, u32[]{:S(2)}) collective-permute-start(bf16[8,30,8,128]{3,2,1,0:T(8,128)(2,1)S(1)} %collective-permute-done.10.refs_2_), channel_id=1, source_target_pairs={{0,1},{1,0},{2,3},{3,2},{4,5},{5,4},{6,7},{7,6},{8,9},{9,8},{10,11... | collective-permute-start | bytes 1474568 | tf_op jit(solution)/shard_map/ppermute | solution.py:26
  50.7 1.9 %collective-permute-start.6 = (bf16[8,30,8,128]{3,2,1,0:T(8,128)(2,1)S(1)}, bf16[8,30,8,128]{3,2,1,0:T(8,128)(2,1)S(1)}, u32[]{:S(2)}, u32[]{:S(2)}) collective-permute-start(bf16[8,30,8,128]{3,2,1,0:T(8,128)(2,1)S(1)} %collective-permute-done.5.refs_2_), channel_id=1, source_target_pairs={{0,1},{1,0},{2,3},{3,2},{4,5},{5,4},{6,7},{7,6},{8,9},{9,8},{10,11... | collective-permute-start | bytes 1474568 | tf_op jit(solution)/shard_map/ppermute | solution.py:26
  50.8 2.5 %collective-permute-start.4 = (bf16[8,30,8,128]{3,2,1,0:T(8,128)(2,1)S(1)}, bf16[8,30,8,128]{3,2,1,0:T(8,128)(2,1)S(1)}, u32[]{:S(2)}, u32[]{:S(2)}) collective-permute-start(bf16[8,30,8,128]{3,2,1,0:T(8,128)(2,1)S(1)} %collective-permute-done.3.refs_0_), channel_id=1, source_target_pairs={{0,1},{1,0},{2,3},{3,2},{4,5},{5,4},{6,7},{7,6},{8,9},{9,8},{10,11... | collective-permute-start | bytes 1474568 | tf_op jit(solution)/shard_map/ppermute | solution.py:26
  53.4 14.6 %collective-permute-start.14 = (bf16[688,128]{1,0:T(8,128)(2,1)S(1)}, bf16[688,128]{1,0:T(8,128)(2,1)S(1)}, u32[]{:S(2)}, u32[]{:S(2)}) collective-permute-start(bf16[688,128]{1,0:T(8,128)(2,1)S(1)} %shard_map.82.msg0), channel_id=1, source_target_pairs={{0,192},{64,0},{128,64},{192,128},{1,193},{65,1},{129,65},{193,129... | collective-permute-start | bytes 528392 | tf_op jit(solution)/shard_map/ppermute | solution.py:26
  56.1 11.9 %collective-permute-start.13 = (bf16[688,128]{1,0:T(8,128)(2,1)S(1)}, bf16[688,128]{1,0:T(8,128)(2,1)S(1)}, u32[]{:S(2)}, u32[]{:S(2)}) collective-permute-start(bf16[688,128]{1,0:T(8,128)(2,1)S(1)} %shard_map.82.msg0), channel_id=1, source_target_pairs={{0,128},{64,192},{128,0},{192,64},{1,129},{65,193},{129,1},{193,65... | collective-permute-start | bytes 528392 | tf_op jit(solution)/shard_map/ppermute | solution.py:26
  57.2 10.8 %collective-permute-start.12 = (bf16[688,128]{1,0:T(8,128)(2,1)S(1)}, bf16[688,128]{1,0:T(8,128)(2,1)S(1)}, u32[]{:S(2)}, u32[]{:S(2)}) collective-permute-start(bf16[688,128]{1,0:T(8,128)(2,1)S(1)} %shard_map.82.msg0), channel_id=1, source_target_pairs={{0,64},{64,128},{128,192},{192,0},{1,65},{65,129},{129,193},{193,1... | collective-permute-start | bytes 528392 | tf_op jit(solution)/shard_map/ppermute | solution.py:26
  60.9 7.6 %copy-start.2 = (f32[512]{0:T(512)S(1)}, f32[512]{0:T(512)}, u32[]{:S(2)}) copy-start(f32[512]{0:T(512)} %param.7) | copy-start | bytes 6148
  60.9 7.6 %copy-start.3 = (f32[512]{0:T(512)S(1)}, f32[512]{0:T(512)}, u32[]{:S(2)}) copy-start(f32[512]{0:T(512)} %param.6) | copy-start | bytes 6148
  64.1 28.5 %collective-permute-start.21 = (f32[4,160,128]{2,1,0:T(8,128)S(1)}, f32[4,160,128]{2,1,0:T(8,128)S(1)}, u32[]{:S(2)}, u32[]{:S(2)}) collective-permute-start(f32[4,160,128]{2,1,0:T(8,128)S(1)} %get-tuple-element.47.part1), channel_id=1, source_target_pairs={{0,192},{64,0},{128,64},{192,128},{1,193},{65,1},{129,65},{193,129... | collective-permute-start | bytes 983048 | tf_op jit(solution)/shard_map/ppermute | solution.py:26
  66.8 25.9 %collective-permute-start.20 = (f32[4,160,128]{2,1,0:T(8,128)S(1)}, f32[4,160,128]{2,1,0:T(8,128)S(1)}, u32[]{:S(2)}, u32[]{:S(2)}) collective-permute-start(f32[4,160,128]{2,1,0:T(8,128)S(1)} %get-tuple-element.48.part2), channel_id=1, source_target_pairs={{0,128},{64,192},{128,0},{192,64},{1,129},{65,193},{129,1},{193,65... | collective-permute-start | bytes 983048 | tf_op jit(solution)/shard_map/ppermute | solution.py:26
  68.0 24.6 %collective-permute-start.19 = (f32[4,160,128]{2,1,0:T(8,128)S(1)}, f32[4,160,128]{2,1,0:T(8,128)S(1)}, u32[]{:S(2)}, u32[]{:S(2)}) collective-permute-start(f32[4,160,128]{2,1,0:T(8,128)S(1)} %get-tuple-element.49.part3), channel_id=1, source_target_pairs={{0,64},{64,128},{128,192},{192,0},{1,65},{65,129},{129,193},{193,1... | collective-permute-start | bytes 983048 | tf_op jit(solution)/shard_map/ppermute | solution.py:26
  69.4 1.3 %collective-permute-start.15 = (f32[8,128]{1,0:T(8,128)S(1)}, f32[8,128]{1,0:T(8,128)S(1)}, u32[]{:S(2)}, u32[]{:S(2)}) collective-permute-start(f32[8,128]{1,0:T(8,128)S(1)} %shard_map.83), channel_id=1, source_target_pairs={{0,1},{1,0},{2,3},{3,2},{4,5},{5,4},{6,7},{7,6},{8,9},{9,8},{10,11... | collective-permute-start | bytes 12296 | tf_op jit(solution)/shard_map/ppermute | solution.py:26
  88.4 4.6 %collective-permute-start.18 = (f32[8,128]{1,0:T(8,128)S(1)}, f32[8,128]{1,0:T(8,128)S(1)}, u32[]{:S(2)}, u32[]{:S(2)}) collective-permute-start(f32[8,128]{1,0:T(8,128)S(1)} %reduce_sum.99.sum0), channel_id=1, source_target_pairs={{0,192},{64,0},{128,64},{192,128},{1,193},{65,1},{129,65},{193,129... | collective-permute-start | bytes 12296 | tf_op jit(solution)/shard_map/ppermute | solution.py:26
  91.6 5.1 %collective-permute-start.17 = (f32[8,128]{1,0:T(8,128)S(1)}, f32[8,128]{1,0:T(8,128)S(1)}, u32[]{:S(2)}, u32[]{:S(2)}) collective-permute-start(f32[8,128]{1,0:T(8,128)S(1)} %reduce_sum.99.sum0), channel_id=1, source_target_pairs={{0,128},{64,192},{128,0},{192,64},{1,129},{65,193},{129,1},{193,65... | collective-permute-start | bytes 12296 | tf_op jit(solution)/shard_map/ppermute | solution.py:26
  92.6 4.8 %collective-permute-start.16 = (f32[8,128]{1,0:T(8,128)S(1)}, f32[8,128]{1,0:T(8,128)S(1)}, u32[]{:S(2)}, u32[]{:S(2)}) collective-permute-start(f32[8,128]{1,0:T(8,128)S(1)} %reduce_sum.99.sum0), channel_id=1, source_target_pairs={{0,64},{64,128},{128,192},{192,0},{1,65},{65,129},{129,193},{193,1... | collective-permute-start | bytes 12296 | tf_op jit(solution)/shard_map/ppermute | solution.py:26

commit v8 on v7

--- a/solution.py
+++ b/solution.py
@@ -388,7 +388,6 @@
         msg if step == 0 else send(msg, "x", step)
         for step, msg in enumerate(split(cotangent))
     ]
-    block, msgs = lax.optimization_barrier((block, msgs))
     pieces = [block] + [send(block, "y", step) for step in range(1, YS)]
     first_rows, last_rows = rims(msgs, cotangent.shape[2])
     pairs = [(i, i + 1) for i in range(1, ROWS - 1, CS)]

time: 98.8 us -> 97.8 us (0.990)
    ppermute x21, waiting for transfers between devices: 26.5 us -> 20.3 us  [send(): lax.ppermute(value, axis, [(i, (i + step) % size) for i in range(size)])]
    all_to_all x1, waiting for transfers between devices: 0.74 us -> 6.7 us  [on_device(): lax.all_to_all(message(latent, conv_weight.reshape(PLANES, 8, 128)), ('z'...]
  transfers between devices with their start and end apart: 23 -> 23, of which waited for: 12 -> 10; matrix products, arithmetic and copies ran while one was open for 1% -> 1% of each run, Pallas kernels for 9% -> 9%
where the time goes in v8:
time: 97.8 us; the launch traced here: 97.5 us
  starting transfers between devices  35.4 us (36%)
  waiting for transfers between devices  30.9 us (32%)
  blocking collectives  16.8 us (17%)
  Pallas kernels  11.7 us (12%)
  local copies, waits for them, and re-layouts  1.51 us (2%)
    ppermute x21, starting transfers between devices, send(): lax.ppermute(value, axis, [(i, (i + step) % size) for i in range(size)])  24.8 us
    ppermute x21, waiting for transfers between devices, send(): lax.ppermute(value, axis, [(i, (i + step) % size) for i in range(size)])  20.3 us
    all_to_all x1, blocking collectives, on_device(): lax.all_to_all(sums, ROW_AXES, 0, 0, axis_index_groups=[list(range(0, ROW...  16.8 us
    all_to_all x1, starting transfers between devices, on_device(): lax.all_to_all(message(latent, conv_weight.reshape(PLANES, 8, 128)), ('z'...  8.71 us
    all_to_all x1, waiting for transfers between devices, on_device(): lax.all_to_all(message(latent, conv_weight.reshape(PLANES, 8, 128)), ('z'...  6.7 us
    pallas_call x2, Pallas kernels, product(): pl.pallas_call(functools.partial(product_kernel, steps, aliased), out_sha...  6.19 us
    ppermute x1, waiting for transfers between devices, on_device(): lax.ppermute(first_rows, ROW_AXES, pairs + [(j, i) for i, j in pairs])  3.85 us
  transfers between devices with their start and end apart: 23, of which 10 were waited for; matrix products, arithmetic and copies ran while one was open for 1% of the time, Pallas kernels for 9%

profile of v8, /device:TPU:32, one launch (start us, length us, event | category | flops | bytes accessed | tf_op | source)
XLA Modules:
  0.0 97.5 jit_solution(6842926354032600613)
XLA Ops:
  0.6 1.8 %shard_map.76 = bf16[8,30,8,128]{3,2,1,0:T(8,128)(2,1)} custom-call(bf16[1,1,160,512]{3,2,1,0:T(8,128)(2,1)} %lat.1, bf16[27,8,128]{2,1,0:T(8,128)(2,1)} %bitcast.17), custom_call_target="tpu_custom_call" | custom-call | flops 250000 | bytes 720000 | tf_op jit(solution)/shard_map/pallas_call | solution.py:156
  2.5 8.7 %all-to-all-start = ((bf16[8,30,8,128]{3,2,1,0:T(8,128)(2,1)}), bf16[8,30,8,128]{3,2,1,0:T(8,128)(2,1)S(1)}, u32[]{:S(2)}, u32[]{:S(2)}) async-start(bf16[8,30,8,128]{3,2,1,0:T(8,128)(2,1)} %shard_map.76), calls=%async_computation | async-start | bytes 983040 | tf_op jit(solution)/shard_map/all_to_all | solution.py:375
  11.2 1.1 %copy-done.1 = bf16[1,2,320,512]{3,2,1,0:T(8,128)(2,1)S(1)} copy-done((bf16[1,2,320,512]{3,2,1,0:T(8,128)(2,1)S(1)}, bf16[1,2,320,512]{3,2,1,0:T(8,128)(2,1)}, u32[]{:S(2)}) %copy-start.1) | copy-done | bytes 655384
  12.5 1.6 %collective-permute-start.4 = (bf16[640,128]{1,0:T(8,128)(2,1)S(1)}, bf16[640,128]{1,0:T(8,128)(2,1)S(1)}, u32[]{:S(2)}, u32[]{:S(2)}) collective-permute-start(bf16[640,128]{1,0:T(8,128)(2,1)S(1)} %get-tuple-element.24), channel_id=1, source_target_pairs={{0,64},{64,128},{128,192},{192,0},{1,65},{65,129},{129,193},{193,1... | collective-permute-start | bytes 491528 | tf_op jit(solution)/shard_map/ppermute | solution.py:26
  14.1 2.7 %collective-permute-start.5 = (bf16[640,128]{1,0:T(8,128)(2,1)S(1)}, bf16[640,128]{1,0:T(8,128)(2,1)S(1)}, u32[]{:S(2)}, u32[]{:S(2)}) collective-permute-start(bf16[640,128]{1,0:T(8,128)(2,1)S(1)} %get-tuple-element.25), channel_id=1, source_target_pairs={{0,128},{64,192},{128,0},{192,64},{1,129},{65,193},{129,1},{193,65... | collective-permute-start | bytes 491528 | tf_op jit(solution)/shard_map/ppermute | solution.py:26
  16.8 1.4 %collective-permute-start.6 = (bf16[640,128]{1,0:T(8,128)(2,1)S(1)}, bf16[640,128]{1,0:T(8,128)(2,1)S(1)}, u32[]{:S(2)}, u32[]{:S(2)}) collective-permute-start(bf16[640,128]{1,0:T(8,128)(2,1)S(1)} %get-tuple-element.26), channel_id=1, source_target_pairs={{0,192},{64,0},{128,64},{192,128},{1,193},{65,1},{129,65},{193,129... | collective-permute-start | bytes 491528 | tf_op jit(solution)/shard_map/ppermute | solution.py:26
  18.2 6.7 %all-to-all-done.refs_0_ = bf16[8,30,8,128]{3,2,1,0:T(8,128)(2,1)S(1)} async-done(((bf16[8,30,8,128]{3,2,1,0:T(8,128)(2,1)}), bf16[8,30,8,128]{3,2,1,0:T(8,128)(2,1)S(1)}, u32[]{:S(2)}, u32[]{:S(2)}) %all-to-all-start) | async-done | bytes 491552 | tf_op jit(solution)/shard_map/all_to_all | solution.py:375
  24.9 3.0 %collective-permute-start.10 = (bf16[8,30,8,128]{3,2,1,0:T(8,128)(2,1)S(1)}, bf16[8,30,8,128]{3,2,1,0:T(8,128)(2,1)S(1)}, u32[]{:S(2)}, u32[]{:S(2)}) collective-permute-start(bf16[8,30,8,128]{3,2,1,0:T(8,128)(2,1)S(1)} %all-to-all-done.refs_0_), channel_id=1, source_target_pairs={{0,48},{16,0},{32,16},{48,32},{1,49},{17,1},{33,17},{49,33},{2,50}... | collective-permute-start | bytes 1474568 | tf_op jit(solution)/shard_map/ppermute | solution.py:26
  28.0 1.9 %collective-permute-start.7 = (bf16[4,320,128]{2,1,0:T(8,128)(2,1)S(1)}, bf16[4,320,128]{2,1,0:T(8,128)(2,1)S(1)}, u32[]{:S(2)}, u32[]{:S(2)}) collective-permute-start(bf16[4,320,128]{2,1,0:T(8,128)(2,1)S(1)} %get-tuple-element.27), channel_id=1, source_target_pairs={{1,2},{3,4},{5,6},{7,8},{9,10},{11,12},{13,14},{15,16},{17,18},{19... | collective-permute-start | bytes 983048 | tf_op jit(solution)/shard_map/ppermute | solution.py:394
  30.4 2.2 %collective-permute-start = (bf16[8,30,8,128]{3,2,1,0:T(8,128)(2,1)S(1)}, bf16[8,30,8,128]{3,2,1,0:T(8,128)(2,1)S(1)}, u32[]{:S(2)}, u32[]{:S(2)}) collective-permute-start(bf16[8,30,8,128]{3,2,1,0:T(8,128)(2,1)S(1)} %all-to-all-done.refs_0_), channel_id=1, source_target_pairs={{0,32},{16,48},{32,0},{48,16},{1,33},{17,49},{33,1},{49,17},{2,34}... | collective-permute-start | bytes 1474568 | tf_op jit(solution)/shard_map/ppermute | solution.py:26
  32.6 3.9 %collective-permute-done.7.cross = bf16[4,320,128]{2,1,0:T(8,128)(2,1)S(1)} collective-permute-done((bf16[4,320,128]{2,1,0:T(8,128)(2,1)S(1)}, bf16[4,320,128]{2,1,0:T(8,128)(2,1)S(1)}, u32[]{:S(2)}, u32[]{:S(2)}) %collective-permute-start.7) | collective-permute-done | bytes 327712 | tf_op jit(solution)/shard_map/ppermute | solution.py:394
  36.4 1.5 %shard_map.79 = (bf16[2,640,1152]{2,1,0:T(8,128)(2,1)S(1)}, bf16[2,480,1152]{2,1,0:T(8,128)(2,1)S(1)}, bf16[2,320,1152]{2,1,0:T(8,128)(2,1)S(1)}) custom-call(bf16[640,128]{1,0:T(8,128)(2,1)S(1)} %get-tuple-element.23.msg0, bf16[640,128]{1,0:T(8,128)(2,1)S(1)} %collective-permute-done.4.msg1, bf16[640,128]{1,0:T(8,128)(2,1)S(1)} %collective-permute-done.5.msg2, ...), custom_call_target="tpu_custom_call" | custom-call | flops 1000 | bytes 1000 | tf_op jit(solution)/shard_map/pallas_call | solution.py:84
  37.9 9.3 %collective-permute-done.10.refs_2_ = bf16[8,30,8,128]{3,2,1,0:T(8,128)(2,1)S(1)} collective-permute-done((bf16[8,30,8,128]{3,2,1,0:T(8,128)(2,1)S(1)}, bf16[8,30,8,128]{3,2,1,0:T(8,128)(2,1)S(1)}, u32[]{:S(2)}, u32[]{:S(2)}) %collective-permute-start.10) | collective-permute-done | bytes 491552 | tf_op jit(solution)/shard_map/ppermute | solution.py:26
  47.3 3.4 %collective-permute-done.2.refs_2_ = bf16[8,30,8,128]{3,2,1,0:T(8,128)(2,1)S(1)} collective-permute-done((bf16[8,30,8,128]{3,2,1,0:T(8,128)(2,1)S(1)}, bf16[8,30,8,128]{3,2,1,0:T(8,128)(2,1)S(1)}, u32[]{:S(2)}, u32[]{:S(2)}) %collective-permute-start.2) | collective-permute-done | bytes 491552 | tf_op jit(solution)/shard_map/ppermute | solution.py:26
  50.7 0.6 collective-permute-start.1
  51.4 1.1 %collective-permute-done.3.refs_3_ = bf16[8,30,8,128]{3,2,1,0:T(8,128)(2,1)S(1)} collective-permute-done((bf16[8,30,8,128]{3,2,1,0:T(8,128)(2,1)S(1)}, bf16[8,30,8,128]{3,2,1,0:T(8,128)(2,1)S(1)}, u32[]{:S(2)}, u32[]{:S(2)}) %collective-permute-start.3) | collective-permute-done | bytes 491552 | tf_op jit(solution)/shard_map/ppermute | solution.py:26
  52.5 0.7 collective-permute-done.1.refs_1_
  53.3 2.8 %collective-permute-start.14 = (bf16[688,128]{1,0:T(8,128)(2,1)S(1)}, bf16[688,128]{1,0:T(8,128)(2,1)S(1)}, u32[]{:S(2)}, u32[]{:S(2)}) collective-permute-start(bf16[688,128]{1,0:T(8,128)(2,1)S(1)} %shard_map.82.msg0), channel_id=1, source_target_pairs={{0,192},{64,0},{128,64},{192,128},{1,193},{65,1},{129,65},{193,129... | collective-permute-start | bytes 528392 | tf_op jit(solution)/shard_map/ppermute | solution.py:26
  56.1 0.8 collective-permute-start.13
  56.9 0.9 collective-permute-start.12
  57.8 3.1 %shard_map.80 = (f32[4,160,128]{2,1,0:T(8,128)S(1)}, f32[4,160,128]{2,1,0:T(8,128)S(1)}, f32[4,160,128]{2,1,0:T(8,128)S(1)}, f32[4,160,128]{2,1,0:T(8,128)S(1)}) custom-call(bf16[8,30,8,128]{3,2,1,0:T(8,128)(2,1)S(1)} %all-to-all-done.refs_0_, bf16[8,30,8,128]{3,2,1,0:T(8,128)(2,1)S(1)} %collective-permute-done.9.refs_1_, ...), custom_call_target="tpu_custom_call" | custom-call | flops 1700000000 | bytes 9000000 | tf_op jit(solution)/shard_map/pallas_call | solution.py:267
  60.9 3.1 %shard_map.81 = (f32[4,160,128]{2,1,0:T(8,128)S(1)}, f32[4,160,128]{2,1,0:T(8,128)S(1)}, f32[4,160,128]{2,1,0:T(8,128)S(1)}, f32[4,160,128]{2,1,0:T(8,128)S(1)}) custom-call(bf16[8,30,8,128]{3,2,1,0:T(8,128)(2,1)S(1)} %collective-permute-done.refs_0_, ...), custom_call_target="tpu_custom_call", output_to_operand_aliasing={{0}: (7, {}), {1}: (8, {}), {2}: (9, {}), {3}: (10, {})} | custom-call | flops 1700000000 | bytes 9000000 | tf_op jit(solution)/shard_map/pallas_call | solution.py:267
  64.1 2.4 %collective-permute-start.21 = (f32[4,160,128]{2,1,0:T(8,128)S(1)}, f32[4,160,128]{2,1,0:T(8,128)S(1)}, u32[]{:S(2)}, u32[]{:S(2)}) collective-permute-start(f32[4,160,128]{2,1,0:T(8,128)S(1)} %get-tuple-element.37.part1), channel_id=1, source_target_pairs={{0,192},{64,0},{128,64},{192,128},{1,193},{65,1},{129,65},{193,129... | collective-permute-start | bytes 983048 | tf_op jit(solution)/shard_map/ppermute | solution.py:26
  66.5 1.5 %collective-permute-start.20 = (f32[4,160,128]{2,1,0:T(8,128)S(1)}, f32[4,160,128]{2,1,0:T(8,128)S(1)}, u32[]{:S(2)}, u32[]{:S(2)}) collective-permute-start(f32[4,160,128]{2,1,0:T(8,128)S(1)} %get-tuple-element.38.part2), channel_id=1, source_target_pairs={{0,128},{64,192},{128,0},{192,64},{1,129},{65,193},{129,1},{193,65... | collective-permute-start | bytes 983048 | tf_op jit(solution)/shard_map/ppermute | solution.py:26
  68.6 0.8 shard_map.83
  69.5 1.2 %collective-permute-done.15 = f32[8,128]{1,0:T(8,128)S(1)} collective-permute-done((f32[8,128]{1,0:T(8,128)S(1)}, f32[8,128]{1,0:T(8,128)S(1)}, u32[]{:S(2)}, u32[]{:S(2)}) %collective-permute-start.15) | collective-permute-done | bytes 4128 | tf_op jit(solution)/shard_map/ppermute | solution.py:26
  70.7 16.8 %all_to_all.10 = f32[32,8,128]{2,1,0:T(8,128)S(1)} all-to-all(f32[32,8,128]{2,1,0:T(8,128)S(1)} %broadcast_in_dim.14), channel_id=1, replica_groups={{0,2,4,6,8,10,12,14,16,18,20,22,24,26,28,30,32,34,36,38,40,42,44,46,48,..., dimensions={0} | all-to-all | bytes 262144 | tf_op jit(solution)/shard_map/all_to_all | solution.py:425
  87.5 3.3 %collective-permute-start.18 = (f32[8,128]{1,0:T(8,128)S(1)}, f32[8,128]{1,0:T(8,128)S(1)}, u32[]{:S(2)}, u32[]{:S(2)}) collective-permute-start(f32[8,128]{1,0:T(8,128)S(1)} %reduce_sum.99.sum0), channel_id=1, source_target_pairs={{0,192},{64,0},{128,64},{192,128},{1,193},{65,1},{129,65},{193,129... | collective-permute-start | bytes 12296 | tf_op jit(solution)/shard_map/ppermute | solution.py:26
  90.8 0.8 collective-permute-start.17
  92.1 3.8 %collective-permute-done.17.sum2 = f32[8,128]{1,0:T(8,128)S(1)} collective-permute-done((f32[8,128]{1,0:T(8,128)S(1)}, f32[8,128]{1,0:T(8,128)S(1)}, u32[]{:S(2)}, u32[]{:S(2)}) %collective-permute-start.17) | collective-permute-done | bytes 4128 | tf_op jit(solution)/shard_map/ppermute | solution.py:26
  95.9 0.5 collective-permute-done.16.sum1
  96.4 1.1 %shard_map.84 = (f32[160,512]{1,0:T(8,128)}, f32[512]{0:T(512)}, f32[512]{0:T(512)}) custom-call(f32[8,128]{1,0:T(8,128)S(1)} %reduce_sum.99.sum0, f32[8,128]{1,0:T(8,128)S(1)} %collective-permute-done.16.sum1, f32[8,128]{1,0:T(8,128)S(1)} %collective-permute-done.17.sum2, f32[8,128]{1,0:T(8,128)S(1)} %collective-permute-done.18.sum3, ...), custom_call_target="tpu_custom_call" | custom-call | flops 2000000 | bytes 1900000 | tf_op jit(solution)/shard_map/pallas_call | solution.py:353
  (55 shorter events, 2.2 us)
Async XLA Ops:
  2.5 50.8 %copy-start = (bf16[1,1,160,512]{3,2,1,0:T(8,128)(2,1)S(1)}, bf16[1,1,160,512]{3,2,1,0:T(8,128)(2,1)}, u32[]{:S(2)}) copy-start(bf16[1,1,160,512]{3,2,1,0:T(8,128)(2,1)} %lat.1) | copy-start | bytes 491524
  2.5 22.4 %all-to-all-start = ((bf16[8,30,8,128]{3,2,1,0:T(8,128)(2,1)}), bf16[8,30,8,128]{3,2,1,0:T(8,128)(2,1)S(1)}, u32[]{:S(2)}, u32[]{:S(2)}) async-start(bf16[8,30,8,128]{3,2,1,0:T(8,128)(2,1)} %shard_map.76), calls=%async_computation | async-start | bytes 983040 | tf_op jit(solution)/shard_map/all_to_all | solution.py:375
  11.2 1.1 %copy-start.1 = (bf16[1,2,320,512]{3,2,1,0:T(8,128)(2,1)S(1)}, bf16[1,2,320,512]{3,2,1,0:T(8,128)(2,1)}, u32[]{:S(2)}) copy-start(bf16[1,2,320,512]{3,2,1,0:T(8,128)(2,1)} %cot.1) | copy-start | bytes 1966084
  12.5 15.5 %collective-permute-start.4 = (bf16[640,128]{1,0:T(8,128)(2,1)S(1)}, bf16[640,128]{1,0:T(8,128)(2,1)S(1)}, u32[]{:S(2)}, u32[]{:S(2)}) collective-permute-start(bf16[640,128]{1,0:T(8,128)(2,1)S(1)} %get-tuple-element.24), channel_id=1, source_target_pairs={{0,64},{64,128},{128,192},{192,0},{1,65},{65,129},{129,193},{193,1... | collective-permute-start | bytes 491528 | tf_op jit(solution)/shard_map/ppermute | solution.py:26
  14.1 13.9 %collective-permute-start.5 = (bf16[640,128]{1,0:T(8,128)(2,1)S(1)}, bf16[640,128]{1,0:T(8,128)(2,1)S(1)}, u32[]{:S(2)}, u32[]{:S(2)}) collective-permute-start(bf16[640,128]{1,0:T(8,128)(2,1)S(1)} %get-tuple-element.25), channel_id=1, source_target_pairs={{0,128},{64,192},{128,0},{192,64},{1,129},{65,193},{129,1},{193,65... | collective-permute-start | bytes 491528 | tf_op jit(solution)/shard_map/ppermute | solution.py:26
  16.8 11.2 %collective-permute-start.6 = (bf16[640,128]{1,0:T(8,128)(2,1)S(1)}, bf16[640,128]{1,0:T(8,128)(2,1)S(1)}, u32[]{:S(2)}, u32[]{:S(2)}) collective-permute-start(bf16[640,128]{1,0:T(8,128)(2,1)S(1)} %get-tuple-element.26), channel_id=1, source_target_pairs={{0,192},{64,0},{128,64},{192,128},{1,193},{65,1},{129,65},{193,129... | collective-permute-start | bytes 491528 | tf_op jit(solution)/shard_map/ppermute | solution.py:26
  24.9 22.3 %collective-permute-start.10 = (bf16[8,30,8,128]{3,2,1,0:T(8,128)(2,1)S(1)}, bf16[8,30,8,128]{3,2,1,0:T(8,128)(2,1)S(1)}, u32[]{:S(2)}, u32[]{:S(2)}) collective-permute-start(bf16[8,30,8,128]{3,2,1,0:T(8,128)(2,1)S(1)} %all-to-all-done.refs_0_), channel_id=1, source_target_pairs={{0,48},{16,0},{32,16},{48,32},{1,49},{17,1},{33,17},{49,33},{2,50}... | collective-permute-start | bytes 1474568 | tf_op jit(solution)/shard_map/ppermute | solution.py:26
  27.9 22.7 %collective-permute-start.2 = (bf16[8,30,8,128]{3,2,1,0:T(8,128)(2,1)S(1)}, bf16[8,30,8,128]{3,2,1,0:T(8,128)(2,1)S(1)}, u32[]{:S(2)}, u32[]{:S(2)}) collective-permute-start(bf16[8,30,8,128]{3,2,1,0:T(8,128)(2,1)S(1)} %all-to-all-done.refs_0_), channel_id=1, source_target_pairs={{0,16},{16,32},{32,48},{48,0},{1,17},{17,33},{33,49},{49,1},{2,18}... | collective-permute-start | bytes 1474568 | tf_op jit(solution)/shard_map/ppermute | solution.py:26
  28.0 8.4 %collective-permute-start.7 = (bf16[4,320,128]{2,1,0:T(8,128)(2,1)S(1)}, bf16[4,320,128]{2,1,0:T(8,128)(2,1)S(1)}, u32[]{:S(2)}, u32[]{:S(2)}) collective-permute-start(bf16[4,320,128]{2,1,0:T(8,128)(2,1)S(1)} %get-tuple-element.27), channel_id=1, source_target_pairs={{1,2},{3,4},{5,6},{7,8},{9,10},{11,12},{13,14},{15,16},{17,18},{19... | collective-permute-start | bytes 983048 | tf_op jit(solution)/shard_map/ppermute | solution.py:394
  30.0 6.5 %collective-permute-start.8 = (bf16[4,320,128]{2,1,0:T(8,128)(2,1)S(1)}, bf16[4,320,128]{2,1,0:T(8,128)(2,1)S(1)}, u32[]{:S(2)}, u32[]{:S(2)}) collective-permute-start(bf16[4,320,128]{2,1,0:T(8,128)(2,1)S(1)} %get-tuple-element.28), channel_id=1, source_target_pairs={{0,1},{1,0},{2,3},{3,2},{4,5},{5,4},{6,7},{7,6},{8,9},{9,8},{10,11... | collective-permute-start | bytes 983048 | tf_op jit(solution)/shard_map/ppermute | solution.py:26
  30.4 20.3 %collective-permute-start = (bf16[8,30,8,128]{3,2,1,0:T(8,128)(2,1)S(1)}, bf16[8,30,8,128]{3,2,1,0:T(8,128)(2,1)S(1)}, u32[]{:S(2)}, u32[]{:S(2)}) collective-permute-start(bf16[8,30,8,128]{3,2,1,0:T(8,128)(2,1)S(1)} %all-to-all-done.refs_0_), channel_id=1, source_target_pairs={{0,32},{16,48},{32,0},{48,16},{1,33},{17,49},{33,1},{49,17},{2,34}... | collective-permute-start | bytes 1474568 | tf_op jit(solution)/shard_map/ppermute | solution.py:26
  36.4 14.9 %collective-permute-start.9 = (bf16[8,30,8,128]{3,2,1,0:T(8,128)(2,1)S(1)}, bf16[8,30,8,128]{3,2,1,0:T(8,128)(2,1)S(1)}, u32[]{:S(2)}, u32[]{:S(2)}) collective-permute-start(bf16[8,30,8,128]{3,2,1,0:T(8,128)(2,1)S(1)} %all-to-all-done.refs_0_), channel_id=1, source_target_pairs={{0,1},{1,0},{2,3},{3,2},{4,5},{5,4},{6,7},{7,6},{8,9},{9,8},{10,11... | collective-permute-start | bytes 1474568 | tf_op jit(solution)/shard_map/ppermute | solution.py:26
  47.2 4.1 %collective-permute-start.11 = (bf16[8,30,8,128]{3,2,1,0:T(8,128)(2,1)S(1)}, bf16[8,30,8,128]{3,2,1,0:T(8,128)(2,1)S(1)}, u32[]{:S(2)}, u32[]{:S(2)}) collective-permute-start(bf16[8,30,8,128]{3,2,1,0:T(8,128)(2,1)S(1)} %collective-permute-done.10.refs_2_), channel_id=1, source_target_pairs={{0,1},{1,0},{2,3},{3,2},{4,5},{5,4},{6,7},{7,6},{8,9},{9,8},{10,11... | collective-permute-start | bytes 1474568 | tf_op jit(solution)/shard_map/ppermute | solution.py:26
  50.6 1.9 %collective-permute-start.3 = (bf16[8,30,8,128]{3,2,1,0:T(8,128)(2,1)S(1)}, bf16[8,30,8,128]{3,2,1,0:T(8,128)(2,1)S(1)}, u32[]{:S(2)}, u32[]{:S(2)}) collective-permute-start(bf16[8,30,8,128]{3,2,1,0:T(8,128)(2,1)S(1)} %collective-permute-done.2.refs_2_), channel_id=1, source_target_pairs={{0,1},{1,0},{2,3},{3,2},{4,5},{5,4},{6,7},{7,6},{8,9},{9,8},{10,11... | collective-permute-start | bytes 1474568 | tf_op jit(solution)/shard_map/ppermute | solution.py:26
  50.7 2.5 %collective-permute-start.1 = (bf16[8,30,8,128]{3,2,1,0:T(8,128)(2,1)S(1)}, bf16[8,30,8,128]{3,2,1,0:T(8,128)(2,1)S(1)}, u32[]{:S(2)}, u32[]{:S(2)}) collective-permute-start(bf16[8,30,8,128]{3,2,1,0:T(8,128)(2,1)S(1)} %collective-permute-done.refs_0_), channel_id=1, source_target_pairs={{0,1},{1,0},{2,3},{3,2},{4,5},{5,4},{6,7},{7,6},{8,9},{9,8},{10,11... | collective-permute-start | bytes 1474568 | tf_op jit(solution)/shard_map/ppermute | solution.py:26
  53.3 14.7 %collective-permute-start.14 = (bf16[688,128]{1,0:T(8,128)(2,1)S(1)}, bf16[688,128]{1,0:T(8,128)(2,1)S(1)}, u32[]{:S(2)}, u32[]{:S(2)}) collective-permute-start(bf16[688,128]{1,0:T(8,128)(2,1)S(1)} %shard_map.82.msg0), channel_id=1, source_target_pairs={{0,192},{64,0},{128,64},{192,128},{1,193},{65,1},{129,65},{193,129... | collective-permute-start | bytes 528392 | tf_op jit(solution)/shard_map/ppermute | solution.py:26
  56.1 11.9 %collective-permute-start.13 = (bf16[688,128]{1,0:T(8,128)(2,1)S(1)}, bf16[688,128]{1,0:T(8,128)(2,1)S(1)}, u32[]{:S(2)}, u32[]{:S(2)}) collective-permute-start(bf16[688,128]{1,0:T(8,128)(2,1)S(1)} %shard_map.82.msg0), channel_id=1, source_target_pairs={{0,128},{64,192},{128,0},{192,64},{1,129},{65,193},{129,1},{193,65... | collective-permute-start | bytes 528392 | tf_op jit(solution)/shard_map/ppermute | solution.py:26
  56.9 11.1 %collective-permute-start.12 = (bf16[688,128]{1,0:T(8,128)(2,1)S(1)}, bf16[688,128]{1,0:T(8,128)(2,1)S(1)}, u32[]{:S(2)}, u32[]{:S(2)}) collective-permute-start(bf16[688,128]{1,0:T(8,128)(2,1)S(1)} %shard_map.82.msg0), channel_id=1, source_target_pairs={{0,64},{64,128},{128,192},{192,0},{1,65},{65,129},{129,193},{193,1... | collective-permute-start | bytes 528392 | tf_op jit(solution)/shard_map/ppermute | solution.py:26
  60.9 7.6 %copy-start.2 = (f32[512]{0:T(512)S(1)}, f32[512]{0:T(512)}, u32[]{:S(2)}) copy-start(f32[512]{0:T(512)} %param.7) | copy-start | bytes 6148
  60.9 7.6 %copy-start.3 = (f32[512]{0:T(512)S(1)}, f32[512]{0:T(512)}, u32[]{:S(2)}) copy-start(f32[512]{0:T(512)} %param.6) | copy-start | bytes 6148
  64.1 27.5 %collective-permute-start.21 = (f32[4,160,128]{2,1,0:T(8,128)S(1)}, f32[4,160,128]{2,1,0:T(8,128)S(1)}, u32[]{:S(2)}, u32[]{:S(2)}) collective-permute-start(f32[4,160,128]{2,1,0:T(8,128)S(1)} %get-tuple-element.37.part1), channel_id=1, source_target_pairs={{0,192},{64,0},{128,64},{192,128},{1,193},{65,1},{129,65},{193,129... | collective-permute-start | bytes 983048 | tf_op jit(solution)/shard_map/ppermute | solution.py:26
  66.5 25.3 %collective-permute-start.20 = (f32[4,160,128]{2,1,0:T(8,128)S(1)}, f32[4,160,128]{2,1,0:T(8,128)S(1)}, u32[]{:S(2)}, u32[]{:S(2)}) collective-permute-start(f32[4,160,128]{2,1,0:T(8,128)S(1)} %get-tuple-element.38.part2), channel_id=1, source_target_pairs={{0,128},{64,192},{128,0},{192,64},{1,129},{65,193},{129,1},{193,65... | collective-permute-start | bytes 983048 | tf_op jit(solution)/shard_map/ppermute | solution.py:26
  68.0 23.7 %collective-permute-start.19 = (f32[4,160,128]{2,1,0:T(8,128)S(1)}, f32[4,160,128]{2,1,0:T(8,128)S(1)}, u32[]{:S(2)}, u32[]{:S(2)}) collective-permute-start(f32[4,160,128]{2,1,0:T(8,128)S(1)} %get-tuple-element.39.part3), channel_id=1, source_target_pairs={{0,64},{64,128},{128,192},{192,0},{1,65},{65,129},{129,193},{193,1... | collective-permute-start | bytes 983048 | tf_op jit(solution)/shard_map/ppermute | solution.py:26
  69.4 1.3 %collective-permute-start.15 = (f32[8,128]{1,0:T(8,128)S(1)}, f32[8,128]{1,0:T(8,128)S(1)}, u32[]{:S(2)}, u32[]{:S(2)}) collective-permute-start(f32[8,128]{1,0:T(8,128)S(1)} %shard_map.83), channel_id=1, source_target_pairs={{0,1},{1,0},{2,3},{3,2},{4,5},{5,4},{6,7},{7,6},{8,9},{9,8},{10,11... | collective-permute-start | bytes 12296 | tf_op jit(solution)/shard_map/ppermute | solution.py:26
  87.5 4.6 %collective-permute-start.18 = (f32[8,128]{1,0:T(8,128)S(1)}, f32[8,128]{1,0:T(8,128)S(1)}, u32[]{:S(2)}, u32[]{:S(2)}) collective-permute-start(f32[8,128]{1,0:T(8,128)S(1)} %reduce_sum.99.sum0), channel_id=1, source_target_pairs={{0,192},{64,0},{128,64},{192,128},{1,193},{65,1},{129,65},{193,129... | collective-permute-start | bytes 12296 | tf_op jit(solution)/shard_map/ppermute | solution.py:26
  90.8 5.1 %collective-permute-start.17 = (f32[8,128]{1,0:T(8,128)S(1)}, f32[8,128]{1,0:T(8,128)S(1)}, u32[]{:S(2)}, u32[]{:S(2)}) collective-permute-start(f32[8,128]{1,0:T(8,128)S(1)} %reduce_sum.99.sum0), channel_id=1, source_target_pairs={{0,128},{64,192},{128,0},{192,64},{1,129},{65,193},{129,1},{193,65... | collective-permute-start | bytes 12296 | tf_op jit(solution)/shard_map/ppermute | solution.py:26
  91.6 4.8 %collective-permute-start.16 = (f32[8,128]{1,0:T(8,128)S(1)}, f32[8,128]{1,0:T(8,128)S(1)}, u32[]{:S(2)}, u32[]{:S(2)}) collective-permute-start(f32[8,128]{1,0:T(8,128)S(1)} %reduce_sum.99.sum0), channel_id=1, source_target_pairs={{0,64},{64,128},{128,192},{192,0},{1,65},{65,129},{129,193},{193,1... | collective-permute-start | bytes 12296 | tf_op jit(solution)/shard_map/ppermute | solution.py:26
